TPU v7x, 32 devices: a whole 2x2x4 slice. The times are simulated.
32 devices in a mesh: dom: 8 (over y, x, core), spec: 4 (over z).
Axes of the slice: x: 2, y: 2, z: 4, core: 2. Of those that a mesh axis runs over, the one named last changes fastest.
Arguments:
- spectrum: float32 [1296, 8192], P('spec', 'dom'), may hold values from 0.2 to 2
- normals: float32 [2, 3, 16384], P(None, None, 'dom'), may hold values from -3 to 3, as said below
- conn: int32 [3, 16384], P(None, 'dom'), may hold values from 0 to 1535
- send_nodes: int32 [8, 4, 128], P('dom'), may hold values from 0 to 1023, as said below
- step_weight: float32 [8192], P('dom'), may hold values from 0.02 to 0.06
- group_speed: float32 [36], replicated, may hold values from 0.25 to 1
- dia_plus: int32 [1296], replicated, may hold values from 0 to 1295, as said below
- dia_minus: int32 [1296], replicated, may hold values from 0 to 1295, as said below
- dia_coeff: float32 [1296], replicated, may hold values from 0.01 to 0.04
Outputs:
- spectrum_out: float32 [1296, 8192], P(None, ('dom', 'spec'))
Inputs may be any that keep to these rules, and one draw needn't show every extreme that they name: `send_nodes`: each row lists distinct owned nodes of the sending partition. `dia_plus`: for bin f * 36 + d the partner has frequency min(f + 1 or f + 2, 35) and a direction 1 to 3 steps higher, modulo 36. `dia_minus`: for bin f * 36 + d the partner has frequency max(f - 1 or f - 2, 0) and a direction 1 to 3 steps lower, modulo 36. `normals`: for each triangle the three vectors sum to zero and no two are parallel.
All inputs are finite; a program needn't handle non-finite values.
Results may differ from a plain program's by a relative error of at most 0.00002.
Values sent between devices are 32-bit elements; how exact they have to be, the bound alone decides.
No kernel may reach another device: no remote copies, remote signals or barrier semaphores. Data moves between devices by JAX's collectives and lax.ppermute only.
A program may use at most 64 MiB of HBM per device.

v0:
```python
import functools
import math

import jax
import jax.numpy as jnp
from jax import lax
from jax.experimental import pallas as pl
from jax.experimental.pallas import tpu as pltpu
from jax.sharding import PartitionSpec as P

NDIR = 36
REACH = 2
STEPS = 2
BLOCKS = 2 * REACH
LANES = 128
GROUPS = 2

weight_plus = 1.25 ** (-4)
weight_minus = 0.75 ** (-4)
weight_both = 0.9375 ** (-4)

VM = pl.BlockSpec(memory_space=pltpu.VMEM)
SM = pl.BlockSpec(memory_space=pltpu.SMEM)


def offset_of(position):
    return position - REACH if position < REACH else position - REACH + 1


def passed_along(value, axis, steps):
    count = lax.axis_size(axis)
    leading, last = (max(0, -steps), min(count, count - steps))
    return lax.ppermute(value, axis, [(source, source + steps) for source in range(leading, last)])


def chunked(total, limit):
    return max(size for size in range(1, limit + 1) if total % size == 0)


def pack_rows(sub, slots, send, energy, outs):
    unroll = chunked(slots, 16)
    for position in range(BLOCKS):

        @pl.loop(0, slots // unroll)
        def _(k):
            first = k * unroll
            for u in range(unroll):
                row = send[(BLOCKS - 1 - position) * slots + first + u]
                outs[position][pl.ds((first + u) * sub, sub), :] = energy[pl.ds(row, sub), :]


def enter_kernel(sub, lanes, slots, send, spectrum, energy, *outs):
    owned = spectrum.shape[2]

    @pl.loop(0, owned // LANES)
    def _(k):
        for part in range(sub):
            block = spectrum[part, :, pl.ds(pl.multiple_of(k * LANES, LANES), LANES)]
            energy[pl.ds(k * LANES * sub + part, LANES, stride=sub), :] = block.T

    pack_rows(sub, slots, send, energy, outs)


def sweep_kernel(sub, shared, slots, conn, energy, coef, weight, *rest):
    ghosts, rest = rest[:BLOCKS], rest[BLOCKS:]
    partial, returned, rest = rest[0], rest[1 : 1 + BLOCKS], rest[1 + BLOCKS :]
    full, sums = rest[0], rest[1:]
    own_rows = energy.shape[0]
    ghost_rows = slots * sub
    rows = full.shape[0]
    elements = conn.shape[0] // 3
    step = chunked(rows, 64)
    zero = jnp.zeros((step, LANES), jnp.float32)

    @pl.loop(0, rows // step)
    def _(k):
        for item in sums:
            item[pl.ds(pl.multiple_of(k * step, step), step), :] = zero

    full[:own_rows, :] = energy[...]
    for position in range(BLOCKS):
        first = own_rows + position * ghost_rows
        full[first : first + ghost_rows, :] = ghosts[position][...]

    share = elements // GROUPS
    unroll = chunked(share, 16)

    def coef_rows(which, element):
        if shared:
            return coef[pl.ds(which * elements + element, sub, stride=0), :]
        return coef[pl.ds((which * elements + element) * sub, sub), :]

    @pl.loop(0, share // unroll)
    def _(k):
        for u in range(unroll):
            for group in range(GROUPS):
                element = group * share + k * unroll + u
                index = [conn[corner * elements + element] for corner in range(3)]
                value = [full[pl.ds(row, sub), :] for row in index]
                inflow = coef_rows(3, element) * value[0]
                inflow = inflow + coef_rows(4, element) * value[1]
                inflow = inflow + coef_rows(5, element) * value[2]
                for corner in range(3):
                    part = coef_rows(corner, element) * (value[corner] - inflow)
                    item = sums[group * 3 + corner]
                    item[pl.ds(index[corner], sub), :] = item[pl.ds(index[corner], sub), :] + part

    def total(at):
        result = sums[0][at, :]
        for item in sums[1:]:
            result = result + item[at, :]
        return result

    own_step = chunked(own_rows, 64)

    @pl.loop(0, own_rows // own_step)
    def _(k):
        at = pl.ds(pl.multiple_of(k * own_step, own_step), own_step)
        partial[at, :] = energy[at, :] - weight[at, :] * total(at)

    ghost_step = chunked(ghost_rows, 64)
    for position in range(BLOCKS):

        @pl.loop(0, ghost_rows // ghost_step)
        def _(k):
            at = pl.multiple_of(k * ghost_step, ghost_step)
            source = pl.ds(own_rows + position * ghost_rows + at, ghost_step)
            returned[position][pl.ds(at, ghost_step), :] = total(source)


def add_returned(sub, slots, send, weight, incoming, energy):
    unroll = chunked(slots, 16)
    for position in range(BLOCKS):

        @pl.loop(0, slots // unroll)
        def _(k):
            first = k * unroll
            rows = [send[(BLOCKS - 1 - position) * slots + first + u] for u in range(unroll)]
            fresh = [
                energy[pl.ds(row, sub), :]
                - weight[pl.ds(row, sub), :] * incoming[position][pl.ds((first + u) * sub, sub), :]
                for u, row in enumerate(rows)
            ]
            for row, item in zip(rows, fresh):
                energy[pl.ds(row, sub), :] = item


def between_kernel(sub, slots, send, partial, weight, *rest):
    incoming, energy, outs = rest[:BLOCKS], rest[BLOCKS], rest[BLOCKS + 1 :]
    energy[...] = partial[...]
    add_returned(sub, slots, send, weight, incoming, energy)
    pack_rows(sub, slots, send, energy, outs)


def leave_kernel(sub, lanes, slots, halves, send, partial, weight, *rest):
    incoming, out, energy = rest[:BLOCKS], rest[BLOCKS], rest[BLOCKS + 1]
    energy[...] = partial[...]
    add_returned(sub, slots, send, weight, incoming, energy)
    owned = energy.shape[0] // sub
    per_target = sub * lanes * halves
    for block in range(owned // LANES):
        target, half = divmod(block, halves)
        for part in range(sub):
            tile = energy[pl.ds(block * LANES * sub + part, LANES, stride=sub), :].T
            first = target * per_target + part * lanes * halves + half
            out[pl.ds(first, lanes, stride=halves), :] = tile[:lanes]


def interact_kernel(halves, plus, minus, rate, energy, out, *sums):
    bins = plus.shape[0]
    rows = energy.shape[0]
    step = chunked(rows, 64)
    zero = jnp.zeros((step, LANES), jnp.float32)

    @pl.loop(0, rows // step)
    def _(k):
        for item in sums[1:]:
            item[pl.ds(pl.multiple_of(k * step, step), step), :] = zero

    share = bins // GROUPS
    unroll = chunked(share, 12)

    @pl.loop(0, share // unroll)
    def _(k):
        for u in range(unroll):
            for group in range(GROUPS):
                index = group * share + k * unroll + u
                up, down = plus[index], minus[index]
                own = energy[pl.ds(index * halves, halves), :]
                upper = energy[pl.ds(up, halves), :]
                lower = energy[pl.ds(down, halves), :]
                term = rate[index] * (
                    own * own * (weight_plus * upper + weight_minus * lower)
                    - 2.0 * weight_both * own * upper * lower
                )
                sums[0][pl.ds(index * halves, halves), :] = own - 2.0 * term
                high, low = sums[1 + 2 * group], sums[2 + 2 * group]
                high[pl.ds(up, halves), :] = high[pl.ds(up, halves), :] + term
                low[pl.ds(down, halves), :] = low[pl.ds(down, halves), :] + term

    step = chunked(bins, 48)

    @pl.loop(0, bins // step)
    def _(k):
        for half in range(halves):
            at = pl.ds(k * step * halves + half, step, stride=halves)
            result = sums[0][at, :]
            for item in sums[1:]:
                result = result + item[at, :]
            out[pl.ds(pl.multiple_of(k * step, step), step), half * LANES : (half + 1) * LANES] = result


def shape_of(*dims):
    return jax.ShapeDtypeStruct(dims, jnp.float32)


def cost(flops, moved):
    return pl.CostEstimate(flops=flops, bytes_accessed=moved, transcendentals=0)


def on_device(
    spectrum, normals, conn, send_nodes, step_weight, group_speed, dia_plus, dia_minus, dia_coeff
):
    row_count, owned = spectrum.shape
    slots = send_nodes.shape[2]
    elements = conn.shape[1]
    bins = dia_plus.shape[0]
    spec_count = lax.axis_size("spec")
    sub = -(-row_count // LANES)
    while row_count % sub:
        sub += 1
    lanes = row_count // sub
    shared = lanes % NDIR == 0
    own_rows = owned * sub
    ghost_rows = slots * sub
    rows = own_rows + BLOCKS * ghost_rows
    halves = owned // (spec_count * LANES)

    send = (send_nodes[0] * sub).reshape(-1)
    nodes = (conn * sub).reshape(-1)

    bin_of = (
        lax.axis_index("spec") * row_count
        + jnp.arange(sub, dtype=jnp.int32)[:, None] * lanes
        + jnp.arange(LANES, dtype=jnp.int32)[None, :]
    )
    angle = (bin_of % NDIR).astype(jnp.float32) * (2.0 * math.pi / NDIR)
    east, north = jnp.cos(angle), jnp.sin(angle)
    select = ((bin_of // NDIR)[:, :, None] == jnp.arange(group_speed.shape[0], dtype=jnp.int32)).astype(jnp.float32)
    speed = jnp.sum(select * group_speed, axis=2)
    if shared:
        east, north = east[:1], north[:1]
    slope = normals[0][:, :, None, None] * east + normals[1][:, :, None, None] * north
    inward = jnp.minimum(slope, 0.0)
    share = inward / jnp.sum(inward, axis=0)
    coef = jnp.concatenate([jnp.maximum(slope, 0.0), share]).reshape(-1, LANES)
    weight = (step_weight[:, None, None] * speed).reshape(own_rows, LANES)

    padded = jnp.pad(spectrum.reshape(sub, lanes, owned), ((0, 0), (0, LANES - lanes), (0, 0)))
    block_shapes = [shape_of(ghost_rows, LANES)] * BLOCKS
    energy, *outs = pl.pallas_call(
        functools.partial(enter_kernel, sub, lanes, slots),
        out_shape=[shape_of(own_rows, LANES)] + block_shapes,
        in_specs=[SM, VM],
        out_specs=[VM] * (1 + BLOCKS),
        cost_estimate=cost(0, 8 * own_rows * LANES),
        name="enter",
    )(send, padded)

    for sweep_index in range(STEPS):
        ghosts = [passed_along(outs[p], "dom", -offset_of(p)) for p in range(BLOCKS)]
        partial, *returned = pl.pallas_call(
            functools.partial(sweep_kernel, sub, shared, slots),
            out_shape=[shape_of(own_rows, LANES)] + block_shapes,
            in_specs=[SM] + [VM] * (3 + BLOCKS),
            out_specs=[VM] * (1 + BLOCKS),
            scratch_shapes=[pltpu.VMEM((rows, LANES), jnp.float32)] * (1 + 3 * GROUPS),
            cost_estimate=cost(elements * 24 * row_count, 4 * LANES * (8 * elements + 4 * rows)),
            name="sweep",
        )(nodes, energy, coef, weight, *ghosts)
        incoming = [passed_along(returned[p], "dom", offset_of(p)) for p in range(BLOCKS)]
        if sweep_index < STEPS - 1:
            energy, *outs = pl.pallas_call(
                functools.partial(between_kernel, sub, slots),
                out_shape=[shape_of(own_rows, LANES)] + block_shapes,
                in_specs=[SM] + [VM] * (2 + BLOCKS),
                out_specs=[VM] * (1 + BLOCKS),
                cost_estimate=cost(2 * owned * row_count, 16 * own_rows * LANES),
                name="between",
            )(send, partial, weight, *incoming)

    leaving = pl.pallas_call(
        functools.partial(leave_kernel, sub, lanes, slots, halves),
        out_shape=shape_of(spec_count * row_count * halves, LANES),
        in_specs=[SM] + [VM] * (2 + BLOCKS),
        out_specs=VM,
        scratch_shapes=[pltpu.VMEM((own_rows, LANES), jnp.float32)],
        cost_estimate=cost(2 * owned * row_count, 16 * own_rows * LANES),
        name="leave",
    )(send, partial, weight, *incoming)
    arrived = lax.all_to_all(
        leaving.reshape(spec_count, row_count * halves, LANES), "spec", split_axis=0, concat_axis=0
    )
    return pl.pallas_call(
        functools.partial(interact_kernel, halves),
        out_shape=shape_of(bins, halves * LANES),
        in_specs=[SM] * 3 + [VM],
        out_specs=VM,
        scratch_shapes=[pltpu.VMEM((bins * halves, LANES), jnp.float32)] * (1 + 2 * GROUPS),
        cost_estimate=cost(16 * bins * halves * LANES, 8 * bins * halves * LANES),
        name="interact",
    )(dia_plus * halves, dia_minus * halves, dia_coeff, arrived.reshape(bins * halves, LANES))


def solution(mesh):
    in_specs = (
        P("spec", "dom"),
        P(None, None, "dom"),
        P(None, "dom"),
        P("dom", None, None),
        P("dom"),
        P(),
        P(),
        P(),
        P(),
    )
    out_specs = P(None, ("dom", "spec"))
    return jax.shard_map(
        on_device, mesh=mesh, in_specs=in_specs, out_specs=out_specs, check_vma=False
    )
```

profile of v0, /device:TPU:4, one launch (start us, length us, event | category | flops | bytes accessed | tf_op | source)
XLA Modules:
  0.0 185.7 jit_solution(18022632544324604646)
XLA Ops:
  4.1 4.5 %enter.1 = (f32[3072,128]{1,0:T(8,128)}, f32[384,128]{1,0:T(8,128)}, f32[384,128]{1,0:T(8,128)}, f32[384,128]{1,0:T(8,128)}, f32[384,128]{1,0:T(8,128)}) custom-call(s32[512]{0:T(512)} %multiply_bitcast_fusion.send, f32[3,128,1024]{2,1,0:T(8,128)} %pad.4.spectrum), custom_call_target="tpu_custom_call" | custom-call | bytes 3145728 | tf_op jit(solution)/shard_map/enter/pallas_call | solution.py:261
  8.6 3.4 %collective-permute-start = (f32[384,128]{1,0:T(8,128)}, f32[384,128]{1,0:T(8,128)S(1)}, u32[]{:S(2)}, u32[]{:S(2)}) collective-permute-start(f32[384,128]{1,0:T(8,128)} %get-tuple-element.26), channel_id=1, source_target_pairs={{0,8},{4,12},{8,16},{12,20},{16,24},{20,28},{1,9},{5,13},{9,17},{1... | collective-permute-start | bytes 589832 | tf_op jit(solution)/shard_map/ppermute | solution.py:33
  13.9 4.5 %collective-permute-start.2 = (f32[384,128]{1,0:T(8,128)}, f32[384,128]{1,0:T(8,128)}, u32[]{:S(2)}, u32[]{:S(2)}) collective-permute-start(f32[384,128]{1,0:T(8,128)} %get-tuple-element.28), channel_id=1, source_target_pairs={{4,0},{8,4},{12,8},{16,12},{20,16},{24,20},{28,24},{5,1},{9,5},{13... | collective-permute-start | bytes 589832 | tf_op jit(solution)/shard_map/ppermute | solution.py:33
  18.4 2.4 %collective-permute-start.3 = (f32[384,128]{1,0:T(8,128)}, f32[384,128]{1,0:T(8,128)}, u32[]{:S(2)}, u32[]{:S(2)}) collective-permute-start(f32[384,128]{1,0:T(8,128)} %get-tuple-element.29), channel_id=1, source_target_pairs={{8,0},{12,4},{16,8},{20,12},{24,16},{28,20},{9,1},{13,5},{17,9},{2... | collective-permute-start | bytes 589832 | tf_op jit(solution)/shard_map/ppermute | solution.py:33
  23.1 3.2 %fusion.2 = f32[3,2048,1,128]{3,1,0,2:T(8,128)} fusion(f32[2048,128]{1,0:T(8,128)S(1)} %get-tuple-element.46, f32[128]{0:T(128)S(1)} %get-tuple-element.51, f32[3,2048]{1,0:T(4,128)S(1)} %get-tuple-element.53, f32[128]{0:T(128)S(1)} %get-tuple-element.52, f32[3,2048]{1,0:T(4,128)S(1)} %get-tuple-element.54), kind=kLoop, calls=%fused_computation.4 | loop fusion | flops 3932160 | bytes 4244480 | tf_op jit(solution)/shard_map/div | solution.py:255
  28.0 3.8 %mul.160 = f32[3072,128]{1,0:T(8,128)} reshape(f32[1024,3,128]{2,1,0:T(4,128)} %mul.159) | data formatting | bytes 3145728 | tf_op jit(solution)/shard_map/mul | solution.py:257
  36.9 3.2 %broadcast_multiply_fusion.weight = f32[3072,128]{1,0:T(8,128)} fusion(f32[3072,128]{1,0:T(8,128)} %mul.160, f32[3072]{0:T(1024)S(1)} %mul.155), kind=kLoop, calls=%fused_computation.6 | loop fusion | flops 393216 | bytes 3158016 | tf_op jit(solution)/shard_map/mul | solution.py:257
  40.1 3.1 %pad_maximum_fusion = f32[6,2048,1,128]{3,1,0,2:T(8,128)} fusion(f32[3,2048,1,128]{3,1,0,2:T(8,128)S(1)} %copy-done, f32[3,2048,1,128]{3,1,0,2:T(8,128)S(1)} %get-tuple-element.45), kind=kLoop, calls=%fused_computation | loop fusion | flops 1572864 | bytes 12582912 | tf_op jit(solution)/shard_map/concatenate | solution.py:256
  43.9 17.5 %sweep.2 = (f32[3072,128]{1,0:T(8,128)}, f32[384,128]{1,0:T(8,128)}, f32[384,128]{1,0:T(8,128)}, f32[384,128]{1,0:T(8,128)}, f32[384,128]{1,0:T(8,128)}) custom-call(s32[6144]{0:T(1024)} %reshape.101.conn, f32[3072,128]{1,0:T(8,128)} %get-tuple-element.25.energy, f32[12288,128]{1,0:T(8,128)} %bitcast.13, f32[3072,128]{1,0:T(8,128)} %broadcast_multiply_fusion.weight, ...), custom_call_target="tpu_custom_call" | custom-call | flops 15925248 | bytes 17825792 | tf_op jit(solution)/shard_map/sweep/pallas_call | solution.py:272
  65.2 2.4 %collective-permute-start.6 = (f32[384,128]{1,0:T(8,128)}, f32[384,128]{1,0:T(8,128)S(1)}, u32[]{:S(2)}, u32[]{:S(2)}) collective-permute-start(f32[384,128]{1,0:T(8,128)} %get-tuple-element.33), channel_id=1, source_target_pairs={{0,4},{4,8},{8,12},{12,16},{16,20},{20,24},{24,28},{1,5},{5,9},{9,... | collective-permute-start | bytes 589832 | tf_op jit(solution)/shard_map/ppermute | solution.py:33
  67.7 3.9 %collective-permute-start.7 = (f32[384,128]{1,0:T(8,128)}, f32[384,128]{1,0:T(8,128)S(1)}, u32[]{:S(2)}, u32[]{:S(2)}) collective-permute-start(f32[384,128]{1,0:T(8,128)} %get-tuple-element.34), channel_id=1, source_target_pairs={{0,8},{4,12},{8,16},{12,20},{16,24},{20,28},{1,9},{5,13},{9,17},{1... | collective-permute-start | bytes 589832 | tf_op jit(solution)/shard_map/ppermute | solution.py:33
  73.3 4.4 %collective-permute-done.7.rest_3_ = f32[384,128]{1,0:T(8,128)S(1)} collective-permute-done((f32[384,128]{1,0:T(8,128)}, f32[384,128]{1,0:T(8,128)S(1)}, u32[]{:S(2)}, u32[]{:S(2)}) %collective-permute-start.7) | collective-permute-done | bytes 196640 | tf_op jit(solution)/shard_map/ppermute | solution.py:33
  78.4 5.2 %between.1 = (f32[3072,128]{1,0:T(8,128)}, f32[384,128]{1,0:T(8,128)}, f32[384,128]{1,0:T(8,128)}, f32[384,128]{1,0:T(8,128)}, f32[384,128]{1,0:T(8,128)}) custom-call(s32[512]{0:T(512)} %multiply_bitcast_fusion.send, f32[3072,128]{1,0:T(8,128)} %get-tuple-element.30.partial, f32[3072,128]{1,0:T(8,128)} %broadcast_multiply_fusion.weight, ...), custom_call_target="tpu_custom_call" | custom-call | flops 663552 | bytes 6291456 | tf_op jit(solution)/shard_map/between/pallas_call | solution.py:283
  87.5 3.9 %collective-permute-start.8 = (f32[384,128]{1,0:T(8,128)}, f32[384,128]{1,0:T(8,128)S(1)}, u32[]{:S(2)}, u32[]{:S(2)}) collective-permute-start(f32[384,128]{1,0:T(8,128)} %get-tuple-element.36), channel_id=1, source_target_pairs={{0,8},{4,12},{8,16},{12,20},{16,24},{20,28},{1,9},{5,13},{9,17},{1... | collective-permute-start | bytes 589832 | tf_op jit(solution)/shard_map/ppermute | solution.py:33
  93.4 2.3 %collective-permute-done.11.rest_3_ = f32[384,128]{1,0:T(8,128)S(1)} collective-permute-done((f32[384,128]{1,0:T(8,128)}, f32[384,128]{1,0:T(8,128)S(1)}, u32[]{:S(2)}, u32[]{:S(2)}) %collective-permute-start.11) | collective-permute-done | bytes 196640 | tf_op jit(solution)/shard_map/ppermute | solution.py:33
  95.7 2.4 %collective-permute-done.8.rest_0_ = f32[384,128]{1,0:T(8,128)S(1)} collective-permute-done((f32[384,128]{1,0:T(8,128)}, f32[384,128]{1,0:T(8,128)S(1)}, u32[]{:S(2)}, u32[]{:S(2)}) %collective-permute-start.8) | collective-permute-done | bytes 196640 | tf_op jit(solution)/shard_map/ppermute | solution.py:33
  100.6 17.4 %sweep.3 = (f32[3072,128]{1,0:T(8,128)}, f32[384,128]{1,0:T(8,128)}, f32[384,128]{1,0:T(8,128)}, f32[384,128]{1,0:T(8,128)}, f32[384,128]{1,0:T(8,128)}) custom-call(s32[6144]{0:T(1024)} %reshape.101.conn, f32[3072,128]{1,0:T(8,128)} %get-tuple-element.35.energy, f32[12288,128]{1,0:T(8,128)} %bitcast.14, f32[3072,128]{1,0:T(8,128)} %broadcast_multiply_fusion.weight, ...), custom_call_target="tpu_custom_call" | custom-call | flops 15925248 | bytes 17825792 | tf_op jit(solution)/shard_map/sweep/pallas_call | solution.py:272
  121.8 2.4 %collective-permute-start.14 = (f32[384,128]{1,0:T(8,128)}, f32[384,128]{1,0:T(8,128)S(1)}, u32[]{:S(2)}, u32[]{:S(2)}) collective-permute-start(f32[384,128]{1,0:T(8,128)} %get-tuple-element.43), channel_id=1, source_target_pairs={{0,4},{4,8},{8,12},{12,16},{16,20},{20,24},{24,28},{1,5},{5,9},{9,... | collective-permute-start | bytes 589832 | tf_op jit(solution)/shard_map/ppermute | solution.py:33
  124.2 3.9 %collective-permute-start.15 = (f32[384,128]{1,0:T(8,128)}, f32[384,128]{1,0:T(8,128)S(1)}, u32[]{:S(2)}, u32[]{:S(2)}) collective-permute-start(f32[384,128]{1,0:T(8,128)} %get-tuple-element.44), channel_id=1, source_target_pairs={{0,8},{4,12},{8,16},{12,20},{16,24},{20,28},{1,9},{5,13},{9,17},{1... | collective-permute-start | bytes 589832 | tf_op jit(solution)/shard_map/ppermute | solution.py:33
  129.9 4.4 %collective-permute-done.15.rest_3_ = f32[384,128]{1,0:T(8,128)S(1)} collective-permute-done((f32[384,128]{1,0:T(8,128)}, f32[384,128]{1,0:T(8,128)S(1)}, u32[]{:S(2)}, u32[]{:S(2)}) %collective-permute-start.15) | collective-permute-done | bytes 196640 | tf_op jit(solution)/shard_map/ppermute | solution.py:33
  135.0 4.7 %leave.1 = f32[2592,128]{1,0:T(8,128)} custom-call(s32[512]{0:T(512)} %multiply_bitcast_fusion.send, f32[3072,128]{1,0:T(8,128)} %get-tuple-element.40.partial, f32[3072,128]{1,0:T(8,128)} %broadcast_multiply_fusion.weight, f32[384,128]{1,0:T(8,128)} %copy-done.4, f32[384,128]{1,0:T(8,128)} %copy-done.6, f32[384,128]{1,0:T(8,128)} %copy-done.8, ...), custom_call_target="tpu_custom_call" | custom-call | flops 663552 | bytes 6291456 | tf_op jit(solution)/shard_map/leave/pallas_call | solution.py:292
  139.8 4.9 %all-to-all-start = ((f32[4,648,128]{2,1,0:T(8,128)}), f32[4,648,128]{2,1,0:T(8,128)S(1)}, u32[]{:S(2)}, u32[]{:S(2)}) async-start(f32[4,648,128]{2,1,0:T(8,128)} %bitcast.15), calls=%async_computation | async-start | bytes 2654208 | tf_op jit(solution)/shard_map/all_to_all | solution.py:301
  145.3 31.7 %all-to-all-done = f32[4,648,128]{2,1,0:T(8,128)S(1)} async-done(((f32[4,648,128]{2,1,0:T(8,128)}), f32[4,648,128]{2,1,0:T(8,128)S(1)}, u32[]{:S(2)}, u32[]{:S(2)}) %all-to-all-start) | async-done | bytes 1327136 | tf_op jit(solution)/shard_map/all_to_all | solution.py:301
  178.1 7.6 %interact.1 = f32[1296,256]{1,0:T(8,128)} custom-call(s32[1296]{0:T(1024)} %get-tuple-element.56.plus, s32[1296]{0:T(1024)} %get-tuple-element.55.minus, f32[1296]{0:T(1024)} %rate.1, f32[2592,128]{1,0:T(8,128)} %bitcast.16), custom_call_target="tpu_custom_call" | custom-call | flops 5308416 | bytes 2654208 | tf_op jit(solution)/shard_map/interact/pallas_call | solution.py:304
  (79 shorter events, 38.0 us)
Async XLA Ops:
  1.3 19.8 %copy-start.16 = (f32[2,3,2048]{2,0,1:T(2,128)S(1)}, f32[2,3,2048]{2,0,1:T(2,128)}, u32[]{:S(2)}) copy-start(f32[2,3,2048]{2,0,1:T(2,128)} %param.10) | copy-start | bytes 147460
  8.6 34.6 %collective-permute-start = (f32[384,128]{1,0:T(8,128)}, f32[384,128]{1,0:T(8,128)S(1)}, u32[]{:S(2)}, u32[]{:S(2)}) collective-permute-start(f32[384,128]{1,0:T(8,128)} %get-tuple-element.26), channel_id=1, source_target_pairs={{0,8},{4,12},{8,16},{12,20},{16,24},{20,28},{1,9},{5,13},{9,17},{1... | collective-permute-start | bytes 589832 | tf_op jit(solution)/shard_map/ppermute | solution.py:33
  12.0 31.2 %collective-permute-start.1 = (f32[384,128]{1,0:T(8,128)}, f32[384,128]{1,0:T(8,128)S(1)}, u32[]{:S(2)}, u32[]{:S(2)}) collective-permute-start(f32[384,128]{1,0:T(8,128)} %get-tuple-element.27), channel_id=1, source_target_pairs={{0,4},{4,8},{8,12},{12,16},{16,20},{20,24},{24,28},{1,5},{5,9},{9,... | collective-permute-start | bytes 589832 | tf_op jit(solution)/shard_map/ppermute | solution.py:33
  13.9 29.3 %collective-permute-start.2 = (f32[384,128]{1,0:T(8,128)}, f32[384,128]{1,0:T(8,128)}, u32[]{:S(2)}, u32[]{:S(2)}) collective-permute-start(f32[384,128]{1,0:T(8,128)} %get-tuple-element.28), channel_id=1, source_target_pairs={{4,0},{8,4},{12,8},{16,12},{20,16},{24,20},{28,24},{5,1},{9,5},{13... | collective-permute-start | bytes 589832 | tf_op jit(solution)/shard_map/ppermute | solution.py:33
  18.4 24.8 %collective-permute-start.3 = (f32[384,128]{1,0:T(8,128)}, f32[384,128]{1,0:T(8,128)}, u32[]{:S(2)}, u32[]{:S(2)}) collective-permute-start(f32[384,128]{1,0:T(8,128)} %get-tuple-element.29), channel_id=1, source_target_pairs={{8,0},{12,4},{16,8},{20,12},{24,16},{28,20},{9,1},{13,5},{17,9},{2... | collective-permute-start | bytes 589832 | tf_op jit(solution)/shard_map/ppermute | solution.py:33
  61.4 10.2 %collective-permute-start.4 = (f32[384,128]{1,0:T(8,128)}, f32[384,128]{1,0:T(8,128)S(1)}, u32[]{:S(2)}, u32[]{:S(2)}) collective-permute-start(f32[384,128]{1,0:T(8,128)} %get-tuple-element.31), channel_id=1, source_target_pairs={{8,0},{12,4},{16,8},{20,12},{24,16},{28,20},{9,1},{13,5},{17,9},{2... | collective-permute-start | bytes 589832 | tf_op jit(solution)/shard_map/ppermute | solution.py:33
  63.3 8.3 %collective-permute-start.5 = (f32[384,128]{1,0:T(8,128)}, f32[384,128]{1,0:T(8,128)S(1)}, u32[]{:S(2)}, u32[]{:S(2)}) collective-permute-start(f32[384,128]{1,0:T(8,128)} %get-tuple-element.32), channel_id=1, source_target_pairs={{4,0},{8,4},{12,8},{16,12},{20,16},{24,20},{28,24},{5,1},{9,5},{13... | collective-permute-start | bytes 589832 | tf_op jit(solution)/shard_map/ppermute | solution.py:33
  65.2 8.1 %collective-permute-start.6 = (f32[384,128]{1,0:T(8,128)}, f32[384,128]{1,0:T(8,128)S(1)}, u32[]{:S(2)}, u32[]{:S(2)}) collective-permute-start(f32[384,128]{1,0:T(8,128)} %get-tuple-element.33), channel_id=1, source_target_pairs={{0,4},{4,8},{8,12},{12,16},{16,20},{20,24},{24,28},{1,5},{5,9},{9,... | collective-permute-start | bytes 589832 | tf_op jit(solution)/shard_map/ppermute | solution.py:33
  67.7 10.1 %collective-permute-start.7 = (f32[384,128]{1,0:T(8,128)}, f32[384,128]{1,0:T(8,128)S(1)}, u32[]{:S(2)}, u32[]{:S(2)}) collective-permute-start(f32[384,128]{1,0:T(8,128)} %get-tuple-element.34), channel_id=1, source_target_pairs={{0,8},{4,12},{8,16},{12,20},{16,24},{20,28},{1,9},{5,13},{9,17},{1... | collective-permute-start | bytes 589832 | tf_op jit(solution)/shard_map/ppermute | solution.py:33
  71.6 6.2 %copy-start.2 = (f32[384,128]{1,0:T(8,128)}, f32[384,128]{1,0:T(8,128)S(1)}, u32[]{:S(2)}) copy-start(f32[384,128]{1,0:T(8,128)S(1)} %collective-permute-done.4.rest_0_) | copy-start | bytes 589828
  83.6 9.7 %collective-permute-start.10 = (f32[384,128]{1,0:T(8,128)}, f32[384,128]{1,0:T(8,128)S(1)}, u32[]{:S(2)}, u32[]{:S(2)}) collective-permute-start(f32[384,128]{1,0:T(8,128)} %get-tuple-element.38), channel_id=1, source_target_pairs={{4,0},{8,4},{12,8},{16,12},{20,16},{24,20},{28,24},{5,1},{9,5},{13... | collective-permute-start | bytes 589832 | tf_op jit(solution)/shard_map/ppermute | solution.py:33
  85.6 10.1 %collective-permute-start.11 = (f32[384,128]{1,0:T(8,128)}, f32[384,128]{1,0:T(8,128)S(1)}, u32[]{:S(2)}, u32[]{:S(2)}) collective-permute-start(f32[384,128]{1,0:T(8,128)} %get-tuple-element.39), channel_id=1, source_target_pairs={{8,0},{12,4},{16,8},{20,12},{24,16},{28,20},{9,1},{13,5},{17,9},{2... | collective-permute-start | bytes 589832 | tf_op jit(solution)/shard_map/ppermute | solution.py:33
  87.5 10.6 %collective-permute-start.8 = (f32[384,128]{1,0:T(8,128)}, f32[384,128]{1,0:T(8,128)S(1)}, u32[]{:S(2)}, u32[]{:S(2)}) collective-permute-start(f32[384,128]{1,0:T(8,128)} %get-tuple-element.36), channel_id=1, source_target_pairs={{0,8},{4,12},{8,16},{12,20},{16,24},{20,28},{1,9},{5,13},{9,17},{1... | collective-permute-start | bytes 589832 | tf_op jit(solution)/shard_map/ppermute | solution.py:33
  91.4 8.4 %collective-permute-start.9 = (f32[384,128]{1,0:T(8,128)}, f32[384,128]{1,0:T(8,128)S(1)}, u32[]{:S(2)}, u32[]{:S(2)}) collective-permute-start(f32[384,128]{1,0:T(8,128)} %get-tuple-element.37), channel_id=1, source_target_pairs={{0,4},{4,8},{8,12},{12,16},{16,20},{20,24},{24,28},{1,5},{5,9},{9,... | collective-permute-start | bytes 589832 | tf_op jit(solution)/shard_map/ppermute | solution.py:33
  93.4 6.5 %copy-start.12 = (f32[384,128]{1,0:T(8,128)}, f32[384,128]{1,0:T(8,128)S(1)}, u32[]{:S(2)}) copy-start(f32[384,128]{1,0:T(8,128)S(1)} %collective-permute-done.10.rest_2_) | copy-start | bytes 589828
  118.0 10.2 %collective-permute-start.12 = (f32[384,128]{1,0:T(8,128)}, f32[384,128]{1,0:T(8,128)S(1)}, u32[]{:S(2)}, u32[]{:S(2)}) collective-permute-start(f32[384,128]{1,0:T(8,128)} %get-tuple-element.41), channel_id=1, source_target_pairs={{8,0},{12,4},{16,8},{20,12},{24,16},{28,20},{9,1},{13,5},{17,9},{2... | collective-permute-start | bytes 589832 | tf_op jit(solution)/shard_map/ppermute | solution.py:33
  119.9 8.3 %collective-permute-start.13 = (f32[384,128]{1,0:T(8,128)}, f32[384,128]{1,0:T(8,128)S(1)}, u32[]{:S(2)}, u32[]{:S(2)}) collective-permute-start(f32[384,128]{1,0:T(8,128)} %get-tuple-element.42), channel_id=1, source_target_pairs={{4,0},{8,4},{12,8},{16,12},{20,16},{24,20},{28,24},{5,1},{9,5},{13... | collective-permute-start | bytes 589832 | tf_op jit(solution)/shard_map/ppermute | solution.py:33
  121.8 8.1 %collective-permute-start.14 = (f32[384,128]{1,0:T(8,128)}, f32[384,128]{1,0:T(8,128)S(1)}, u32[]{:S(2)}, u32[]{:S(2)}) collective-permute-start(f32[384,128]{1,0:T(8,128)} %get-tuple-element.43), channel_id=1, source_target_pairs={{0,4},{4,8},{8,12},{12,16},{16,20},{20,24},{24,28},{1,5},{5,9},{9,... | collective-permute-start | bytes 589832 | tf_op jit(solution)/shard_map/ppermute | solution.py:33
  124.2 10.1 %collective-permute-start.15 = (f32[384,128]{1,0:T(8,128)}, f32[384,128]{1,0:T(8,128)S(1)}, u32[]{:S(2)}, u32[]{:S(2)}) collective-permute-start(f32[384,128]{1,0:T(8,128)} %get-tuple-element.44), channel_id=1, source_target_pairs={{0,8},{4,12},{8,16},{12,20},{16,24},{20,28},{1,9},{5,13},{9,17},{1... | collective-permute-start | bytes 589832 | tf_op jit(solution)/shard_map/ppermute | solution.py:33
  128.2 6.2 %copy-start.4 = (f32[384,128]{1,0:T(8,128)}, f32[384,128]{1,0:T(8,128)S(1)}, u32[]{:S(2)}) copy-start(f32[384,128]{1,0:T(8,128)S(1)} %collective-permute-done.12.rest_0_) | copy-start | bytes 589828
  128.2 6.1 %copy-start.6 = (f32[384,128]{1,0:T(8,128)}, f32[384,128]{1,0:T(8,128)S(1)}, u32[]{:S(2)}) copy-start(f32[384,128]{1,0:T(8,128)S(1)} %collective-permute-done.13.rest_1_) | copy-start | bytes 589828
  135.0 9.6 %copy-start.17 = (s32[1296]{0:T(1024)S(1)}, s32[1296]{0:T(1024)}, u32[]{:S(2)}) copy-start(s32[1296]{0:T(1024)} %param.16) | copy-start | bytes 15556
  135.0 9.6 %copy-start.18 = (s32[1296]{0:T(1024)S(1)}, s32[1296]{0:T(1024)}, u32[]{:S(2)}) copy-start(s32[1296]{0:T(1024)} %param.15) | copy-start | bytes 15556
  139.8 37.2 %all-to-all-start = ((f32[4,648,128]{2,1,0:T(8,128)}), f32[4,648,128]{2,1,0:T(8,128)S(1)}, u32[]{:S(2)}, u32[]{:S(2)}) async-start(f32[4,648,128]{2,1,0:T(8,128)} %bitcast.15), calls=%async_computation | async-start | bytes 2654208 | tf_op jit(solution)/shard_map/all_to_all | solution.py:301
  (14 other events, 37.4 us)
where the time goes:
time: 187 us; the launch traced here: 186 us
  Pallas kernels  56.9 us (30%)
  waiting for transfers between devices  50.5 us (27%)
  starting transfers between devices  47.2 us (25%)
  local copies, waits for them, and re-layouts  15.8 us (8%)
  other arithmetic  14.9 us (8%)
    ppermute x16, starting transfers between devices, passed_along(): lax.ppermute(value, axis, [(source, source + steps) for source in range(l...  42.3 us
    pallas_call x2, Pallas kernels, on_device(): pl.pallas_call(functools.partial(sweep_kernel, sub, shared, slots), out_s...  34.9 us
    all_to_all x1, waiting for transfers between devices, on_device(): lax.all_to_all(leaving.reshape(spec_count, row_count * halves, LANES), 's...  31.7 us
    ppermute x16, waiting for transfers between devices, passed_along(): lax.ppermute(value, axis, [(source, source + steps) for source in range(l...  18.8 us
    mul x4, local copies, waits for them, and re-layouts, on_device(): weight = (step_weight[:, None, None] * speed).reshape(own_rows, LANES)  7.73 us
    pallas_call x1, Pallas kernels, on_device(): pl.pallas_call(functools.partial(interact_kernel, halves), out_shape=shap...  7.58 us
    pallas_call x1, Pallas kernels, on_device(): pl.pallas_call(functools.partial(between_kernel, sub, slots), out_shape=[...  5.2 us
    all_to_all x1, starting transfers between devices, on_device(): lax.all_to_all(leaving.reshape(spec_count, row_count * halves, LANES), 's...  4.87 us
  transfers between devices with their start and end apart: 17, of which 8 were waited for; matrix products, arithmetic and copies ran while one was open for 12% of the time, Pallas kernels for 0%

commit v1 on v0

--- a/solution.py
+++ b/solution.py
@@ -44,21 +44,59 @@
         @pl.loop(0, slots // unroll)
         def _(k):
             first = k * unroll
+            listed = send.at[pl.ds((BLOCKS - 1 - position) * slots + first, unroll)]
             for u in range(unroll):
-                row = send[(BLOCKS - 1 - position) * slots + first + u]
-                outs[position][pl.ds((first + u) * sub, sub), :] = energy[pl.ds(row, sub), :]
-
-
-def enter_kernel(sub, lanes, slots, send, spectrum, energy, *outs):
-    owned = spectrum.shape[2]
-
-    @pl.loop(0, owned // LANES)
-    def _(k):
+                outs[position][pl.ds((first + u) * sub, sub), :] = energy[pl.ds(listed[u], sub), :]
+
+
+def enter_kernel(sub, lanes, slots, send, spectrum, energy, *rest):
+    outs, square = rest[:BLOCKS], rest[BLOCKS]
+    owned = spectrum.shape[1]
+    square[...] = jnp.zeros_like(square)
+    for block in range(owned // LANES):
         for part in range(sub):
-            block = spectrum[part, :, pl.ds(pl.multiple_of(k * LANES, LANES), LANES)]
-            energy[pl.ds(k * LANES * sub + part, LANES, stride=sub), :] = block.T
-
+            slot = square.at[(block * sub + part) % square.shape[0]]
+            slot[:lanes, :] = spectrum[part * lanes : (part + 1) * lanes, block * LANES : (block + 1) * LANES]
+            energy[pl.ds(block * LANES * sub + part, LANES, stride=sub), :] = slot[...].T
     pack_rows(sub, slots, send, energy, outs)
+
+
+def slope_kernel(sub, shared, normals, step_weight, wave, coef, weight, lines):
+    elements = normals.shape[2]
+    parts = 1 if shared else sub
+    pitch = coef.shape[0] // elements
+    lines[...] = jnp.zeros_like(lines)
+    for component in range(2):
+        for corner in range(2):
+            row = component * 2 + corner
+            lines[row : row + 1, :] = normals[component, corner : corner + 1, :]
+
+    def spread(column):
+        return jnp.broadcast_to(column, (8, LANES))
+
+    @pl.loop(0, elements // LANES)
+    def _(k):
+        turned = lines[:, pl.ds(pl.multiple_of(k * LANES, LANES), LANES)].T
+        for group in range(LANES // 8):
+            at = slice(group * 8, group * 8 + 8)
+            x0, x1, y0, y1 = (spread(turned[at, j : j + 1]) for j in range(4))
+            base = (k * LANES + group * 8) * pitch
+            for part in range(parts):
+                east, north = wave[part : part + 1, :], wave[sub + part : sub + part + 1, :]
+                first = x0 * east + y0 * north
+                second = x1 * east + y1 * north
+                inward = jnp.minimum(first, 0.0) + jnp.minimum(second, 0.0) - jnp.maximum(first + second, 0.0)
+                for which, value in enumerate((first, second, 1.0 / inward)):
+                    coef[pl.ds(base + which * parts + part, 8, stride=pitch), :] = value
+
+    nodes = step_weight.shape[1]
+    for block in range(nodes // LANES):
+        turned = jnp.broadcast_to(step_weight[0:1, block * LANES : (block + 1) * LANES], (8, LANES)).T
+        for group in range(LANES // 8):
+            value = spread(turned[group * 8 : group * 8 + 8, 0:1])
+            for part in range(sub):
+                at = pl.ds((block * LANES + group * 8) * sub + part, 8, stride=sub)
+                weight[at, :] = value * wave[2 * sub + part : 2 * sub + part + 1, :]
 
 
 def sweep_kernel(sub, shared, slots, conn, energy, coef, weight, *rest):
@@ -69,6 +107,8 @@
     ghost_rows = slots * sub
     rows = full.shape[0]
     elements = conn.shape[0] // 3
+    parts = 1 if shared else sub
+    pitch = coef.shape[0] // elements
     step = chunked(rows, 64)
     zero = jnp.zeros((step, LANES), jnp.float32)
 
@@ -85,25 +125,33 @@
     share = elements // GROUPS
     unroll = chunked(share, 16)
 
-    def coef_rows(which, element):
-        if shared:
-            return coef[pl.ds(which * elements + element, sub, stride=0), :]
-        return coef[pl.ds((which * elements + element) * sub, sub), :]
-
     @pl.loop(0, share // unroll)
     def _(k):
+        listed = [
+            [conn.at[pl.ds(corner * elements + group * share + k * unroll, unroll)] for corner in range(3)]
+            for group in range(GROUPS)
+        ]
         for u in range(unroll):
             for group in range(GROUPS):
                 element = group * share + k * unroll + u
-                index = [conn[corner * elements + element] for corner in range(3)]
+                index = [item[u] for item in listed[group]]
                 value = [full[pl.ds(row, sub), :] for row in index]
-                inflow = coef_rows(3, element) * value[0]
-                inflow = inflow + coef_rows(4, element) * value[1]
-                inflow = inflow + coef_rows(5, element) * value[2]
+                tile = coef[pl.ds(element * pitch, pitch), :]
+                first, second, inverse = (
+                    jnp.broadcast_to(tile[j * parts : (j + 1) * parts], (sub, LANES)) for j in range(3)
+                )
+                both = first + second
+                inflow = jnp.minimum(first, 0.0) * value[0] + jnp.minimum(second, 0.0) * value[1]
+                inflow = (inflow - jnp.maximum(both, 0.0) * value[2]) * inverse
+                residual = (
+                    jnp.maximum(first, 0.0) * (value[0] - inflow),
+                    jnp.maximum(second, 0.0) * (value[1] - inflow),
+                    jnp.minimum(both, 0.0) * (inflow - value[2]),
+                )
                 for corner in range(3):
-                    part = coef_rows(corner, element) * (value[corner] - inflow)
                     item = sums[group * 3 + corner]
-                    item[pl.ds(index[corner], sub), :] = item[pl.ds(index[corner], sub), :] + part
+                    at = pl.ds(index[corner], sub)
+                    item[at, :] = item[at, :] + residual[corner]
 
     def total(at):
         result = sums[0][at, :]
@@ -135,7 +183,8 @@
         @pl.loop(0, slots // unroll)
         def _(k):
             first = k * unroll
-            rows = [send[(BLOCKS - 1 - position) * slots + first + u] for u in range(unroll)]
+            listed = send.at[pl.ds((BLOCKS - 1 - position) * slots + first, unroll)]
+            rows = [listed[u] for u in range(unroll)]
             fresh = [
                 energy[pl.ds(row, sub), :]
                 - weight[pl.ds(row, sub), :] * incoming[position][pl.ds((first + u) * sub, sub), :]
@@ -216,6 +265,10 @@
 
 def cost(flops, moved):
     return pl.CostEstimate(flops=flops, bytes_accessed=moved, transcendentals=0)
+
+
+def limit(mebibytes):
+    return pltpu.CompilerParams(vmem_limit_bytes=mebibytes << 20)
 
 
 def on_device(
@@ -248,24 +301,30 @@
     east, north = jnp.cos(angle), jnp.sin(angle)
     select = ((bin_of // NDIR)[:, :, None] == jnp.arange(group_speed.shape[0], dtype=jnp.int32)).astype(jnp.float32)
     speed = jnp.sum(select * group_speed, axis=2)
-    if shared:
-        east, north = east[:1], north[:1]
-    slope = normals[0][:, :, None, None] * east + normals[1][:, :, None, None] * north
-    inward = jnp.minimum(slope, 0.0)
-    share = inward / jnp.sum(inward, axis=0)
-    coef = jnp.concatenate([jnp.maximum(slope, 0.0), share]).reshape(-1, LANES)
-    weight = (step_weight[:, None, None] * speed).reshape(own_rows, LANES)
-
-    padded = jnp.pad(spectrum.reshape(sub, lanes, owned), ((0, 0), (0, LANES - lanes), (0, 0)))
+    wave = jnp.concatenate([east, north, speed])
+
     block_shapes = [shape_of(ghost_rows, LANES)] * BLOCKS
     energy, *outs = pl.pallas_call(
         functools.partial(enter_kernel, sub, lanes, slots),
         out_shape=[shape_of(own_rows, LANES)] + block_shapes,
         in_specs=[SM, VM],
         out_specs=[VM] * (1 + BLOCKS),
+        scratch_shapes=[pltpu.VMEM((4, LANES, LANES), jnp.float32)],
         cost_estimate=cost(0, 8 * own_rows * LANES),
+        compiler_params=limit(8),
         name="enter",
-    )(send, padded)
+    )(send, spectrum)
+    pitch = 3 if shared else 3 * sub
+    coef, weight = pl.pallas_call(
+        functools.partial(slope_kernel, sub, shared),
+        out_shape=[shape_of(elements * pitch, LANES), shape_of(own_rows, LANES)],
+        in_specs=[VM] * 3,
+        out_specs=[VM] * 2,
+        scratch_shapes=[pltpu.VMEM((LANES, elements), jnp.float32)],
+        cost_estimate=cost(20 * elements * LANES, 4 * LANES * (elements * pitch + own_rows)),
+        compiler_params=limit(12),
+        name="slopes",
+    )(normals, step_weight.reshape(1, owned), wave)
 
     for sweep_index in range(STEPS):
         ghosts = [passed_along(outs[p], "dom", -offset_of(p)) for p in range(BLOCKS)]
@@ -275,7 +334,8 @@
             in_specs=[SM] + [VM] * (3 + BLOCKS),
             out_specs=[VM] * (1 + BLOCKS),
             scratch_shapes=[pltpu.VMEM((rows, LANES), jnp.float32)] * (1 + 3 * GROUPS),
-            cost_estimate=cost(elements * 24 * row_count, 4 * LANES * (8 * elements + 4 * rows)),
+            cost_estimate=cost(elements * 24 * row_count, 4 * LANES * (3 * elements + 4 * rows)),
+            compiler_params=limit(32),
             name="sweep",
         )(nodes, energy, coef, weight, *ghosts)
         incoming = [passed_along(returned[p], "dom", offset_of(p)) for p in range(BLOCKS)]
@@ -286,6 +346,7 @@
                 in_specs=[SM] + [VM] * (2 + BLOCKS),
                 out_specs=[VM] * (1 + BLOCKS),
                 cost_estimate=cost(2 * owned * row_count, 16 * own_rows * LANES),
+                compiler_params=limit(8),
                 name="between",
             )(send, partial, weight, *incoming)
 
@@ -296,6 +357,7 @@
         out_specs=VM,
         scratch_shapes=[pltpu.VMEM((own_rows, LANES), jnp.float32)],
         cost_estimate=cost(2 * owned * row_count, 16 * own_rows * LANES),
+        compiler_params=limit(8),
         name="leave",
     )(send, partial, weight, *incoming)
     arrived = lax.all_to_all(
@@ -308,6 +370,7 @@
         out_specs=VM,
         scratch_shapes=[pltpu.VMEM((bins * halves, LANES), jnp.float32)] * (1 + 2 * GROUPS),
         cost_estimate=cost(16 * bins * halves * LANES, 8 * bins * halves * LANES),
+        compiler_params=limit(12),
         name="interact",
     )(dia_plus * halves, dia_minus * halves, dia_coeff, arrived.reshape(bins * halves, LANES))
 

time: 187 us -> 145 us (0.78)
  Pallas kernels: 56.9 us -> 40.9 us
  local copies, waits for them, and re-layouts: 15.8 us -> 2.21 us
  other arithmetic: 14.9 us -> 1.78 us
    pallas_call x2, Pallas kernels: 34.9 us -> 21.6 us  [on_device(): pl.pallas_call(functools.partial(sweep_kernel, sub, shared, slots), out_s...]
    mul x5 -> x0, local copies, waits for them, and re-layouts: 7.73 us -> none  [the longest x4 7.73 us: on_device(): weight = (step_weight[:, None, None] * speed).reshape(own_rows, LANES)]
    pallas_call x0 -> x1, Pallas kernels: none -> 4.88 us  [on_device(): pl.pallas_call(functools.partial(slope_kernel, sub, shared), out_shape=[s...]
    div x1 -> x0, other arithmetic: 3.25 us -> none  [on_device(): share = inward / jnp.sum(inward, axis=0)]
    mul x1 -> x0, other arithmetic: 3.17 us -> none  [on_device(): weight = (step_weight[:, None, None] * speed).reshape(own_rows, LANES)]
    concatenate x1, other arithmetic: 3.09 us -> 0.01 us  [on_device(): wave = jnp.concatenate([east, north, speed])]
    pallas_call x1, Pallas kernels: 4.49 us -> 1.62 us  [on_device(): pl.pallas_call(functools.partial(enter_kernel, sub, lanes, slots), out_sh...]
    pallas_call x1, Pallas kernels: 5.2 us -> 2.4 us  [on_device(): pl.pallas_call(functools.partial(between_kernel, sub, slots), out_shape=[...]
  transfers between devices with their start and end apart: 17 -> 17, of which waited for: 8 -> 8; matrix products, arithmetic and copies ran while one was open for 12% -> 1% of each run, Pallas kernels for 0% -> 3%
where the time goes in v1:
time: 145 us; the launch traced here: 144 us
  waiting for transfers between devices  52 us (36%)
  starting transfers between devices  47.4 us (33%)
  Pallas kernels  40.9 us (28%)
  local copies, waits for them, and re-layouts  2.21 us (2%)
  other arithmetic  1.78 us (1%)
    ppermute x16, starting transfers between devices, passed_along(): lax.ppermute(value, axis, [(source, source + steps) for source in range(l...  42.4 us
    all_to_all x1, waiting for transfers between devices, on_device(): lax.all_to_all(leaving.reshape(spec_count, row_count * halves, LANES), 's...  32.3 us
    pallas_call x2, Pallas kernels, on_device(): pl.pallas_call(functools.partial(sweep_kernel, sub, shared, slots), out_s...  21.6 us
    ppermute x16, waiting for transfers between devices, passed_along(): lax.ppermute(value, axis, [(source, source + steps) for source in range(l...  19.6 us
    pallas_call x1, Pallas kernels, on_device(): pl.pallas_call(functools.partial(interact_kernel, halves), out_shape=shap...  7.02 us
    all_to_all x1, starting transfers between devices, on_device(): lax.all_to_all(leaving.reshape(spec_count, row_count * halves, LANES), 's...  5 us
    pallas_call x1, Pallas kernels, on_device(): pl.pallas_call(functools.partial(slope_kernel, sub, shared), out_shape=[s...  4.88 us
    pallas_call x1, Pallas kernels, on_device(): pl.pallas_call(functools.partial(leave_kernel, sub, lanes, slots, halves)...  3.3 us
  transfers between devices with their start and end apart: 17, of which 8 were waited for; matrix products, arithmetic and copies ran while one was open for 1% of the time, Pallas kernels for 3%

profile of v1, /device:TPU:4, one launch (start us, length us, event | category | flops | bytes accessed | tf_op | source)
XLA Modules:
  0.0 144.4 jit_solution(15783130736458226532)
XLA Ops:
  3.7 3.4 %collective-permute-start = (f32[384,128]{1,0:T(8,128)S(1)}, f32[384,128]{1,0:T(8,128)S(1)}, u32[]{:S(2)}, u32[]{:S(2)}) collective-permute-start(f32[384,128]{1,0:T(8,128)S(1)} %get-tuple-element.30), channel_id=1, source_target_pairs={{0,8},{4,12},{8,16},{12,20},{16,24},{20,28},{1,9},{5,13},{9,17},{1... | collective-permute-start | bytes 589832 | tf_op jit(solution)/shard_map/ppermute | solution.py:33
  7.1 1.9 %collective-permute-start.1 = (f32[384,128]{1,0:T(8,128)S(1)}, f32[384,128]{1,0:T(8,128)S(1)}, u32[]{:S(2)}, u32[]{:S(2)}) collective-permute-start(f32[384,128]{1,0:T(8,128)S(1)} %get-tuple-element.31), channel_id=1, source_target_pairs={{0,4},{4,8},{8,12},{12,16},{16,20},{20,24},{24,28},{1,5},{5,9},{9,... | collective-permute-start | bytes 589832 | tf_op jit(solution)/shard_map/ppermute | solution.py:33
  9.0 4.5 %collective-permute-start.2 = (f32[384,128]{1,0:T(8,128)S(1)}, f32[384,128]{1,0:T(8,128)S(1)}, u32[]{:S(2)}, u32[]{:S(2)}) collective-permute-start(f32[384,128]{1,0:T(8,128)S(1)} %get-tuple-element.32), channel_id=1, source_target_pairs={{4,0},{8,4},{12,8},{16,12},{20,16},{24,20},{28,24},{5,1},{9,5},{13... | collective-permute-start | bytes 589832 | tf_op jit(solution)/shard_map/ppermute | solution.py:33
  13.5 2.4 %collective-permute-start.3 = (f32[384,128]{1,0:T(8,128)S(1)}, f32[384,128]{1,0:T(8,128)S(1)}, u32[]{:S(2)}, u32[]{:S(2)}) collective-permute-start(f32[384,128]{1,0:T(8,128)S(1)} %get-tuple-element.33), channel_id=1, source_target_pairs={{8,0},{12,4},{16,8},{20,12},{24,16},{28,20},{9,1},{13,5},{17,9},{2... | collective-permute-start | bytes 589832 | tf_op jit(solution)/shard_map/ppermute | solution.py:33
  18.0 4.9 %slopes.1 = (f32[6144,128]{1,0:T(8,128)S(1)}, f32[3072,128]{1,0:T(8,128)S(1)}) custom-call(f32[2,3,2048]{2,1,0:T(4,128)S(1)} %copy.11.normals, f32[1,1024]{1,0:T(1,128)S(1)} %bitcast.6, f32[9,128]{1,0:T(8,128)S(1)} %pad_maximum_fusion.wave), custom_call_target="tpu_custom_call" | custom-call | flops 5242880 | bytes 4718592 | tf_op jit(solution)/shard_map/slopes/pallas_call | solution.py:318
  22.9 10.8 %sweep.2 = (f32[3072,128]{1,0:T(8,128)S(1)}, f32[384,128]{1,0:T(8,128)S(1)}, f32[384,128]{1,0:T(8,128)S(1)}, f32[384,128]{1,0:T(8,128)S(1)}, f32[384,128]{1,0:T(8,128)S(1)}) custom-call(s32[6144]{0:T(1024)S(1)} %reshape.52.conn, f32[3072,128]{1,0:T(8,128)S(1)} %get-tuple-element.27.energy, f32[6144,128]{1,0:T(8,128)S(1)} %get-tuple-element.28.coef, ...), custom_call_target="tpu_custom_call" | custom-call | flops 15925248 | bytes 12582912 | tf_op jit(solution)/shard_map/sweep/pallas_call | solution.py:331
  33.7 3.3 %collective-permute-start.4 = (f32[384,128]{1,0:T(8,128)S(1)}, f32[384,128]{1,0:T(8,128)S(1)}, u32[]{:S(2)}, u32[]{:S(2)}) collective-permute-start(f32[384,128]{1,0:T(8,128)S(1)} %get-tuple-element.35), channel_id=1, source_target_pairs={{8,0},{12,4},{16,8},{20,12},{24,16},{28,20},{9,1},{13,5},{17,9},{2... | collective-permute-start | bytes 589832 | tf_op jit(solution)/shard_map/ppermute | solution.py:33
  37.0 1.9 %collective-permute-start.5 = (f32[384,128]{1,0:T(8,128)S(1)}, f32[384,128]{1,0:T(8,128)S(1)}, u32[]{:S(2)}, u32[]{:S(2)}) collective-permute-start(f32[384,128]{1,0:T(8,128)S(1)} %get-tuple-element.36), channel_id=1, source_target_pairs={{4,0},{8,4},{12,8},{16,12},{20,16},{24,20},{28,24},{5,1},{9,5},{13... | collective-permute-start | bytes 589832 | tf_op jit(solution)/shard_map/ppermute | solution.py:33
  38.9 2.4 %collective-permute-start.6 = (f32[384,128]{1,0:T(8,128)S(1)}, f32[384,128]{1,0:T(8,128)S(1)}, u32[]{:S(2)}, u32[]{:S(2)}) collective-permute-start(f32[384,128]{1,0:T(8,128)S(1)} %get-tuple-element.37), channel_id=1, source_target_pairs={{0,4},{4,8},{8,12},{12,16},{16,20},{20,24},{24,28},{1,5},{5,9},{9,... | collective-permute-start | bytes 589832 | tf_op jit(solution)/shard_map/ppermute | solution.py:33
  41.3 2.6 %collective-permute-start.7 = (f32[384,128]{1,0:T(8,128)S(1)}, f32[384,128]{1,0:T(8,128)S(1)}, u32[]{:S(2)}, u32[]{:S(2)}) collective-permute-start(f32[384,128]{1,0:T(8,128)S(1)} %get-tuple-element.38), channel_id=1, source_target_pairs={{0,8},{4,12},{8,16},{12,20},{16,24},{20,28},{1,9},{5,13},{9,17},{1... | collective-permute-start | bytes 589832 | tf_op jit(solution)/shard_map/ppermute | solution.py:33
  43.9 2.9 %collective-permute-done.6.rest_2_ = f32[384,128]{1,0:T(8,128)S(1)} collective-permute-done((f32[384,128]{1,0:T(8,128)S(1)}, f32[384,128]{1,0:T(8,128)S(1)}, u32[]{:S(2)}, u32[]{:S(2)}) %collective-permute-start.6) | collective-permute-done | bytes 196640 | tf_op jit(solution)/shard_map/ppermute | solution.py:33
  46.8 4.5 %collective-permute-done.7.rest_3_ = f32[384,128]{1,0:T(8,128)S(1)} collective-permute-done((f32[384,128]{1,0:T(8,128)S(1)}, f32[384,128]{1,0:T(8,128)S(1)}, u32[]{:S(2)}, u32[]{:S(2)}) %collective-permute-start.7) | collective-permute-done | bytes 196640 | tf_op jit(solution)/shard_map/ppermute | solution.py:33
  51.3 2.4 %between.1 = (f32[3072,128]{1,0:T(8,128)S(1)}, f32[384,128]{1,0:T(8,128)S(1)}, f32[384,128]{1,0:T(8,128)S(1)}, f32[384,128]{1,0:T(8,128)S(1)}, f32[384,128]{1,0:T(8,128)S(1)}) custom-call(s32[512]{0:T(512)S(1)} %multiply_bitcast_fusion.send, f32[3072,128]{1,0:T(8,128)S(1)} %get-tuple-element.34.partial, f32[3072,128]{1,0:T(8,128)S(1)} %get-tuple-element.29.weight, ...), custom_call_target="tpu_custom_call" | custom-call | flops 663552 | bytes 6291456 | tf_op jit(solution)/shard_map/between/pallas_call | solution.py:343
  57.5 3.9 %collective-permute-start.8 = (f32[384,128]{1,0:T(8,128)S(1)}, f32[384,128]{1,0:T(8,128)S(1)}, u32[]{:S(2)}, u32[]{:S(2)}) collective-permute-start(f32[384,128]{1,0:T(8,128)S(1)} %get-tuple-element.40), channel_id=1, source_target_pairs={{0,8},{4,12},{8,16},{12,20},{16,24},{20,28},{1,9},{5,13},{9,17},{1... | collective-permute-start | bytes 589832 | tf_op jit(solution)/shard_map/ppermute | solution.py:33
  61.5 1.9 %collective-permute-start.9 = (f32[384,128]{1,0:T(8,128)S(1)}, f32[384,128]{1,0:T(8,128)S(1)}, u32[]{:S(2)}, u32[]{:S(2)}) collective-permute-start(f32[384,128]{1,0:T(8,128)S(1)} %get-tuple-element.41), channel_id=1, source_target_pairs={{0,4},{4,8},{8,12},{12,16},{16,20},{20,24},{24,28},{1,5},{5,9},{9,... | collective-permute-start | bytes 589832 | tf_op jit(solution)/shard_map/ppermute | solution.py:33
  64.8 3.2 %collective-permute-done.8.rest_0_ = f32[384,128]{1,0:T(8,128)S(1)} collective-permute-done((f32[384,128]{1,0:T(8,128)S(1)}, f32[384,128]{1,0:T(8,128)S(1)}, u32[]{:S(2)}, u32[]{:S(2)}) %collective-permute-start.8) | collective-permute-done | bytes 196640 | tf_op jit(solution)/shard_map/ppermute | solution.py:33
  69.7 10.9 %sweep.3 = (f32[3072,128]{1,0:T(8,128)S(1)}, f32[384,128]{1,0:T(8,128)S(1)}, f32[384,128]{1,0:T(8,128)S(1)}, f32[384,128]{1,0:T(8,128)S(1)}, f32[384,128]{1,0:T(8,128)S(1)}) custom-call(s32[6144]{0:T(1024)S(1)} %reshape.52.conn, f32[3072,128]{1,0:T(8,128)S(1)} %get-tuple-element.39.energy, f32[6144,128]{1,0:T(8,128)S(1)} %get-tuple-element.28.coef, ...), custom_call_target="tpu_custom_call" | custom-call | flops 15925248 | bytes 12582912 | tf_op jit(solution)/shard_map/sweep/pallas_call | solution.py:331
  84.5 2.4 %collective-permute-start.14 = (f32[384,128]{1,0:T(8,128)S(1)}, f32[384,128]{1,0:T(8,128)S(1)}, u32[]{:S(2)}, u32[]{:S(2)}) collective-permute-start(f32[384,128]{1,0:T(8,128)S(1)} %get-tuple-element.47), channel_id=1, source_target_pairs={{0,4},{4,8},{8,12},{12,16},{16,20},{20,24},{24,28},{1,5},{5,9},{9,... | collective-permute-start | bytes 589832 | tf_op jit(solution)/shard_map/ppermute | solution.py:33
  86.9 3.9 %collective-permute-start.15 = (f32[384,128]{1,0:T(8,128)S(1)}, f32[384,128]{1,0:T(8,128)S(1)}, u32[]{:S(2)}, u32[]{:S(2)}) collective-permute-start(f32[384,128]{1,0:T(8,128)S(1)} %get-tuple-element.48), channel_id=1, source_target_pairs={{0,8},{4,12},{8,16},{12,20},{16,24},{20,28},{1,9},{5,13},{9,17},{1... | collective-permute-start | bytes 589832 | tf_op jit(solution)/shard_map/ppermute | solution.py:33
  92.3 4.4 %collective-permute-done.15.rest_3_ = f32[384,128]{1,0:T(8,128)S(1)} collective-permute-done((f32[384,128]{1,0:T(8,128)S(1)}, f32[384,128]{1,0:T(8,128)S(1)}, u32[]{:S(2)}, u32[]{:S(2)}) %collective-permute-start.15) | collective-permute-done | bytes 196640 | tf_op jit(solution)/shard_map/ppermute | solution.py:33
  96.8 3.3 %leave.1 = f32[2592,128]{1,0:T(8,128)} custom-call(s32[512]{0:T(512)S(1)} %multiply_bitcast_fusion.send, f32[3072,128]{1,0:T(8,128)S(1)} %get-tuple-element.44.partial, f32[3072,128]{1,0:T(8,128)S(1)} %get-tuple-element.29.weight, f32[384,128]{1,0:T(8,128)S(1)} %collective-permute-done.12.rest_0_, f32[384,128]{1,0:T(8,128)S(1)} %collective-permute-done.13.rest_1_, ...), custom_call_target="tpu_custom_call" | custom-call | flops 663552 | bytes 6291456 | tf_op jit(solution)/shard_map/leave/pallas_call | solution.py:353
  100.1 5.0 %all-to-all-start = ((f32[4,648,128]{2,1,0:T(8,128)}), f32[4,648,128]{2,1,0:T(8,128)S(1)}, u32[]{:S(2)}, u32[]{:S(2)}) async-start(f32[4,648,128]{2,1,0:T(8,128)} %bitcast.2), calls=%async_computation | async-start | bytes 2654208 | tf_op jit(solution)/shard_map/all_to_all | solution.py:363
  105.1 32.3 %all-to-all-done = f32[4,648,128]{2,1,0:T(8,128)S(1)} async-done(((f32[4,648,128]{2,1,0:T(8,128)}), f32[4,648,128]{2,1,0:T(8,128)S(1)}, u32[]{:S(2)}, u32[]{:S(2)}) %all-to-all-start) | async-done | bytes 1327136 | tf_op jit(solution)/shard_map/all_to_all | solution.py:363
  137.4 7.0 %interact.1 = f32[1296,256]{1,0:T(8,128)} custom-call(s32[1296]{0:T(1024)S(1)} %get-tuple-element.52.plus, s32[1296]{0:T(1024)S(1)} %get-tuple-element.51.minus, f32[1296]{0:T(1024)S(1)} %copy-done.1, f32[2592,128]{1,0:T(8,128)S(1)} %bitcast.5), custom_call_target="tpu_custom_call" | custom-call | flops 5308416 | bytes 2654208 | tf_op jit(solution)/shard_map/interact/pallas_call | solution.py:366
  (39 shorter events, 17.9 us)
Async XLA Ops:
  0.0 18.0 %copy-start.2 = (f32[1024]{0:T(1024)S(1)}, f32[1024]{0:T(1024)}, u32[]{:S(2)}) copy-start(f32[1024]{0:T(1024)} %param.13) | copy-start | bytes 12292
  0.7 1.3 copy-start
  2.0 15.8 %copy-start.5 = (f32[36]{0:T(128)S(1)}, f32[36]{0:T(128)}, u32[]{:S(2)}) copy-start(f32[36]{0:T(128)} %param.14) | copy-start | bytes 436
  3.7 19.2 %collective-permute-start = (f32[384,128]{1,0:T(8,128)S(1)}, f32[384,128]{1,0:T(8,128)S(1)}, u32[]{:S(2)}, u32[]{:S(2)}) collective-permute-start(f32[384,128]{1,0:T(8,128)S(1)} %get-tuple-element.30), channel_id=1, source_target_pairs={{0,8},{4,12},{8,16},{12,20},{16,24},{20,28},{1,9},{5,13},{9,17},{1... | collective-permute-start | bytes 589832 | tf_op jit(solution)/shard_map/ppermute | solution.py:33
  7.1 15.8 %collective-permute-start.1 = (f32[384,128]{1,0:T(8,128)S(1)}, f32[384,128]{1,0:T(8,128)S(1)}, u32[]{:S(2)}, u32[]{:S(2)}) collective-permute-start(f32[384,128]{1,0:T(8,128)S(1)} %get-tuple-element.31), channel_id=1, source_target_pairs={{0,4},{4,8},{8,12},{12,16},{16,20},{20,24},{24,28},{1,5},{5,9},{9,... | collective-permute-start | bytes 589832 | tf_op jit(solution)/shard_map/ppermute | solution.py:33
  9.0 13.9 %collective-permute-start.2 = (f32[384,128]{1,0:T(8,128)S(1)}, f32[384,128]{1,0:T(8,128)S(1)}, u32[]{:S(2)}, u32[]{:S(2)}) collective-permute-start(f32[384,128]{1,0:T(8,128)S(1)} %get-tuple-element.32), channel_id=1, source_target_pairs={{4,0},{8,4},{12,8},{16,12},{20,16},{24,20},{28,24},{5,1},{9,5},{13... | collective-permute-start | bytes 589832 | tf_op jit(solution)/shard_map/ppermute | solution.py:33
  13.5 9.3 %collective-permute-start.3 = (f32[384,128]{1,0:T(8,128)S(1)}, f32[384,128]{1,0:T(8,128)S(1)}, u32[]{:S(2)}, u32[]{:S(2)}) collective-permute-start(f32[384,128]{1,0:T(8,128)S(1)} %get-tuple-element.33), channel_id=1, source_target_pairs={{8,0},{12,4},{16,8},{20,12},{24,16},{28,20},{9,1},{13,5},{17,9},{2... | collective-permute-start | bytes 589832 | tf_op jit(solution)/shard_map/ppermute | solution.py:33
  33.7 10.2 %collective-permute-start.4 = (f32[384,128]{1,0:T(8,128)S(1)}, f32[384,128]{1,0:T(8,128)S(1)}, u32[]{:S(2)}, u32[]{:S(2)}) collective-permute-start(f32[384,128]{1,0:T(8,128)S(1)} %get-tuple-element.35), channel_id=1, source_target_pairs={{8,0},{12,4},{16,8},{20,12},{24,16},{28,20},{9,1},{13,5},{17,9},{2... | collective-permute-start | bytes 589832 | tf_op jit(solution)/shard_map/ppermute | solution.py:33
  37.0 6.9 %collective-permute-start.5 = (f32[384,128]{1,0:T(8,128)S(1)}, f32[384,128]{1,0:T(8,128)S(1)}, u32[]{:S(2)}, u32[]{:S(2)}) collective-permute-start(f32[384,128]{1,0:T(8,128)S(1)} %get-tuple-element.36), channel_id=1, source_target_pairs={{4,0},{8,4},{12,8},{16,12},{20,16},{24,20},{28,24},{5,1},{9,5},{13... | collective-permute-start | bytes 589832 | tf_op jit(solution)/shard_map/ppermute | solution.py:33
  38.9 7.9 %collective-permute-start.6 = (f32[384,128]{1,0:T(8,128)S(1)}, f32[384,128]{1,0:T(8,128)S(1)}, u32[]{:S(2)}, u32[]{:S(2)}) collective-permute-start(f32[384,128]{1,0:T(8,128)S(1)} %get-tuple-element.37), channel_id=1, source_target_pairs={{0,4},{4,8},{8,12},{12,16},{16,20},{20,24},{24,28},{1,5},{5,9},{9,... | collective-permute-start | bytes 589832 | tf_op jit(solution)/shard_map/ppermute | solution.py:33
  41.3 9.9 %collective-permute-start.7 = (f32[384,128]{1,0:T(8,128)S(1)}, f32[384,128]{1,0:T(8,128)S(1)}, u32[]{:S(2)}, u32[]{:S(2)}) collective-permute-start(f32[384,128]{1,0:T(8,128)S(1)} %get-tuple-element.38), channel_id=1, source_target_pairs={{0,8},{4,12},{8,16},{12,20},{16,24},{20,28},{1,9},{5,13},{9,17},{1... | collective-permute-start | bytes 589832 | tf_op jit(solution)/shard_map/ppermute | solution.py:33
  53.7 9.7 %collective-permute-start.10 = (f32[384,128]{1,0:T(8,128)S(1)}, f32[384,128]{1,0:T(8,128)S(1)}, u32[]{:S(2)}, u32[]{:S(2)}) collective-permute-start(f32[384,128]{1,0:T(8,128)S(1)} %get-tuple-element.42), channel_id=1, source_target_pairs={{4,0},{8,4},{12,8},{16,12},{20,16},{24,20},{28,24},{5,1},{9,5},{13... | collective-permute-start | bytes 589832 | tf_op jit(solution)/shard_map/ppermute | solution.py:33
  55.6 9.2 %collective-permute-start.11 = (f32[384,128]{1,0:T(8,128)S(1)}, f32[384,128]{1,0:T(8,128)S(1)}, u32[]{:S(2)}, u32[]{:S(2)}) collective-permute-start(f32[384,128]{1,0:T(8,128)S(1)} %get-tuple-element.43), channel_id=1, source_target_pairs={{8,0},{12,4},{16,8},{20,12},{24,16},{28,20},{9,1},{13,5},{17,9},{2... | collective-permute-start | bytes 589832 | tf_op jit(solution)/shard_map/ppermute | solution.py:33
  57.5 10.5 %collective-permute-start.8 = (f32[384,128]{1,0:T(8,128)S(1)}, f32[384,128]{1,0:T(8,128)S(1)}, u32[]{:S(2)}, u32[]{:S(2)}) collective-permute-start(f32[384,128]{1,0:T(8,128)S(1)} %get-tuple-element.40), channel_id=1, source_target_pairs={{0,8},{4,12},{8,16},{12,20},{16,24},{20,28},{1,9},{5,13},{9,17},{1... | collective-permute-start | bytes 589832 | tf_op jit(solution)/shard_map/ppermute | solution.py:33
  61.5 8.3 %collective-permute-start.9 = (f32[384,128]{1,0:T(8,128)S(1)}, f32[384,128]{1,0:T(8,128)S(1)}, u32[]{:S(2)}, u32[]{:S(2)}) collective-permute-start(f32[384,128]{1,0:T(8,128)S(1)} %get-tuple-element.41), channel_id=1, source_target_pairs={{0,4},{4,8},{8,12},{12,16},{16,20},{20,24},{24,28},{1,5},{5,9},{9,... | collective-permute-start | bytes 589832 | tf_op jit(solution)/shard_map/ppermute | solution.py:33
  80.6 10.2 %collective-permute-start.12 = (f32[384,128]{1,0:T(8,128)S(1)}, f32[384,128]{1,0:T(8,128)S(1)}, u32[]{:S(2)}, u32[]{:S(2)}) collective-permute-start(f32[384,128]{1,0:T(8,128)S(1)} %get-tuple-element.45), channel_id=1, source_target_pairs={{8,0},{12,4},{16,8},{20,12},{24,16},{28,20},{9,1},{13,5},{17,9},{2... | collective-permute-start | bytes 589832 | tf_op jit(solution)/shard_map/ppermute | solution.py:33
  82.5 8.3 %collective-permute-start.13 = (f32[384,128]{1,0:T(8,128)S(1)}, f32[384,128]{1,0:T(8,128)S(1)}, u32[]{:S(2)}, u32[]{:S(2)}) collective-permute-start(f32[384,128]{1,0:T(8,128)S(1)} %get-tuple-element.46), channel_id=1, source_target_pairs={{4,0},{8,4},{12,8},{16,12},{20,16},{24,20},{28,24},{5,1},{9,5},{13... | collective-permute-start | bytes 589832 | tf_op jit(solution)/shard_map/ppermute | solution.py:33
  84.5 7.9 %collective-permute-start.14 = (f32[384,128]{1,0:T(8,128)S(1)}, f32[384,128]{1,0:T(8,128)S(1)}, u32[]{:S(2)}, u32[]{:S(2)}) collective-permute-start(f32[384,128]{1,0:T(8,128)S(1)} %get-tuple-element.47), channel_id=1, source_target_pairs={{0,4},{4,8},{8,12},{12,16},{16,20},{20,24},{24,28},{1,5},{5,9},{9,... | collective-permute-start | bytes 589832 | tf_op jit(solution)/shard_map/ppermute | solution.py:33
  86.9 9.9 %collective-permute-start.15 = (f32[384,128]{1,0:T(8,128)S(1)}, f32[384,128]{1,0:T(8,128)S(1)}, u32[]{:S(2)}, u32[]{:S(2)}) collective-permute-start(f32[384,128]{1,0:T(8,128)S(1)} %get-tuple-element.48), channel_id=1, source_target_pairs={{0,8},{4,12},{8,16},{12,20},{16,24},{20,28},{1,9},{5,13},{9,17},{1... | collective-permute-start | bytes 589832 | tf_op jit(solution)/shard_map/ppermute | solution.py:33
  100.1 5.0 %copy-start.3 = (s32[1296]{0:T(1024)S(1)}, s32[1296]{0:T(1024)}, u32[]{:S(2)}) copy-start(s32[1296]{0:T(1024)} %param.16) | copy-start | bytes 15556
  100.1 5.0 %copy-start.4 = (s32[1296]{0:T(1024)S(1)}, s32[1296]{0:T(1024)}, u32[]{:S(2)}) copy-start(s32[1296]{0:T(1024)} %param.15) | copy-start | bytes 15556
  100.1 37.4 %copy-start.1 = (f32[1296]{0:T(1024)S(1)}, f32[1296]{0:T(1024)}, u32[]{:S(2)}) copy-start(f32[1296]{0:T(1024)} %rate.1) | copy-start | bytes 15556
  100.1 37.4 %all-to-all-start = ((f32[4,648,128]{2,1,0:T(8,128)}), f32[4,648,128]{2,1,0:T(8,128)S(1)}, u32[]{:S(2)}, u32[]{:S(2)}) async-start(f32[4,648,128]{2,1,0:T(8,128)} %bitcast.2), calls=%async_computation | async-start | bytes 2654208 | tf_op jit(solution)/shard_map/all_to_all | solution.py:363

commit v2 on v1

v2 whole, which is shorter than its diff:
```python
import functools
import math

import jax
import jax.numpy as jnp
from jax import lax
from jax.experimental import pallas as pl
from jax.experimental.pallas import tpu as pltpu
from jax.sharding import PartitionSpec as P

NDIR = 36
REACH = 2
STEPS = 2
BLOCKS = 2 * REACH
LANES = 128
GROUPS = 2

weight_plus = 1.25 ** (-4)
weight_minus = 0.75 ** (-4)
weight_both = 0.9375 ** (-4)

VM = pl.BlockSpec(memory_space=pltpu.VMEM)
SM = pl.BlockSpec(memory_space=pltpu.SMEM)


def offset_of(position):
    return position - REACH if position < REACH else position - REACH + 1


def passed_along(value, axis, steps):
    count = lax.axis_size(axis)
    return lax.ppermute(value, axis, [(source, (source + steps) % count) for source in range(count)])


def chunked(total, limit):
    return max(size for size in range(1, limit + 1) if total % size == 0)


def rows_to_block(sub, lanes, stage, block):
    for column in range(block.shape[1] // LANES):
        for part in range(sub):
            tile = stage[pl.ds(column * LANES * sub + part, LANES, stride=sub), :].T
            block[part * lanes : (part + 1) * lanes, column * LANES : (column + 1) * LANES] = tile[:lanes]


def block_to_rows(sub, lanes, block, square, rows, first):
    for column in range(block.shape[1] // LANES):
        for part in range(sub):
            slot = square.at[(column * sub + part) % square.shape[0]]
            slot[:lanes, :] = block[part * lanes : (part + 1) * lanes, column * LANES : (column + 1) * LANES]
            rows[pl.ds(first + column * LANES * sub + part, LANES, stride=sub), :] = slot[...].T


def pack_rows(sub, lanes, send, energy, stages, outs):
    slots = outs[0].shape[1]
    unroll = chunked(slots, 32)
    for position in range(BLOCKS):
        stage = stages.at[position]

        @pl.loop(0, slots // unroll)
        def _(k):
            first = k * unroll
            listed = send.at[pl.ds((BLOCKS - 1 - position) * slots + first, unroll)]
            for u in range(unroll):
                stage[pl.ds((first + u) * sub, sub), :] = energy[pl.ds(listed[u], sub), :]

        rows_to_block(sub, lanes, stage, outs[position])


def enter_kernel(sub, lanes, send, spectrum, full, *rest):
    outs, square, stages = rest[:BLOCKS], rest[BLOCKS], rest[BLOCKS + 1]
    square[...] = jnp.zeros_like(square)
    block_to_rows(sub, lanes, spectrum, square, full, 0)
    pack_rows(sub, lanes, send, full, stages, outs)


def clear(items):
    rows = items[0].shape[0]
    step = chunked(rows, 64)
    zero = jnp.zeros((step, LANES), jnp.float32)

    @pl.loop(0, rows // step)
    def _(k):
        for item in items:
            item[pl.ds(pl.multiple_of(k * step, step), step), :] = zero


def slope_kernel(sub, shared, normals, step_weight, wave, coef, weight, lines):
    elements = normals.shape[2]
    parts = 1 if shared else sub
    pitch = coef.shape[0] // elements
    lines[...] = jnp.zeros_like(lines)
    for component in range(2):
        for corner in range(2):
            row = component * 2 + corner
            lines[row : row + 1, :] = normals[component, corner : corner + 1, :]

    def spread(column):
        return jnp.broadcast_to(column, (8, LANES))

    @pl.loop(0, elements // LANES)
    def _(k):
        turned = lines[:, pl.ds(pl.multiple_of(k * LANES, LANES), LANES)].T
        for group in range(LANES // 8):
            at = slice(group * 8, group * 8 + 8)
            x0, x1, y0, y1 = (spread(turned[at, j : j + 1]) for j in range(4))
            base = (k * LANES + group * 8) * pitch
            for part in range(parts):
                east, north = wave[part : part + 1, :], wave[sub + part : sub + part + 1, :]
                first = x0 * east + y0 * north
                second = x1 * east + y1 * north
                inward = jnp.minimum(first, 0.0) + jnp.minimum(second, 0.0) - jnp.maximum(first + second, 0.0)
                for which, value in enumerate((first, second, 1.0 / inward)):
                    coef[pl.ds(base + which * parts + part, 8, stride=pitch), :] = value

    nodes = step_weight.shape[1]
    for block in range(nodes // LANES):
        turned = jnp.broadcast_to(step_weight[0:1, block * LANES : (block + 1) * LANES], (8, LANES)).T
        for group in range(LANES // 8):
            value = spread(turned[group * 8 : group * 8 + 8, 0:1])
            for part in range(sub):
                at = pl.ds((block * LANES + group * 8) * sub + part, 8, stride=sub)
                weight[at, :] = value * wave[2 * sub + part : 2 * sub + part + 1, :]


def total(sums, at):
    result = sums[0][at, :]
    for item in sums[1:]:
        result = result + item[at, :]
    return result


def sweep_kernel(sub, lanes, shared, own_rows, conn, coef, weight, *rest):
    ghosts, full, rest = rest[:BLOCKS], rest[BLOCKS + 1], rest[BLOCKS + 2 :]
    returned, square, stages, sums = rest[:BLOCKS], rest[BLOCKS], rest[BLOCKS + 1], rest[BLOCKS + 2 :]
    clear(sums)
    ghost_rows = (full.shape[0] - own_rows) // BLOCKS
    elements = conn.shape[0] // 3
    parts = 1 if shared else sub
    pitch = coef.shape[0] // elements
    square[...] = jnp.zeros_like(square)
    for position in range(BLOCKS):
        block_to_rows(sub, lanes, ghosts[position], square, full, own_rows + position * ghost_rows)

    share = elements // GROUPS
    unroll = chunked(share, 16)

    @pl.loop(0, share // unroll)
    def _(k):
        listed = [
            [conn.at[pl.ds(corner * elements + group * share + k * unroll, unroll)] for corner in range(3)]
            for group in range(GROUPS)
        ]
        for u in range(unroll):
            for group in range(GROUPS):
                element = group * share + k * unroll + u
                index = [item[u] for item in listed[group]]
                value = [full[pl.ds(row, sub), :] for row in index]
                tile = coef[pl.ds(element * pitch, pitch), :]
                first, second, inverse = (
                    jnp.broadcast_to(tile[j * parts : (j + 1) * parts], (sub, LANES)) for j in range(3)
                )
                both = first + second
                inflow = jnp.minimum(first, 0.0) * value[0] + jnp.minimum(second, 0.0) * value[1]
                inflow = (inflow - jnp.maximum(both, 0.0) * value[2]) * inverse
                residual = (
                    jnp.maximum(first, 0.0) * (value[0] - inflow),
                    jnp.maximum(second, 0.0) * (value[1] - inflow),
                    jnp.minimum(both, 0.0) * (inflow - value[2]),
                )
                for corner in range(3):
                    item = sums[group * 3 + corner]
                    at = pl.ds(index[corner], sub)
                    item[at, :] = item[at, :] + residual[corner]

    step = chunked(ghost_rows, 64)
    for position in range(BLOCKS):
        stage = stages.at[position]

        @pl.loop(0, ghost_rows // step)
        def _(k):
            at = pl.multiple_of(k * step, step)
            stage[pl.ds(at, step), :] = total(sums, pl.ds(own_rows + position * ghost_rows + at, step))

        rows_to_block(sub, lanes, stage, returned[position])

    own_step = chunked(own_rows, 64)

    @pl.loop(0, own_rows // own_step)
    def _(k):
        at = pl.ds(pl.multiple_of(k * own_step, own_step), own_step)
        full[at, :] = full[at, :] - weight[at, :] * total(sums, at)


def add_returned(sub, lanes, send, weight, incoming, square, stages, full):
    slots = incoming[0].shape[1]
    square[...] = jnp.zeros_like(square)
    unroll = chunked(slots, 16)
    for position in range(BLOCKS):
        block_to_rows(sub, lanes, incoming[position], square, stages.at[position], 0)
    for position in range(BLOCKS):
        stage = stages.at[position]

        @pl.loop(0, slots // unroll)
        def _(k):
            first = k * unroll
            listed = send.at[pl.ds((BLOCKS - 1 - position) * slots + first, unroll)]
            rows = [listed[u] for u in range(unroll)]
            fresh = [
                full[pl.ds(row, sub), :] - weight[pl.ds(row, sub), :] * stage[pl.ds((first + u) * sub, sub), :]
                for u, row in enumerate(rows)
            ]
            for row, item in zip(rows, fresh):
                full[pl.ds(row, sub), :] = item


def between_kernel(sub, lanes, send, weight, *rest):
    incoming, rest = rest[:BLOCKS], rest[BLOCKS + 1 :]
    full, outs, square, stages = rest[0], rest[1 : 1 + BLOCKS], rest[1 + BLOCKS], rest[2 + BLOCKS]
    add_returned(sub, lanes, send, weight, incoming, square, stages, full)
    pack_rows(sub, lanes, send, full, stages, outs)


def leave_kernel(sub, lanes, halves, owned, send, weight, *rest):
    incoming, rest = rest[:BLOCKS], rest[BLOCKS + 1 :]
    full, out, square, stages = rest
    add_returned(sub, lanes, send, weight, incoming, square, stages, full)
    per_target = sub * lanes * halves
    for block in range(owned // LANES):
        target, half = divmod(block, halves)
        for part in range(sub):
            tile = full[pl.ds(block * LANES * sub + part, LANES, stride=sub), :].T
            first = target * per_target + part * lanes * halves + half
            out[pl.ds(first, lanes, stride=halves), :] = tile[:lanes]


def interact_kernel(halves, plus, minus, rate, energy, *rest):
    out, kept, added = rest[0], rest[1], rest[2:]
    clear(added)
    bins = plus.shape[0]
    share = bins // GROUPS
    unroll = chunked(share, 12)

    @pl.loop(0, share // unroll)
    def _(k):
        for u in range(unroll):
            for group in range(GROUPS):
                index = group * share + k * unroll + u
                up, down = plus[index], minus[index]
                here = pl.ds(index * halves, halves)
                own = energy[here, :]
                upper = energy[pl.ds(up, halves), :]
                lower = energy[pl.ds(down, halves), :]
                term = rate[index] * (
                    own * own * (weight_plus * upper + weight_minus * lower)
                    - 2.0 * weight_both * own * upper * lower
                )
                kept[here, :] = own - 2.0 * term
                for item, row in zip(added[2 * group :], (up, down)):
                    item[pl.ds(row, halves), :] = item[pl.ds(row, halves), :] + term

    step = chunked(bins, 48)

    @pl.loop(0, bins // step)
    def _(k):
        for half in range(halves):
            at = pl.ds(k * step * halves + half, step, stride=halves)
            result = kept[at, :] + total(added, at)
            out[pl.ds(pl.multiple_of(k * step, step), step), half * LANES : (half + 1) * LANES] = result


def shape_of(*dims):
    return jax.ShapeDtypeStruct(dims, jnp.float32)


def cost(flops, moved):
    return pl.CostEstimate(flops=flops, bytes_accessed=moved, transcendentals=0)


def limit(mebibytes):
    return pltpu.CompilerParams(vmem_limit_bytes=mebibytes << 20)


def on_device(
    spectrum, normals, conn, send_nodes, step_weight, group_speed, dia_plus, dia_minus, dia_coeff
):
    row_count, owned = spectrum.shape
    slots = send_nodes.shape[2]
    elements = conn.shape[1]
    bins = dia_plus.shape[0]
    spec_count = lax.axis_size("spec")
    sub = -(-row_count // LANES)
    while row_count % sub:
        sub += 1
    lanes = row_count // sub
    shared = lanes % NDIR == 0
    own_rows = owned * sub
    ghost_rows = slots * sub
    rows = own_rows + BLOCKS * ghost_rows
    halves = owned // (spec_count * LANES)

    send = (send_nodes[0] * sub).reshape(-1)
    nodes = (conn * sub).reshape(-1)

    bin_of = (
        lax.axis_index("spec") * row_count
        + jnp.arange(sub, dtype=jnp.int32)[:, None] * lanes
        + jnp.arange(LANES, dtype=jnp.int32)[None, :]
    )
    angle = (bin_of % NDIR).astype(jnp.float32) * (2.0 * math.pi / NDIR)
    east, north = jnp.cos(angle), jnp.sin(angle)
    select = ((bin_of // NDIR)[:, :, None] == jnp.arange(group_speed.shape[0], dtype=jnp.int32)).astype(jnp.float32)
    speed = jnp.sum(select * group_speed, axis=2)
    wave = jnp.concatenate([east, north, speed])

    block_shapes = [shape_of(row_count, slots)] * BLOCKS
    full_shape = shape_of(rows, LANES)
    sums = [pltpu.VMEM((rows, LANES), jnp.float32)] * (3 * GROUPS)
    squares = pltpu.VMEM((4, LANES, LANES), jnp.float32)
    stages = pltpu.VMEM((BLOCKS, ghost_rows, LANES), jnp.float32)
    moved = 4 * LANES * own_rows

    full, *outs = pl.pallas_call(
        functools.partial(enter_kernel, sub, lanes),
        out_shape=[full_shape] + block_shapes,
        in_specs=[SM, VM],
        out_specs=[VM] * (1 + BLOCKS),
        scratch_shapes=[squares, stages],
        cost_estimate=cost(0, 2 * moved),
        compiler_params=limit(4),
        name="enter",
    )(send, spectrum)
    pitch = 3 if shared else 3 * sub
    coef, weight = pl.pallas_call(
        functools.partial(slope_kernel, sub, shared),
        out_shape=[shape_of(elements * pitch, LANES), shape_of(own_rows, LANES)],
        in_specs=[VM] * 3,
        out_specs=[VM] * 2,
        scratch_shapes=[pltpu.VMEM((LANES, elements), jnp.float32)],
        cost_estimate=cost(20 * elements * LANES, 4 * LANES * (elements * pitch + own_rows)),
        compiler_params=limit(4),
        name="slopes",
    )(normals, step_weight.reshape(1, owned), wave)

    for sweep_index in range(STEPS):
        again = sweep_index < STEPS - 1
        ghosts = [passed_along(outs[p], "dom", -offset_of(p)) for p in range(BLOCKS)]
        full, *returned = pl.pallas_call(
            functools.partial(sweep_kernel, sub, lanes, shared, own_rows),
            out_shape=[full_shape] + block_shapes,
            in_specs=[SM] + [VM] * (3 + BLOCKS),
            out_specs=[VM] * (1 + BLOCKS),
            input_output_aliases={3 + BLOCKS: 0},
            scratch_shapes=[squares, stages] + sums,
            cost_estimate=cost(elements * 24 * row_count, 4 * LANES * (3 * elements + 4 * rows)),
            compiler_params=limit(20),
            name="sweep",
        )(nodes, coef, weight, *ghosts, full)
        incoming = [passed_along(returned[p], "dom", offset_of(p)) for p in range(BLOCKS)]
        if again:
            full, *outs = pl.pallas_call(
                functools.partial(between_kernel, sub, lanes),
                out_shape=[full_shape] + block_shapes,
                in_specs=[SM] + [VM] * (2 + BLOCKS),
                out_specs=[VM] * (1 + BLOCKS),
                input_output_aliases={2 + BLOCKS: 0},
                scratch_shapes=[squares, stages],
                cost_estimate=cost(2 * owned * row_count, 4 * moved),
                compiler_params=limit(4),
                name="between",
            )(send, weight, *incoming, full)

    full, leaving = pl.pallas_call(
        functools.partial(leave_kernel, sub, lanes, halves, owned),
        out_shape=[full_shape, shape_of(spec_count * row_count * halves, LANES)],
        in_specs=[SM] + [VM] * (2 + BLOCKS),
        out_specs=[VM] * 2,
        input_output_aliases={2 + BLOCKS: 0},
        scratch_shapes=[squares, stages],
        cost_estimate=cost(2 * owned * row_count, 4 * moved),
        compiler_params=limit(4),
        name="leave",
    )(send, weight, *incoming, full)
    arrived = lax.all_to_all(
        leaving.reshape(spec_count, row_count * halves, LANES), "spec", split_axis=0, concat_axis=0
    )
    return pl.pallas_call(
        functools.partial(interact_kernel, halves),
        out_shape=shape_of(bins, halves * LANES),
        in_specs=[SM] * 3 + [VM],
        out_specs=VM,
        scratch_shapes=[pltpu.VMEM((bins * halves, LANES), jnp.float32)] * (1 + 2 * GROUPS),
        cost_estimate=cost(16 * bins * halves * LANES, 8 * bins * halves * LANES),
        compiler_params=limit(10),
        name="interact",
    )(dia_plus * halves, dia_minus * halves, dia_coeff, arrived.reshape(bins * halves, LANES))


def solution(mesh):
    in_specs = (
        P("spec", "dom"),
        P(None, None, "dom"),
        P(None, "dom"),
        P("dom", None, None),
        P("dom"),
        P(),
        P(),
        P(),
        P(),
    )
    out_specs = P(None, ("dom", "spec"))
    return jax.shard_map(
        on_device, mesh=mesh, in_specs=in_specs, out_specs=out_specs, check_vma=False
    )
```

time: 145 us -> 134 us (0.924)
  the two profiles are of different devices: /device:TPU:4 before, /device:TPU:0 now
where the time goes in v2:
time: 134 us; the launch traced here: 133 us
  waiting for transfers between devices  64.8 us (48%)
  Pallas kernels  43 us (32%)
  starting transfers between devices  18.9 us (14%)
  local copies, waits for them, and re-layouts  3.93 us (3%)
  other arithmetic  2.42 us (2%)
    ppermute x16, waiting for transfers between devices, passed_along(): lax.ppermute(value, axis, [(source, (source + steps) % count) for source...  33.7 us
    all_to_all x1, waiting for transfers between devices, on_device(): lax.all_to_all(leaving.reshape(spec_count, row_count * halves, LANES), 's...  31 us
    pallas_call x2, Pallas kernels, on_device(): pl.pallas_call(functools.partial(sweep_kernel, sub, lanes, shared, own_ro...  23.2 us
    ppermute x16, starting transfers between devices, passed_along(): lax.ppermute(value, axis, [(source, (source + steps) % count) for source...  13.8 us
    pallas_call x1, Pallas kernels, on_device(): pl.pallas_call(functools.partial(interact_kernel, halves), out_shape=shap...  7.02 us
    all_to_all x1, starting transfers between devices, on_device(): lax.all_to_all(leaving.reshape(spec_count, row_count * halves, LANES), 's...  5.14 us
    pallas_call x1, Pallas kernels, on_device(): pl.pallas_call(functools.partial(slope_kernel, sub, shared), out_shape=[s...  4.88 us
    unnamed x13, local copies, waits for them, and re-layouts  3.91 us
  transfers between devices with their start and end apart: 17, of which 12 were waited for; matrix products, arithmetic and copies ran while one was open for 2% of the time, Pallas kernels for 4%

profile of v2, /device:TPU:0, one launch (start us, length us, event | category | flops | bytes accessed | tf_op | source)
XLA Modules:
  0.0 133.2 jit_solution(2512012193802004728)
XLA Ops:
  0.7 1.3 copy-done
  2.0 2.6 %enter.1 = (f32[4608,128]{1,0:T(8,128)S(1)}, f32[324,128]{1,0:T(8,128)}, f32[324,128]{1,0:T(8,128)}, f32[324,128]{1,0:T(8,128)S(1)}, f32[324,128]{1,0:T(8,128)S(1)}) custom-call(s32[512]{0:T(512)S(1)} %multiply_bitcast_fusion.send, f32[324,1024]{1,0:T(8,128)S(1)} %copy-done), custom_call_target="tpu_custom_call" | custom-call | bytes 3145728 | tf_op jit(solution)/shard_map/enter/pallas_call | solution.py:323
  4.6 3.0 %collective-permute-start = (f32[324,128]{1,0:T(8,128)}, f32[324,128]{1,0:T(8,128)S(1)}, u32[]{:S(2)}, u32[]{:S(2)}) collective-permute-start(f32[324,128]{1,0:T(8,128)} %get-tuple-element.30), channel_id=1, source_target_pairs={{0,8},{4,12},{8,16},{12,20},{16,24},{20,28},{24,0},{28,4},{1,9},{5... | collective-permute-start | bytes 497672 | tf_op jit(solution)/shard_map/ppermute | solution.py:32
  7.6 2.6 %collective-permute-start.2 = (f32[324,128]{1,0:T(8,128)S(1)}, f32[324,128]{1,0:T(8,128)S(1)}, u32[]{:S(2)}, u32[]{:S(2)}) collective-permute-start(f32[324,128]{1,0:T(8,128)S(1)} %get-tuple-element.32), channel_id=1, source_target_pairs={{0,28},{4,0},{8,4},{12,8},{16,12},{20,16},{24,20},{28,24},{1,29},{... | collective-permute-start | bytes 497672 | tf_op jit(solution)/shard_map/ppermute | solution.py:32
  13.6 4.9 %slopes.1 = (f32[6144,128]{1,0:T(8,128)S(1)}, f32[3072,128]{1,0:T(8,128)S(1)}) custom-call(f32[2,3,2048]{2,1,0:T(4,128)S(1)} %copy.15.normals, f32[1,1024]{1,0:T(1,128)S(1)} %bitcast.7, f32[9,128]{1,0:T(8,128)S(1)} %pad_maximum_fusion.wave), custom_call_target="tpu_custom_call" | custom-call | flops 5242880 | bytes 4718592 | tf_op jit(solution)/shard_map/slopes/pallas_call | solution.py:334
  18.5 2.0 %collective-permute-done.3.rest_3_ = f32[324,128]{1,0:T(8,128)S(1)} collective-permute-done((f32[324,128]{1,0:T(8,128)S(1)}, f32[324,128]{1,0:T(8,128)S(1)}, u32[]{:S(2)}, u32[]{:S(2)}) %collective-permute-start.3) | collective-permute-done | bytes 165920 | tf_op jit(solution)/shard_map/ppermute | solution.py:32
  20.5 11.6 %sweep.2 = (f32[4608,128]{1,0:T(8,128)S(1)}, f32[324,128]{1,0:T(8,128)S(1)}, f32[324,128]{1,0:T(8,128)S(1)}, f32[324,128]{1,0:T(8,128)S(1)}, f32[324,128]{1,0:T(8,128)S(1)}) custom-call(s32[6144]{0:T(1024)S(1)} %reshape.53.conn, f32[6144,128]{1,0:T(8,128)S(1)} %get-tuple-element.29.coef, ...), custom_call_target="tpu_custom_call", output_to_operand_aliasing={{0}: (7, {})} | custom-call | flops 15925248 | bytes 12582912 | tf_op jit(solution)/shard_map/sweep/pallas_call | solution.py:348
  32.1 1.5 %collective-permute-start.4 = (f32[324,128]{1,0:T(8,128)S(1)}, f32[324,128]{1,0:T(8,128)S(1)}, u32[]{:S(2)}, u32[]{:S(2)}) collective-permute-start(f32[324,128]{1,0:T(8,128)S(1)} %get-tuple-element.35), channel_id=1, source_target_pairs={{0,24},{4,28},{8,0},{12,4},{16,8},{20,12},{24,16},{28,20},{1,25},{... | collective-permute-start | bytes 497672 | tf_op jit(solution)/shard_map/ppermute | solution.py:32
  34.7 3.6 %collective-permute-done.4.rest_0_ = f32[324,128]{1,0:T(8,128)S(1)} collective-permute-done((f32[324,128]{1,0:T(8,128)S(1)}, f32[324,128]{1,0:T(8,128)S(1)}, u32[]{:S(2)}, u32[]{:S(2)}) %collective-permute-start.4) | collective-permute-done | bytes 165920 | tf_op jit(solution)/shard_map/ppermute | solution.py:32
  38.3 3.6 %collective-permute-done.5.rest_1_ = f32[324,128]{1,0:T(8,128)S(1)} collective-permute-done((f32[324,128]{1,0:T(8,128)S(1)}, f32[324,128]{1,0:T(8,128)S(1)}, u32[]{:S(2)}, u32[]{:S(2)}) %collective-permute-start.5) | collective-permute-done | bytes 165920 | tf_op jit(solution)/shard_map/ppermute | solution.py:32
  41.9 2.6 %collective-permute-done.7.rest_3_ = f32[324,128]{1,0:T(8,128)S(1)} collective-permute-done((f32[324,128]{1,0:T(8,128)S(1)}, f32[324,128]{1,0:T(8,128)S(1)}, u32[]{:S(2)}, u32[]{:S(2)}) %collective-permute-start.7) | collective-permute-done | bytes 165920 | tf_op jit(solution)/shard_map/ppermute | solution.py:32
  44.5 2.9 %between.1 = (f32[4608,128]{1,0:T(8,128)S(1)}, f32[324,128]{1,0:T(8,128)S(1)}, f32[324,128]{1,0:T(8,128)S(1)}, f32[324,128]{1,0:T(8,128)S(1)}, f32[324,128]{1,0:T(8,128)S(1)}) custom-call(s32[512]{0:T(512)S(1)} %multiply_bitcast_fusion.send, f32[3072,128]{1,0:T(8,128)S(1)} %get-tuple-element.28.weight, ...), custom_call_target="tpu_custom_call", output_to_operand_aliasing={{0}: (6, {})} | custom-call | flops 663552 | bytes 6291456 | tf_op jit(solution)/shard_map/between/pallas_call | solution.py:361
  47.6 2.7 %collective-permute-start.11 = (f32[324,128]{1,0:T(8,128)S(1)}, f32[324,128]{1,0:T(8,128)S(1)}, u32[]{:S(2)}, u32[]{:S(2)}) collective-permute-start(f32[324,128]{1,0:T(8,128)S(1)} %get-tuple-element.43), channel_id=1, source_target_pairs={{0,24},{4,28},{8,0},{12,4},{16,8},{20,12},{24,16},{28,20},{1,25},{... | collective-permute-start | bytes 497672 | tf_op jit(solution)/shard_map/ppermute | solution.py:32
  50.5 7.4 %collective-permute-done.11.rest_3_ = f32[324,128]{1,0:T(8,128)S(1)} collective-permute-done((f32[324,128]{1,0:T(8,128)S(1)}, f32[324,128]{1,0:T(8,128)S(1)}, u32[]{:S(2)}, u32[]{:S(2)}) %collective-permute-start.11) | collective-permute-done | bytes 165920 | tf_op jit(solution)/shard_map/ppermute | solution.py:32
  57.9 4.5 %collective-permute-done.8.rest_0_ = f32[324,128]{1,0:T(8,128)S(1)} collective-permute-done((f32[324,128]{1,0:T(8,128)S(1)}, f32[324,128]{1,0:T(8,128)S(1)}, u32[]{:S(2)}, u32[]{:S(2)}) %collective-permute-start.8) | collective-permute-done | bytes 165920 | tf_op jit(solution)/shard_map/ppermute | solution.py:32
  62.5 11.6 %sweep.3 = (f32[4608,128]{1,0:T(8,128)S(1)}, f32[324,128]{1,0:T(8,128)S(1)}, f32[324,128]{1,0:T(8,128)S(1)}, f32[324,128]{1,0:T(8,128)S(1)}, f32[324,128]{1,0:T(8,128)S(1)}) custom-call(s32[6144]{0:T(1024)S(1)} %reshape.53.conn, f32[6144,128]{1,0:T(8,128)S(1)} %get-tuple-element.29.coef, ...), custom_call_target="tpu_custom_call", output_to_operand_aliasing={{0}: (7, {})} | custom-call | flops 15925248 | bytes 12582912 | tf_op jit(solution)/shard_map/sweep/pallas_call | solution.py:348
  75.1 1.6 %collective-permute-start.15 = (f32[324,128]{1,0:T(8,128)S(1)}, f32[324,128]{1,0:T(8,128)S(1)}, u32[]{:S(2)}, u32[]{:S(2)}) collective-permute-start(f32[324,128]{1,0:T(8,128)S(1)} %get-tuple-element.48), channel_id=1, source_target_pairs={{0,8},{4,12},{8,16},{12,20},{16,24},{20,28},{24,0},{28,4},{1,9},{5... | collective-permute-start | bytes 497672 | tf_op jit(solution)/shard_map/ppermute | solution.py:32
  76.7 4.6 %collective-permute-done.12.rest_0_ = f32[324,128]{1,0:T(8,128)S(1)} collective-permute-done((f32[324,128]{1,0:T(8,128)S(1)}, f32[324,128]{1,0:T(8,128)S(1)}, u32[]{:S(2)}, u32[]{:S(2)}) %collective-permute-start.12) | collective-permute-done | bytes 165920 | tf_op jit(solution)/shard_map/ppermute | solution.py:32
  82.1 4.4 %collective-permute-done.15.rest_3_ = f32[324,128]{1,0:T(8,128)S(1)} collective-permute-done((f32[324,128]{1,0:T(8,128)S(1)}, f32[324,128]{1,0:T(8,128)S(1)}, u32[]{:S(2)}, u32[]{:S(2)}) %collective-permute-start.15) | collective-permute-done | bytes 165920 | tf_op jit(solution)/shard_map/ppermute | solution.py:32
  86.5 2.4 %leave.1 = (f32[4608,128]{1,0:T(8,128)S(1)}, f32[2592,128]{1,0:T(8,128)S(1)}) custom-call(s32[512]{0:T(512)S(1)} %multiply_bitcast_fusion.send, f32[3072,128]{1,0:T(8,128)S(1)} %get-tuple-element.28.weight, f32[324,128]{1,0:T(8,128)S(1)} %collective-permute-done.12.rest_0_, ...), custom_call_target="tpu_custom_call", output_to_operand_aliasing={{0}: (6, {})} | custom-call | flops 663552 | bytes 6291456 | tf_op jit(solution)/shard_map/leave/pallas_call | solution.py:373
  88.9 1.1 copy-done.1
  89.9 5.1 %all-to-all-start = ((f32[4,648,128]{2,1,0:T(8,128)}), f32[4,648,128]{2,1,0:T(8,128)S(1)}, u32[]{:S(2)}, u32[]{:S(2)}) async-start(f32[4,648,128]{2,1,0:T(8,128)} %bitcast.6), calls=%async_computation | async-start | bytes 2654208 | tf_op jit(solution)/shard_map/all_to_all | solution.py:384
  95.1 31.0 %all-to-all-done = f32[4,648,128]{2,1,0:T(8,128)S(1)} async-done(((f32[4,648,128]{2,1,0:T(8,128)}), f32[4,648,128]{2,1,0:T(8,128)S(1)}, u32[]{:S(2)}, u32[]{:S(2)}) %all-to-all-start) | async-done | bytes 1327136 | tf_op jit(solution)/shard_map/all_to_all | solution.py:384
  126.1 7.0 %interact.1 = f32[1296,256]{1,0:T(8,128)} custom-call(s32[1296]{0:T(1024)S(1)} %get-tuple-element.54.plus, s32[1296]{0:T(1024)S(1)} %get-tuple-element.53.minus, f32[1296]{0:T(1024)S(1)} %copy-done.2, f32[2592,128]{1,0:T(8,128)S(1)} %bitcast.5), custom_call_target="tpu_custom_call" | custom-call | flops 5308416 | bytes 2654208 | tf_op jit(solution)/shard_map/interact/pallas_call | solution.py:387
  (39 shorter events, 7.4 us)
Async XLA Ops:
  0.7 1.3 copy-start
  4.6 13.9 %collective-permute-start = (f32[324,128]{1,0:T(8,128)}, f32[324,128]{1,0:T(8,128)S(1)}, u32[]{:S(2)}, u32[]{:S(2)}) collective-permute-start(f32[324,128]{1,0:T(8,128)} %get-tuple-element.30), channel_id=1, source_target_pairs={{0,8},{4,12},{8,16},{12,20},{16,24},{20,28},{24,0},{28,4},{1,9},{5... | collective-permute-start | bytes 497672 | tf_op jit(solution)/shard_map/ppermute | solution.py:32
  7.6 10.9 %collective-permute-start.1 = (f32[324,128]{1,0:T(8,128)}, f32[324,128]{1,0:T(8,128)S(1)}, u32[]{:S(2)}, u32[]{:S(2)}) collective-permute-start(f32[324,128]{1,0:T(8,128)} %get-tuple-element.31), channel_id=1, source_target_pairs={{0,4},{4,8},{8,12},{12,16},{16,20},{20,24},{24,28},{28,0},{1,5},{5... | collective-permute-start | bytes 497672 | tf_op jit(solution)/shard_map/ppermute | solution.py:32
  7.6 10.9 %collective-permute-start.2 = (f32[324,128]{1,0:T(8,128)S(1)}, f32[324,128]{1,0:T(8,128)S(1)}, u32[]{:S(2)}, u32[]{:S(2)}) collective-permute-start(f32[324,128]{1,0:T(8,128)S(1)} %get-tuple-element.32), channel_id=1, source_target_pairs={{0,28},{4,0},{8,4},{12,8},{16,12},{20,16},{24,20},{28,24},{1,29},{... | collective-permute-start | bytes 497672 | tf_op jit(solution)/shard_map/ppermute | solution.py:32
  10.3 10.3 %collective-permute-start.3 = (f32[324,128]{1,0:T(8,128)S(1)}, f32[324,128]{1,0:T(8,128)S(1)}, u32[]{:S(2)}, u32[]{:S(2)}) collective-permute-start(f32[324,128]{1,0:T(8,128)S(1)} %get-tuple-element.33), channel_id=1, source_target_pairs={{0,24},{4,28},{8,0},{12,4},{16,8},{20,12},{24,16},{28,20},{1,25},{... | collective-permute-start | bytes 497672 | tf_op jit(solution)/shard_map/ppermute | solution.py:32
  12.9 0.7 copy-start.3
  32.1 6.1 %collective-permute-start.4 = (f32[324,128]{1,0:T(8,128)S(1)}, f32[324,128]{1,0:T(8,128)S(1)}, u32[]{:S(2)}, u32[]{:S(2)}) collective-permute-start(f32[324,128]{1,0:T(8,128)S(1)} %get-tuple-element.35), channel_id=1, source_target_pairs={{0,24},{4,28},{8,0},{12,4},{16,8},{20,12},{24,16},{28,20},{1,25},{... | collective-permute-start | bytes 497672 | tf_op jit(solution)/shard_map/ppermute | solution.py:32
  33.6 8.3 %collective-permute-start.5 = (f32[324,128]{1,0:T(8,128)S(1)}, f32[324,128]{1,0:T(8,128)S(1)}, u32[]{:S(2)}, u32[]{:S(2)}) collective-permute-start(f32[324,128]{1,0:T(8,128)S(1)} %get-tuple-element.36), channel_id=1, source_target_pairs={{0,28},{4,0},{8,4},{12,8},{16,12},{20,16},{24,20},{28,24},{1,29},{... | collective-permute-start | bytes 497672 | tf_op jit(solution)/shard_map/ppermute | solution.py:32
  33.6 8.3 %collective-permute-start.6 = (f32[324,128]{1,0:T(8,128)S(1)}, f32[324,128]{1,0:T(8,128)S(1)}, u32[]{:S(2)}, u32[]{:S(2)}) collective-permute-start(f32[324,128]{1,0:T(8,128)S(1)} %get-tuple-element.37), channel_id=1, source_target_pairs={{0,4},{4,8},{8,12},{12,16},{16,20},{20,24},{24,28},{28,0},{1,5},{5... | collective-permute-start | bytes 497672 | tf_op jit(solution)/shard_map/ppermute | solution.py:32
  34.1 10.4 %collective-permute-start.7 = (f32[324,128]{1,0:T(8,128)S(1)}, f32[324,128]{1,0:T(8,128)S(1)}, u32[]{:S(2)}, u32[]{:S(2)}) collective-permute-start(f32[324,128]{1,0:T(8,128)S(1)} %get-tuple-element.38), channel_id=1, source_target_pairs={{0,8},{4,12},{8,16},{12,20},{16,24},{20,28},{24,0},{28,4},{1,9},{5... | collective-permute-start | bytes 497672 | tf_op jit(solution)/shard_map/ppermute | solution.py:32
  47.4 3.1 %collective-permute-start.10 = (f32[324,128]{1,0:T(8,128)S(1)}, f32[324,128]{1,0:T(8,128)S(1)}, u32[]{:S(2)}, u32[]{:S(2)}) collective-permute-start(f32[324,128]{1,0:T(8,128)S(1)} %get-tuple-element.42), channel_id=1, source_target_pairs={{0,28},{4,0},{8,4},{12,8},{16,12},{20,16},{24,20},{28,24},{1,29},{... | collective-permute-start | bytes 497672 | tf_op jit(solution)/shard_map/ppermute | solution.py:32
  47.6 10.3 %collective-permute-start.11 = (f32[324,128]{1,0:T(8,128)S(1)}, f32[324,128]{1,0:T(8,128)S(1)}, u32[]{:S(2)}, u32[]{:S(2)}) collective-permute-start(f32[324,128]{1,0:T(8,128)S(1)} %get-tuple-element.43), channel_id=1, source_target_pairs={{0,24},{4,28},{8,0},{12,4},{16,8},{20,12},{24,16},{28,20},{1,25},{... | collective-permute-start | bytes 497672 | tf_op jit(solution)/shard_map/ppermute | solution.py:32
  50.3 12.2 %collective-permute-start.8 = (f32[324,128]{1,0:T(8,128)S(1)}, f32[324,128]{1,0:T(8,128)S(1)}, u32[]{:S(2)}, u32[]{:S(2)}) collective-permute-start(f32[324,128]{1,0:T(8,128)S(1)} %get-tuple-element.40), channel_id=1, source_target_pairs={{0,8},{4,12},{8,16},{12,20},{16,24},{20,28},{24,0},{28,4},{1,9},{5... | collective-permute-start | bytes 497672 | tf_op jit(solution)/shard_map/ppermute | solution.py:32
  50.3 12.2 %collective-permute-start.9 = (f32[324,128]{1,0:T(8,128)S(1)}, f32[324,128]{1,0:T(8,128)S(1)}, u32[]{:S(2)}, u32[]{:S(2)}) collective-permute-start(f32[324,128]{1,0:T(8,128)S(1)} %get-tuple-element.41), channel_id=1, source_target_pairs={{0,4},{4,8},{8,12},{12,16},{16,20},{20,24},{24,28},{28,0},{1,5},{5... | collective-permute-start | bytes 497672 | tf_op jit(solution)/shard_map/ppermute | solution.py:32
  74.1 7.2 %collective-permute-start.12 = (f32[324,128]{1,0:T(8,128)S(1)}, f32[324,128]{1,0:T(8,128)S(1)}, u32[]{:S(2)}, u32[]{:S(2)}) collective-permute-start(f32[324,128]{1,0:T(8,128)S(1)} %get-tuple-element.45), channel_id=1, source_target_pairs={{0,24},{4,28},{8,0},{12,4},{16,8},{20,12},{24,16},{28,20},{1,25},{... | collective-permute-start | bytes 497672 | tf_op jit(solution)/shard_map/ppermute | solution.py:32
  74.6 7.3 %collective-permute-start.13 = (f32[324,128]{1,0:T(8,128)S(1)}, f32[324,128]{1,0:T(8,128)S(1)}, u32[]{:S(2)}, u32[]{:S(2)}) collective-permute-start(f32[324,128]{1,0:T(8,128)S(1)} %get-tuple-element.46), channel_id=1, source_target_pairs={{0,28},{4,0},{8,4},{12,8},{16,12},{20,16},{24,20},{28,24},{1,29},{... | collective-permute-start | bytes 497672 | tf_op jit(solution)/shard_map/ppermute | solution.py:32
  74.6 7.5 %collective-permute-start.14 = (f32[324,128]{1,0:T(8,128)S(1)}, f32[324,128]{1,0:T(8,128)S(1)}, u32[]{:S(2)}, u32[]{:S(2)}) collective-permute-start(f32[324,128]{1,0:T(8,128)S(1)} %get-tuple-element.47), channel_id=1, source_target_pairs={{0,4},{4,8},{8,12},{12,16},{16,20},{20,24},{24,28},{28,0},{1,5},{5... | collective-permute-start | bytes 497672 | tf_op jit(solution)/shard_map/ppermute | solution.py:32
  75.1 11.4 %collective-permute-start.15 = (f32[324,128]{1,0:T(8,128)S(1)}, f32[324,128]{1,0:T(8,128)S(1)}, u32[]{:S(2)}, u32[]{:S(2)}) collective-permute-start(f32[324,128]{1,0:T(8,128)S(1)} %get-tuple-element.48), channel_id=1, source_target_pairs={{0,8},{4,12},{8,16},{12,20},{16,24},{20,28},{24,0},{28,4},{1,9},{5... | collective-permute-start | bytes 497672 | tf_op jit(solution)/shard_map/ppermute | solution.py:32
  88.9 1.1 copy-start.1
  89.9 5.1 %copy-start.4 = (s32[1296]{0:T(1024)S(1)}, s32[1296]{0:T(1024)}, u32[]{:S(2)}) copy-start(s32[1296]{0:T(1024)} %param.16) | copy-start | bytes 15556
  89.9 5.1 %copy-start.5 = (s32[1296]{0:T(1024)S(1)}, s32[1296]{0:T(1024)}, u32[]{:S(2)}) copy-start(s32[1296]{0:T(1024)} %param.15) | copy-start | bytes 15556
  89.9 36.2 %copy-start.2 = (f32[1296]{0:T(1024)S(1)}, f32[1296]{0:T(1024)}, u32[]{:S(2)}) copy-start(f32[1296]{0:T(1024)} %rate.1) | copy-start | bytes 15556
  89.9 36.2 %all-to-all-start = ((f32[4,648,128]{2,1,0:T(8,128)}), f32[4,648,128]{2,1,0:T(8,128)S(1)}, u32[]{:S(2)}, u32[]{:S(2)}) async-start(f32[4,648,128]{2,1,0:T(8,128)} %bitcast.6), calls=%async_computation | async-start | bytes 2654208 | tf_op jit(solution)/shard_map/all_to_all | solution.py:384

commit v3 on v2

--- a/solution.py
+++ b/solution.py
@@ -221,22 +221,29 @@
     pack_rows(sub, lanes, send, full, stages, outs)
 
 
-def leave_kernel(sub, lanes, halves, owned, send, weight, *rest):
+def leave_kernel(sub, lanes, halves, count, place, send, weight, *rest):
     incoming, rest = rest[:BLOCKS], rest[BLOCKS + 1 :]
-    full, out, square, stages = rest
+    full, outs, square, stages = rest[0], rest[1 : 1 + count], rest[1 + count], rest[2 + count]
     add_returned(sub, lanes, send, weight, incoming, square, stages, full)
-    per_target = sub * lanes * halves
-    for block in range(owned // LANES):
-        target, half = divmod(block, halves)
-        for part in range(sub):
-            tile = full[pl.ds(block * LANES * sub + part, LANES, stride=sub), :].T
-            first = target * per_target + part * lanes * halves + half
-            out[pl.ds(first, lanes, stride=halves), :] = tile[:lanes]
-
-
-def interact_kernel(halves, plus, minus, rate, energy, *rest):
-    out, kept, added = rest[0], rest[1], rest[2:]
+    for distance in range(count):
+        target = lax.rem(place[0] + distance, count)
+        for half in range(halves):
+            first = (target * halves + half) * LANES * sub
+            for part in range(sub):
+                tile = full[pl.ds(first + part, LANES, stride=sub), :].T
+                outs[distance][pl.ds(part * lanes * halves + half, lanes, stride=halves), :] = tile[:lanes]
+
+
+def interact_kernel(halves, count, place, plus, minus, rate, *rest):
+    pieces, rest = rest[:count], rest[count:]
+    out, energy, kept, added = rest[0], rest[1], rest[2], rest[3:]
     clear(added)
+    rows = pieces[0].shape[0]
+    for distance in range(count):
+        first = lax.rem(place[0] + count - distance, count) * rows
+        if rows % 8 == 0:
+            first = pl.multiple_of(first, 8)
+        energy[pl.ds(first, rows), :] = pieces[distance][...]
     bins = plus.shape[0]
     share = bins // GROUPS
     unroll = chunked(share, 12)
@@ -301,6 +308,7 @@
 
     send = (send_nodes[0] * sub).reshape(-1)
     nodes = (conn * sub).reshape(-1)
+    place = lax.axis_index("spec").reshape(1)
 
     bin_of = (
         lax.axis_index("spec") * row_count
@@ -370,30 +378,28 @@
                 name="between",
             )(send, weight, *incoming, full)
 
-    full, leaving = pl.pallas_call(
-        functools.partial(leave_kernel, sub, lanes, halves, owned),
-        out_shape=[full_shape, shape_of(spec_count * row_count * halves, LANES)],
-        in_specs=[SM] + [VM] * (2 + BLOCKS),
-        out_specs=[VM] * 2,
-        input_output_aliases={2 + BLOCKS: 0},
+    _, *blocks = pl.pallas_call(
+        functools.partial(leave_kernel, sub, lanes, halves, spec_count),
+        out_shape=[full_shape] + [shape_of(row_count * halves, LANES)] * spec_count,
+        in_specs=[SM] * 2 + [VM] * (2 + BLOCKS),
+        out_specs=[VM] * (1 + spec_count),
+        input_output_aliases={3 + BLOCKS: 0},
         scratch_shapes=[squares, stages],
         cost_estimate=cost(2 * owned * row_count, 4 * moved),
         compiler_params=limit(4),
         name="leave",
-    )(send, weight, *incoming, full)
-    arrived = lax.all_to_all(
-        leaving.reshape(spec_count, row_count * halves, LANES), "spec", split_axis=0, concat_axis=0
-    )
+    )(place, send, weight, *incoming, full)
+    pieces = [blocks[0]] + [passed_along(blocks[d], "spec", d) for d in range(1, spec_count)]
     return pl.pallas_call(
-        functools.partial(interact_kernel, halves),
+        functools.partial(interact_kernel, halves, spec_count),
         out_shape=shape_of(bins, halves * LANES),
-        in_specs=[SM] * 3 + [VM],
+        in_specs=[SM] * 4 + [VM] * spec_count,
         out_specs=VM,
-        scratch_shapes=[pltpu.VMEM((bins * halves, LANES), jnp.float32)] * (1 + 2 * GROUPS),
+        scratch_shapes=[pltpu.VMEM((bins * halves, LANES), jnp.float32)] * (2 + 2 * GROUPS),
         cost_estimate=cost(16 * bins * halves * LANES, 8 * bins * halves * LANES),
-        compiler_params=limit(10),
+        compiler_params=limit(12),
         name="interact",
-    )(dia_plus * halves, dia_minus * halves, dia_coeff, arrived.reshape(bins * halves, LANES))
+    )(place, dia_plus * halves, dia_minus * halves, dia_coeff, *pieces)
 
 
 def solution(mesh):

time: 134 us -> 126 us (0.940)
  the two profiles are of different devices: /device:TPU:0 before, /device:TPU:9 now
where the time goes in v3:
time: 126 us
  waiting for transfers between devices  54 us (43%)
  Pallas kernels  43 us (34%)
  starting transfers between devices  23.5 us (19%)
  local copies, waits for them, and re-layouts  2.88 us (2%)
  other arithmetic  2.42 us (2%)
    ppermute x19, waiting for transfers between devices, passed_along(): lax.ppermute(value, axis, [(source, (source + steps) % count) for source...  54 us
    ppermute x19, starting transfers between devices, passed_along(): lax.ppermute(value, axis, [(source, (source + steps) % count) for source...  23.5 us
    pallas_call x2, Pallas kernels, on_device(): pl.pallas_call(functools.partial(sweep_kernel, sub, lanes, shared, own_ro...  23.2 us
    pallas_call x1, Pallas kernels, on_device(): pl.pallas_call(functools.partial(interact_kernel, halves, spec_count), ou...  7 us
    pallas_call x1, Pallas kernels, on_device(): pl.pallas_call(functools.partial(slope_kernel, sub, shared), out_shape=[s...  4.88 us
    pallas_call x1, Pallas kernels, on_device(): pl.pallas_call(functools.partial(between_kernel, sub, lanes), out_shape=[...  2.91 us
    unnamed x11, local copies, waits for them, and re-layouts  2.86 us
    pallas_call x1, Pallas kernels, on_device(): pl.pallas_call(functools.partial(enter_kernel, sub, lanes), out_shape=[fu...  2.63 us
  transfers between devices with their start and end apart: 19, of which 11 were waited for; matrix products, arithmetic and copies ran while one was open for 2% of the time, Pallas kernels for 4%

profile of v3, /device:TPU:9, one launch (start us, length us, event | category | flops | bytes accessed | tf_op | source)
XLA Modules:
  0.0 125.9 jit_solution(17891998943975157896)
XLA Ops:
  2.0 2.6 %enter.1 = (f32[4608,128]{1,0:T(8,128)S(1)}, f32[324,128]{1,0:T(8,128)}, f32[324,128]{1,0:T(8,128)}, f32[324,128]{1,0:T(8,128)S(1)}, f32[324,128]{1,0:T(8,128)S(1)}) custom-call(s32[512]{0:T(512)S(1)} %multiply_bitcast_fusion.send, f32[324,1024]{1,0:T(8,128)S(1)} %copy-done), custom_call_target="tpu_custom_call" | custom-call | bytes 3145728 | tf_op jit(solution)/shard_map/enter/pallas_call | solution.py:331
  5.9 2.1 %collective-permute-start.1 = (f32[324,128]{1,0:T(8,128)}, f32[324,128]{1,0:T(8,128)S(1)}, u32[]{:S(2)}, u32[]{:S(2)}) collective-permute-start(f32[324,128]{1,0:T(8,128)} %get-tuple-element.34), channel_id=1, source_target_pairs={{0,4},{4,8},{8,12},{12,16},{16,20},{20,24},{24,28},{28,0},{1,5},{5... | collective-permute-start | bytes 497672 | tf_op jit(solution)/shard_map/ppermute | solution.py:32
  12.4 4.9 %slopes.1 = (f32[6144,128]{1,0:T(8,128)S(1)}, f32[3072,128]{1,0:T(8,128)S(1)}) custom-call(f32[2,3,2048]{2,1,0:T(4,128)S(1)} %copy.15.normals, f32[1,1024]{1,0:T(1,128)S(1)} %bitcast.4, f32[9,128]{1,0:T(8,128)S(1)} %pad_maximum_fusion.wave), custom_call_target="tpu_custom_call" | custom-call | flops 5242880 | bytes 4718592 | tf_op jit(solution)/shard_map/slopes/pallas_call | solution.py:342
  18.2 11.6 %sweep.2 = (f32[4608,128]{1,0:T(8,128)S(1)}, f32[324,128]{1,0:T(8,128)S(1)}, f32[324,128]{1,0:T(8,128)S(1)}, f32[324,128]{1,0:T(8,128)S(1)}, f32[324,128]{1,0:T(8,128)S(1)}) custom-call(s32[6144]{0:T(1024)S(1)} %reshape.51.conn, f32[6144,128]{1,0:T(8,128)S(1)} %get-tuple-element.32.coef, ...), custom_call_target="tpu_custom_call", output_to_operand_aliasing={{0}: (7, {})} | custom-call | flops 15925248 | bytes 12582912 | tf_op jit(solution)/shard_map/sweep/pallas_call | solution.py:356
  31.0 1.8 %collective-permute-start.5 = (f32[324,128]{1,0:T(8,128)S(1)}, f32[324,128]{1,0:T(8,128)S(1)}, u32[]{:S(2)}, u32[]{:S(2)}) collective-permute-start(f32[324,128]{1,0:T(8,128)S(1)} %get-tuple-element.39), channel_id=1, source_target_pairs={{0,28},{4,0},{8,4},{12,8},{16,12},{20,16},{24,20},{28,24},{1,29},{... | collective-permute-start | bytes 497672 | tf_op jit(solution)/shard_map/ppermute | solution.py:32
  33.0 2.1 %collective-permute-start.7 = (f32[324,128]{1,0:T(8,128)S(1)}, f32[324,128]{1,0:T(8,128)S(1)}, u32[]{:S(2)}, u32[]{:S(2)}) collective-permute-start(f32[324,128]{1,0:T(8,128)S(1)} %get-tuple-element.41), channel_id=1, source_target_pairs={{0,8},{4,12},{8,16},{12,20},{16,24},{20,28},{24,0},{28,4},{1,9},{5... | collective-permute-start | bytes 497672 | tf_op jit(solution)/shard_map/ppermute | solution.py:32
  35.1 4.8 %collective-permute-done.5.rest_1_ = f32[324,128]{1,0:T(8,128)S(1)} collective-permute-done((f32[324,128]{1,0:T(8,128)S(1)}, f32[324,128]{1,0:T(8,128)S(1)}, u32[]{:S(2)}, u32[]{:S(2)}) %collective-permute-start.5) | collective-permute-done | bytes 165920 | tf_op jit(solution)/shard_map/ppermute | solution.py:32
  39.9 3.5 %collective-permute-done.7.rest_3_ = f32[324,128]{1,0:T(8,128)S(1)} collective-permute-done((f32[324,128]{1,0:T(8,128)S(1)}, f32[324,128]{1,0:T(8,128)S(1)}, u32[]{:S(2)}, u32[]{:S(2)}) %collective-permute-start.7) | collective-permute-done | bytes 165920 | tf_op jit(solution)/shard_map/ppermute | solution.py:32
  43.5 2.9 %between.1 = (f32[4608,128]{1,0:T(8,128)S(1)}, f32[324,128]{1,0:T(8,128)S(1)}, f32[324,128]{1,0:T(8,128)S(1)}, f32[324,128]{1,0:T(8,128)S(1)}, f32[324,128]{1,0:T(8,128)S(1)}) custom-call(s32[512]{0:T(512)S(1)} %multiply_bitcast_fusion.send, f32[3072,128]{1,0:T(8,128)S(1)} %get-tuple-element.31.weight, ...), custom_call_target="tpu_custom_call", output_to_operand_aliasing={{0}: (6, {})} | custom-call | flops 663552 | bytes 6291456 | tf_op jit(solution)/shard_map/between/pallas_call | solution.py:369
  46.8 2.0 %collective-permute-start.11 = (f32[324,128]{1,0:T(8,128)S(1)}, f32[324,128]{1,0:T(8,128)S(1)}, u32[]{:S(2)}, u32[]{:S(2)}) collective-permute-start(f32[324,128]{1,0:T(8,128)S(1)} %get-tuple-element.46), channel_id=1, source_target_pairs={{0,24},{4,28},{8,0},{12,4},{16,8},{20,12},{24,16},{28,20},{1,25},{... | collective-permute-start | bytes 497672 | tf_op jit(solution)/shard_map/ppermute | solution.py:32
  48.8 2.3 %collective-permute-start.9 = (f32[324,128]{1,0:T(8,128)S(1)}, f32[324,128]{1,0:T(8,128)S(1)}, u32[]{:S(2)}, u32[]{:S(2)}) collective-permute-start(f32[324,128]{1,0:T(8,128)S(1)} %get-tuple-element.44), channel_id=1, source_target_pairs={{0,4},{4,8},{8,12},{12,16},{16,20},{20,24},{24,28},{28,0},{1,5},{5... | collective-permute-start | bytes 497672 | tf_op jit(solution)/shard_map/ppermute | solution.py:32
  51.1 1.9 %collective-permute-done.10.rest_2_ = f32[324,128]{1,0:T(8,128)S(1)} collective-permute-done((f32[324,128]{1,0:T(8,128)S(1)}, f32[324,128]{1,0:T(8,128)S(1)}, u32[]{:S(2)}, u32[]{:S(2)}) %collective-permute-start.10) | collective-permute-done | bytes 165920 | tf_op jit(solution)/shard_map/ppermute | solution.py:32
  53.0 4.2 %collective-permute-done.8.rest_0_ = f32[324,128]{1,0:T(8,128)S(1)} collective-permute-done((f32[324,128]{1,0:T(8,128)S(1)}, f32[324,128]{1,0:T(8,128)S(1)}, u32[]{:S(2)}, u32[]{:S(2)}) %collective-permute-start.8) | collective-permute-done | bytes 165920 | tf_op jit(solution)/shard_map/ppermute | solution.py:32
  58.3 11.6 %sweep.3 = (f32[4608,128]{1,0:T(8,128)S(1)}, f32[324,128]{1,0:T(8,128)S(1)}, f32[324,128]{1,0:T(8,128)S(1)}, f32[324,128]{1,0:T(8,128)S(1)}, f32[324,128]{1,0:T(8,128)S(1)}) custom-call(s32[6144]{0:T(1024)S(1)} %reshape.51.conn, f32[6144,128]{1,0:T(8,128)S(1)} %get-tuple-element.32.coef, ...), custom_call_target="tpu_custom_call", output_to_operand_aliasing={{0}: (7, {})} | custom-call | flops 15925248 | bytes 12582912 | tf_op jit(solution)/shard_map/sweep/pallas_call | solution.py:356
  70.0 2.1 %collective-permute-start.12 = (f32[324,128]{1,0:T(8,128)S(1)}, f32[324,128]{1,0:T(8,128)S(1)}, u32[]{:S(2)}, u32[]{:S(2)}) collective-permute-start(f32[324,128]{1,0:T(8,128)S(1)} %get-tuple-element.48), channel_id=1, source_target_pairs={{0,24},{4,28},{8,0},{12,4},{16,8},{20,12},{24,16},{28,20},{1,25},{... | collective-permute-start | bytes 497672 | tf_op jit(solution)/shard_map/ppermute | solution.py:32
  72.1 1.8 %collective-permute-start.13 = (f32[324,128]{1,0:T(8,128)S(1)}, f32[324,128]{1,0:T(8,128)S(1)}, u32[]{:S(2)}, u32[]{:S(2)}) collective-permute-start(f32[324,128]{1,0:T(8,128)S(1)} %get-tuple-element.49), channel_id=1, source_target_pairs={{0,28},{4,0},{8,4},{12,8},{16,12},{20,16},{24,20},{28,24},{1,29},{... | collective-permute-start | bytes 497672 | tf_op jit(solution)/shard_map/ppermute | solution.py:32
  75.2 8.4 %collective-permute-done.13.rest_1_ = f32[324,128]{1,0:T(8,128)S(1)} collective-permute-done((f32[324,128]{1,0:T(8,128)S(1)}, f32[324,128]{1,0:T(8,128)S(1)}, u32[]{:S(2)}, u32[]{:S(2)}) %collective-permute-start.13) | collective-permute-done | bytes 165920 | tf_op jit(solution)/shard_map/ppermute | solution.py:32
  84.5 2.4 %leave.1 = (f32[4608,128]{1,0:T(8,128)S(1)}, f32[648,128]{1,0:T(8,128)S(1)}, f32[648,128]{1,0:T(8,128)S(1)}, f32[648,128]{1,0:T(8,128)S(1)}, f32[648,128]{1,0:T(8,128)S(1)}) custom-call(s32[1]{0:T(128)} %bitcast.place, s32[512]{0:T(512)S(1)} %multiply_bitcast_fusion.send, f32[3072,128]{1,0:T(8,128)S(1)} %get-tuple-element.31.weight, ...), custom_call_target="tpu_custom_call", output_to_operand_aliasing={{0}: (7, {})} | custom-call | flops 663552 | bytes 6291456 | tf_op jit(solution)/shard_map/leave/pallas_call | solution.py:381
  86.9 1.4 %collective-permute-start.16 = (f32[648,128]{1,0:T(8,128)S(1)}, f32[648,128]{1,0:T(8,128)S(1)}, u32[]{:S(2)}, u32[]{:S(2)}) collective-permute-start(f32[648,128]{1,0:T(8,128)S(1)} %get-tuple-element.54), channel_id=1, source_target_pairs={{0,1},{1,2},{2,3},{3,0},{4,5},{5,6},{6,7},{7,4},{8,9},{9,10},{10,1... | collective-permute-start | bytes 995336 | tf_op jit(solution)/shard_map/ppermute | solution.py:32
  89.4 1.4 %collective-permute-start.18 = (f32[648,128]{1,0:T(8,128)S(1)}, f32[648,128]{1,0:T(8,128)S(1)}, u32[]{:S(2)}, u32[]{:S(2)}) collective-permute-start(f32[648,128]{1,0:T(8,128)S(1)} %get-tuple-element.56), channel_id=1, source_target_pairs={{0,3},{1,0},{2,1},{3,2},{4,7},{5,4},{6,5},{7,6},{8,11},{9,8},{10,9... | collective-permute-start | bytes 995336 | tf_op jit(solution)/shard_map/ppermute | solution.py:32
  90.8 4.2 %collective-permute-done.16.rest_1_ = f32[648,128]{1,0:T(8,128)S(1)} collective-permute-done((f32[648,128]{1,0:T(8,128)S(1)}, f32[648,128]{1,0:T(8,128)S(1)}, u32[]{:S(2)}, u32[]{:S(2)}) %collective-permute-start.16) | collective-permute-done | bytes 331808 | tf_op jit(solution)/shard_map/ppermute | solution.py:32
  95.0 20.4 %collective-permute-done.17.rest_2_ = f32[648,128]{1,0:T(8,128)S(1)} collective-permute-done((f32[648,128]{1,0:T(8,128)S(1)}, f32[648,128]{1,0:T(8,128)S(1)}, u32[]{:S(2)}, u32[]{:S(2)}) %collective-permute-start.17) | collective-permute-done | bytes 331808 | tf_op jit(solution)/shard_map/ppermute | solution.py:32
  115.4 3.5 %collective-permute-done.18.rest_3_ = f32[648,128]{1,0:T(8,128)S(1)} collective-permute-done((f32[648,128]{1,0:T(8,128)S(1)}, f32[648,128]{1,0:T(8,128)S(1)}, u32[]{:S(2)}, u32[]{:S(2)}) %collective-permute-start.18) | collective-permute-done | bytes 331808 | tf_op jit(solution)/shard_map/ppermute | solution.py:32
  118.9 7.0 %interact.1 = f32[1296,256]{1,0:T(8,128)} custom-call(s32[1]{0:T(128)} %bitcast.place, s32[1296]{0:T(1024)S(1)} %get-tuple-element.60.plus, s32[1296]{0:T(1024)S(1)} %get-tuple-element.59.minus, f32[1296]{0:T(1024)S(1)} %copy-done.1, f32[648,128]{1,0:T(8,128)S(1)} %get-tuple-element.53.rest_0_, f32[648,128]{1,0:T(8,128)S(1)} %collective-permute-done.16.rest_1_, ...), custom_call_target="tpu_custom_call" | custom-call | flops 5308416 | bytes 2654208 | tf_op jit(solution)/shard_map/interact/pallas_call | solution.py:393
  (41 shorter events, 14.9 us)
Async XLA Ops:
  0.7 1.3 %copy-start = (f32[324,1024]{1,0:T(8,128)S(1)}, f32[324,1024]{1,0:T(8,128)}, u32[]{:S(2)}) copy-start(f32[324,1024]{1,0:T(8,128)} %spectrum.1) | copy-start | bytes 3981316
  4.6 12.6 %collective-permute-start = (f32[324,128]{1,0:T(8,128)}, f32[324,128]{1,0:T(8,128)S(1)}, u32[]{:S(2)}, u32[]{:S(2)}) collective-permute-start(f32[324,128]{1,0:T(8,128)} %get-tuple-element.33), channel_id=1, source_target_pairs={{0,8},{4,12},{8,16},{12,20},{16,24},{20,28},{24,0},{28,4},{1,9},{5... | collective-permute-start | bytes 497672 | tf_op jit(solution)/shard_map/ppermute | solution.py:32
  5.9 11.4 %collective-permute-start.1 = (f32[324,128]{1,0:T(8,128)}, f32[324,128]{1,0:T(8,128)S(1)}, u32[]{:S(2)}, u32[]{:S(2)}) collective-permute-start(f32[324,128]{1,0:T(8,128)} %get-tuple-element.34), channel_id=1, source_target_pairs={{0,4},{4,8},{8,12},{12,16},{16,20},{20,24},{24,28},{28,0},{1,5},{5... | collective-permute-start | bytes 497672 | tf_op jit(solution)/shard_map/ppermute | solution.py:32
  7.9 9.4 %collective-permute-start.2 = (f32[324,128]{1,0:T(8,128)S(1)}, f32[324,128]{1,0:T(8,128)S(1)}, u32[]{:S(2)}, u32[]{:S(2)}) collective-permute-start(f32[324,128]{1,0:T(8,128)S(1)} %get-tuple-element.35), channel_id=1, source_target_pairs={{0,28},{4,0},{8,4},{12,8},{16,12},{20,16},{24,20},{28,24},{1,29},{... | collective-permute-start | bytes 497672 | tf_op jit(solution)/shard_map/ppermute | solution.py:32
  7.9 10.3 %collective-permute-start.3 = (f32[324,128]{1,0:T(8,128)S(1)}, f32[324,128]{1,0:T(8,128)S(1)}, u32[]{:S(2)}, u32[]{:S(2)}) collective-permute-start(f32[324,128]{1,0:T(8,128)S(1)} %get-tuple-element.36), channel_id=1, source_target_pairs={{0,24},{4,28},{8,0},{12,4},{16,8},{20,12},{24,16},{28,20},{1,25},{... | collective-permute-start | bytes 497672 | tf_op jit(solution)/shard_map/ppermute | solution.py:32
  11.7 0.7 copy-start.2
  29.8 5.3 %collective-permute-start.4 = (f32[324,128]{1,0:T(8,128)S(1)}, f32[324,128]{1,0:T(8,128)S(1)}, u32[]{:S(2)}, u32[]{:S(2)}) collective-permute-start(f32[324,128]{1,0:T(8,128)S(1)} %get-tuple-element.38), channel_id=1, source_target_pairs={{0,24},{4,28},{8,0},{12,4},{16,8},{20,12},{24,16},{28,20},{1,25},{... | collective-permute-start | bytes 497672 | tf_op jit(solution)/shard_map/ppermute | solution.py:32
  31.0 8.9 %collective-permute-start.5 = (f32[324,128]{1,0:T(8,128)S(1)}, f32[324,128]{1,0:T(8,128)S(1)}, u32[]{:S(2)}, u32[]{:S(2)}) collective-permute-start(f32[324,128]{1,0:T(8,128)S(1)} %get-tuple-element.39), channel_id=1, source_target_pairs={{0,28},{4,0},{8,4},{12,8},{16,12},{20,16},{24,20},{28,24},{1,29},{... | collective-permute-start | bytes 497672 | tf_op jit(solution)/shard_map/ppermute | solution.py:32
  32.8 7.1 %collective-permute-start.6 = (f32[324,128]{1,0:T(8,128)S(1)}, f32[324,128]{1,0:T(8,128)S(1)}, u32[]{:S(2)}, u32[]{:S(2)}) collective-permute-start(f32[324,128]{1,0:T(8,128)S(1)} %get-tuple-element.40), channel_id=1, source_target_pairs={{0,4},{4,8},{8,12},{12,16},{16,20},{20,24},{24,28},{28,0},{1,5},{5... | collective-permute-start | bytes 497672 | tf_op jit(solution)/shard_map/ppermute | solution.py:32
  33.0 10.5 %collective-permute-start.7 = (f32[324,128]{1,0:T(8,128)S(1)}, f32[324,128]{1,0:T(8,128)S(1)}, u32[]{:S(2)}, u32[]{:S(2)}) collective-permute-start(f32[324,128]{1,0:T(8,128)S(1)} %get-tuple-element.41), channel_id=1, source_target_pairs={{0,8},{4,12},{8,16},{12,20},{16,24},{20,28},{24,0},{28,4},{1,9},{5... | collective-permute-start | bytes 497672 | tf_op jit(solution)/shard_map/ppermute | solution.py:32
  46.4 6.6 %collective-permute-start.10 = (f32[324,128]{1,0:T(8,128)S(1)}, f32[324,128]{1,0:T(8,128)S(1)}, u32[]{:S(2)}, u32[]{:S(2)}) collective-permute-start(f32[324,128]{1,0:T(8,128)S(1)} %get-tuple-element.45), channel_id=1, source_target_pairs={{0,28},{4,0},{8,4},{12,8},{16,12},{20,16},{24,20},{28,24},{1,29},{... | collective-permute-start | bytes 497672 | tf_op jit(solution)/shard_map/ppermute | solution.py:32
  46.8 6.2 %collective-permute-start.11 = (f32[324,128]{1,0:T(8,128)S(1)}, f32[324,128]{1,0:T(8,128)S(1)}, u32[]{:S(2)}, u32[]{:S(2)}) collective-permute-start(f32[324,128]{1,0:T(8,128)S(1)} %get-tuple-element.46), channel_id=1, source_target_pairs={{0,24},{4,28},{8,0},{12,4},{16,8},{20,12},{24,16},{28,20},{1,25},{... | collective-permute-start | bytes 497672 | tf_op jit(solution)/shard_map/ppermute | solution.py:32
  48.8 8.4 %collective-permute-start.8 = (f32[324,128]{1,0:T(8,128)S(1)}, f32[324,128]{1,0:T(8,128)S(1)}, u32[]{:S(2)}, u32[]{:S(2)}) collective-permute-start(f32[324,128]{1,0:T(8,128)S(1)} %get-tuple-element.43), channel_id=1, source_target_pairs={{0,8},{4,12},{8,16},{12,20},{16,24},{20,28},{24,0},{28,4},{1,9},{5... | collective-permute-start | bytes 497672 | tf_op jit(solution)/shard_map/ppermute | solution.py:32
  48.8 9.5 %collective-permute-start.9 = (f32[324,128]{1,0:T(8,128)S(1)}, f32[324,128]{1,0:T(8,128)S(1)}, u32[]{:S(2)}, u32[]{:S(2)}) collective-permute-start(f32[324,128]{1,0:T(8,128)S(1)} %get-tuple-element.44), channel_id=1, source_target_pairs={{0,4},{4,8},{8,12},{12,16},{16,20},{20,24},{24,28},{28,0},{1,5},{5... | collective-permute-start | bytes 497672 | tf_op jit(solution)/shard_map/ppermute | solution.py:32
  70.0 20.8 %copy-start.3 = (s32[1296]{0:T(1024)S(1)}, s32[1296]{0:T(1024)}, u32[]{:S(2)}) copy-start(s32[1296]{0:T(1024)} %param.16) | copy-start | bytes 15556
  70.0 20.8 %copy-start.4 = (s32[1296]{0:T(1024)S(1)}, s32[1296]{0:T(1024)}, u32[]{:S(2)}) copy-start(s32[1296]{0:T(1024)} %param.15) | copy-start | bytes 15556
  70.0 48.9 %copy-start.1 = (f32[1296]{0:T(1024)S(1)}, f32[1296]{0:T(1024)}, u32[]{:S(2)}) copy-start(f32[1296]{0:T(1024)} %rate.1) | copy-start | bytes 15556
  70.0 5.2 %collective-permute-start.12 = (f32[324,128]{1,0:T(8,128)S(1)}, f32[324,128]{1,0:T(8,128)S(1)}, u32[]{:S(2)}, u32[]{:S(2)}) collective-permute-start(f32[324,128]{1,0:T(8,128)S(1)} %get-tuple-element.48), channel_id=1, source_target_pairs={{0,24},{4,28},{8,0},{12,4},{16,8},{20,12},{24,16},{28,20},{1,25},{... | collective-permute-start | bytes 497672 | tf_op jit(solution)/shard_map/ppermute | solution.py:32
  72.1 11.6 %collective-permute-start.13 = (f32[324,128]{1,0:T(8,128)S(1)}, f32[324,128]{1,0:T(8,128)S(1)}, u32[]{:S(2)}, u32[]{:S(2)}) collective-permute-start(f32[324,128]{1,0:T(8,128)S(1)} %get-tuple-element.49), channel_id=1, source_target_pairs={{0,28},{4,0},{8,4},{12,8},{16,12},{20,16},{24,20},{28,24},{1,29},{... | collective-permute-start | bytes 497672 | tf_op jit(solution)/shard_map/ppermute | solution.py:32
  73.8 9.8 %collective-permute-start.14 = (f32[324,128]{1,0:T(8,128)S(1)}, f32[324,128]{1,0:T(8,128)S(1)}, u32[]{:S(2)}, u32[]{:S(2)}) collective-permute-start(f32[324,128]{1,0:T(8,128)S(1)} %get-tuple-element.50), channel_id=1, source_target_pairs={{0,4},{4,8},{8,12},{12,16},{16,20},{20,24},{24,28},{28,0},{1,5},{5... | collective-permute-start | bytes 497672 | tf_op jit(solution)/shard_map/ppermute | solution.py:32
  75.0 9.5 %collective-permute-start.15 = (f32[324,128]{1,0:T(8,128)S(1)}, f32[324,128]{1,0:T(8,128)S(1)}, u32[]{:S(2)}, u32[]{:S(2)}) collective-permute-start(f32[324,128]{1,0:T(8,128)S(1)} %get-tuple-element.51), channel_id=1, source_target_pairs={{0,8},{4,12},{8,16},{12,20},{16,24},{20,28},{24,0},{28,4},{1,9},{5... | collective-permute-start | bytes 497672 | tf_op jit(solution)/shard_map/ppermute | solution.py:32
  86.9 8.1 %collective-permute-start.16 = (f32[648,128]{1,0:T(8,128)S(1)}, f32[648,128]{1,0:T(8,128)S(1)}, u32[]{:S(2)}, u32[]{:S(2)}) collective-permute-start(f32[648,128]{1,0:T(8,128)S(1)} %get-tuple-element.54), channel_id=1, source_target_pairs={{0,1},{1,2},{2,3},{3,0},{4,5},{5,6},{6,7},{7,4},{8,9},{9,10},{10,1... | collective-permute-start | bytes 995336 | tf_op jit(solution)/shard_map/ppermute | solution.py:32
  88.3 27.1 %collective-permute-start.17 = (f32[648,128]{1,0:T(8,128)S(1)}, f32[648,128]{1,0:T(8,128)S(1)}, u32[]{:S(2)}, u32[]{:S(2)}) collective-permute-start(f32[648,128]{1,0:T(8,128)S(1)} %get-tuple-element.55), channel_id=1, source_target_pairs={{0,2},{1,3},{2,0},{3,1},{4,6},{5,7},{6,4},{7,5},{8,10},{9,11},{10,... | collective-permute-start | bytes 995336 | tf_op jit(solution)/shard_map/ppermute | solution.py:32
  89.4 29.6 %collective-permute-start.18 = (f32[648,128]{1,0:T(8,128)S(1)}, f32[648,128]{1,0:T(8,128)S(1)}, u32[]{:S(2)}, u32[]{:S(2)}) collective-permute-start(f32[648,128]{1,0:T(8,128)S(1)} %get-tuple-element.56), channel_id=1, source_target_pairs={{0,3},{1,0},{2,1},{3,2},{4,7},{5,4},{6,5},{7,6},{8,11},{9,8},{10,9... | collective-permute-start | bytes 995336 | tf_op jit(solution)/shard_map/ppermute | solution.py:32

commit v4 on v3

--- a/solution.py
+++ b/solution.py
@@ -8,6 +8,7 @@
 from jax.experimental.pallas import tpu as pltpu
 from jax.sharding import PartitionSpec as P
 
+
 NDIR = 36
 REACH = 2
 STEPS = 2
@@ -15,6 +16,7 @@
 LANES = 128
 GROUPS = 2
 
+
 weight_plus = 1.25 ** (-4)
 weight_minus = 0.75 ** (-4)
 weight_both = 0.9375 ** (-4)
@@ -36,10 +38,10 @@
     return max(size for size in range(1, limit + 1) if total % size == 0)
 
 
-def rows_to_block(sub, lanes, stage, block):
+def rows_to_block(sub, lanes, stage, block, start=0):
     for column in range(block.shape[1] // LANES):
-        for part in range(sub):
-            tile = stage[pl.ds(column * LANES * sub + part, LANES, stride=sub), :].T
+        for part in range(block.shape[0] // lanes):
+            tile = stage[pl.ds(column * LANES * sub + start + part, LANES, stride=sub), :].T
             block[part * lanes : (part + 1) * lanes, column * LANES : (column + 1) * LANES] = tile[:lanes]
 
 
@@ -88,7 +90,7 @@
 def slope_kernel(sub, shared, normals, step_weight, wave, coef, weight, lines):
     elements = normals.shape[2]
     parts = 1 if shared else sub
-    pitch = coef.shape[0] // elements
+    plane = elements * parts
     lines[...] = jnp.zeros_like(lines)
     for component in range(2):
         for corner in range(2):
@@ -104,14 +106,18 @@
         for group in range(LANES // 8):
             at = slice(group * 8, group * 8 + 8)
             x0, x1, y0, y1 = (spread(turned[at, j : j + 1]) for j in range(4))
-            base = (k * LANES + group * 8) * pitch
+            base = (k * LANES + group * 8) * parts
             for part in range(parts):
                 east, north = wave[part : part + 1, :], wave[sub + part : sub + part + 1, :]
                 first = x0 * east + y0 * north
                 second = x1 * east + y1 * north
                 inward = jnp.minimum(first, 0.0) + jnp.minimum(second, 0.0) - jnp.maximum(first + second, 0.0)
                 for which, value in enumerate((first, second, 1.0 / inward)):
-                    coef[pl.ds(base + which * parts + part, 8, stride=pitch), :] = value
+                    first_row = which * plane + base
+                    if parts == 1:
+                        coef[pl.ds(pl.multiple_of(first_row, 8), 8), :] = value
+                    else:
+                        coef[pl.ds(first_row + part, 8, stride=parts), :] = value
 
     nodes = step_weight.shape[1]
     for block in range(nodes // LANES):
@@ -130,14 +136,14 @@
     return result
 
 
-def sweep_kernel(sub, lanes, shared, own_rows, conn, coef, weight, *rest):
+def sweep_kernel(sub, groups, lanes, shared, own_rows, conn, coef, weight, *rest):
     ghosts, full, rest = rest[:BLOCKS], rest[BLOCKS + 1], rest[BLOCKS + 2 :]
-    returned, square, stages, sums = rest[:BLOCKS], rest[BLOCKS], rest[BLOCKS + 1], rest[BLOCKS + 2 :]
+    returned, rest = rest[: BLOCKS * len(groups)], rest[BLOCKS * len(groups) :]
+    square, stages, sums = rest[0], rest[1], rest[2:]
     clear(sums)
     ghost_rows = (full.shape[0] - own_rows) // BLOCKS
     elements = conn.shape[0] // 3
     parts = 1 if shared else sub
-    pitch = coef.shape[0] // elements
     square[...] = jnp.zeros_like(square)
     for position in range(BLOCKS):
         block_to_rows(sub, lanes, ghosts[position], square, full, own_rows + position * ghost_rows)
@@ -156,9 +162,9 @@
                 element = group * share + k * unroll + u
                 index = [item[u] for item in listed[group]]
                 value = [full[pl.ds(row, sub), :] for row in index]
-                tile = coef[pl.ds(element * pitch, pitch), :]
                 first, second, inverse = (
-                    jnp.broadcast_to(tile[j * parts : (j + 1) * parts], (sub, LANES)) for j in range(3)
+                    jnp.broadcast_to(coef[pl.ds((j * elements + element) * parts, parts), :], (sub, LANES))
+                    for j in range(3)
                 )
                 both = first + second
                 inflow = jnp.minimum(first, 0.0) * value[0] + jnp.minimum(second, 0.0) * value[1]
@@ -182,7 +188,9 @@
             at = pl.multiple_of(k * step, step)
             stage[pl.ds(at, step), :] = total(sums, pl.ds(own_rows + position * ghost_rows + at, step))
 
-        rows_to_block(sub, lanes, stage, returned[position])
+    for which, (start, _) in enumerate(groups):
+        for position in range(BLOCKS):
+            rows_to_block(sub, lanes, stages.at[position], returned[which * BLOCKS + position], start)
 
     own_step = chunked(own_rows, 64)
 
@@ -192,12 +200,13 @@
         full[at, :] = full[at, :] - weight[at, :] * total(sums, at)
 
 
-def add_returned(sub, lanes, send, weight, incoming, square, stages, full):
+def add_returned(parts, lanes, send, weight, incoming, square, stages, full):
+    start, size = parts
     slots = incoming[0].shape[1]
     square[...] = jnp.zeros_like(square)
     unroll = chunked(slots, 16)
     for position in range(BLOCKS):
-        block_to_rows(sub, lanes, incoming[position], square, stages.at[position], 0)
+        block_to_rows(size, lanes, incoming[position], square, stages.at[position], 0)
     for position in range(BLOCKS):
         stage = stages.at[position]
 
@@ -205,45 +214,47 @@
         def _(k):
             first = k * unroll
             listed = send.at[pl.ds((BLOCKS - 1 - position) * slots + first, unroll)]
-            rows = [listed[u] for u in range(unroll)]
+            rows = [pl.ds(listed[u] + start, size) for u in range(unroll)]
             fresh = [
-                full[pl.ds(row, sub), :] - weight[pl.ds(row, sub), :] * stage[pl.ds((first + u) * sub, sub), :]
+                full[row, :] - weight[row, :] * stage[pl.ds((first + u) * size, size), :]
                 for u, row in enumerate(rows)
             ]
             for row, item in zip(rows, fresh):
-                full[pl.ds(row, sub), :] = item
+                full[row, :] = item
 
 
 def between_kernel(sub, lanes, send, weight, *rest):
     incoming, rest = rest[:BLOCKS], rest[BLOCKS + 1 :]
     full, outs, square, stages = rest[0], rest[1 : 1 + BLOCKS], rest[1 + BLOCKS], rest[2 + BLOCKS]
-    add_returned(sub, lanes, send, weight, incoming, square, stages, full)
+    add_returned((0, sub), lanes, send, weight, incoming, square, stages, full)
     pack_rows(sub, lanes, send, full, stages, outs)
 
 
-def leave_kernel(sub, lanes, halves, count, place, send, weight, *rest):
+def leave_kernel(sub, parts, lanes, halves, count, place, send, weight, *rest):
     incoming, rest = rest[:BLOCKS], rest[BLOCKS + 1 :]
     full, outs, square, stages = rest[0], rest[1 : 1 + count], rest[1 + count], rest[2 + count]
-    add_returned(sub, lanes, send, weight, incoming, square, stages, full)
+    add_returned(parts, lanes, send, weight, incoming, square, stages, full)
+    start, size = parts
     for distance in range(count):
         target = lax.rem(place[0] + distance, count)
         for half in range(halves):
-            first = (target * halves + half) * LANES * sub
-            for part in range(sub):
+            first = (target * halves + half) * LANES * sub + start
+            for part in range(size):
                 tile = full[pl.ds(first + part, LANES, stride=sub), :].T
                 outs[distance][pl.ds(part * lanes * halves + half, lanes, stride=halves), :] = tile[:lanes]
 
 
-def interact_kernel(halves, count, place, plus, minus, rate, *rest):
-    pieces, rest = rest[:count], rest[count:]
-    out, energy, kept, added = rest[0], rest[1], rest[2], rest[3:]
+def interact_kernel(per_source, halves, count, starts, place, plus, minus, rate, *rest):
+    pieces, rest = rest[: count * len(starts)], rest[count * len(starts) :]
+    target, energy, kept, added, out, done = rest[0], rest[1], rest[2], rest[3:-2], rest[-2], rest[-1]
     clear(added)
-    rows = pieces[0].shape[0]
-    for distance in range(count):
-        first = lax.rem(place[0] + count - distance, count) * rows
-        if rows % 8 == 0:
-            first = pl.multiple_of(first, 8)
-        energy[pl.ds(first, rows), :] = pieces[distance][...]
+    for which, start in enumerate(starts):
+        for distance in range(count):
+            piece = pieces[which * count + distance]
+            first = lax.rem(place[0] + count - distance, count) * per_source + start
+            if per_source % 8 == 0 and start % 8 == 0:
+                first = pl.multiple_of(first, 8)
+            energy[pl.ds(first, piece.shape[0]), :] = piece[...]
     bins = plus.shape[0]
     share = bins // GROUPS
     unroll = chunked(share, 12)
@@ -266,14 +277,23 @@
                 for item, row in zip(added[2 * group :], (up, down)):
                     item[pl.ds(row, halves), :] = item[pl.ds(row, halves), :] + term
 
-    step = chunked(bins, 48)
-
-    @pl.loop(0, bins // step)
-    def _(k):
-        for half in range(halves):
-            at = pl.ds(k * step * halves + half, step, stride=halves)
-            result = kept[at, :] + total(added, at)
-            out[pl.ds(pl.multiple_of(k * step, step), step), half * LANES : (half + 1) * LANES] = result
+    copies = done.shape[0]
+    share = bins // copies
+    step = chunked(share, 48)
+    for which in range(copies):
+
+        @pl.loop(which * share // step, (which + 1) * share // step)
+        def _(k):
+            for half in range(halves):
+                at = pl.ds(k * step * halves + half, step, stride=halves)
+                result = kept[at, :] + total(added, at)
+                out[pl.ds(pl.multiple_of(k * step, step), step), half * LANES : (half + 1) * LANES] = result
+
+        at = pl.ds(which * share, share)
+        pltpu.make_async_copy(out.at[at], target.at[at], done.at[which]).start()
+    for which in range(copies):
+        at = pl.ds(which * share, share)
+        pltpu.make_async_copy(out.at[at], target.at[at], done.at[which]).wait()
 
 
 def shape_of(*dims):
@@ -321,7 +341,11 @@
     speed = jnp.sum(select * group_speed, axis=2)
     wave = jnp.concatenate([east, north, speed])
 
-    block_shapes = [shape_of(row_count, slots)] * BLOCKS
+    def blocks_of(groups):
+        return [shape_of(size * lanes, slots) for _, size in groups for _ in range(BLOCKS)]
+
+    whole = ((0, sub),)
+    block_shapes = blocks_of(whole)
     full_shape = shape_of(rows, LANES)
     sums = [pltpu.VMEM((rows, LANES), jnp.float32)] * (3 * GROUPS)
     squares = pltpu.VMEM((4, LANES, LANES), jnp.float32)
@@ -352,19 +376,22 @@
 
     for sweep_index in range(STEPS):
         again = sweep_index < STEPS - 1
+        groups = whole if again or sub == 1 else ((0, 1), (1, sub - 1))
         ghosts = [passed_along(outs[p], "dom", -offset_of(p)) for p in range(BLOCKS)]
         full, *returned = pl.pallas_call(
-            functools.partial(sweep_kernel, sub, lanes, shared, own_rows),
-            out_shape=[full_shape] + block_shapes,
+            functools.partial(sweep_kernel, sub, groups, lanes, shared, own_rows),
+            out_shape=[full_shape] + blocks_of(groups),
             in_specs=[SM] + [VM] * (3 + BLOCKS),
-            out_specs=[VM] * (1 + BLOCKS),
+            out_specs=[VM] * (1 + BLOCKS * len(groups)),
             input_output_aliases={3 + BLOCKS: 0},
             scratch_shapes=[squares, stages] + sums,
             cost_estimate=cost(elements * 24 * row_count, 4 * LANES * (3 * elements + 4 * rows)),
             compiler_params=limit(20),
             name="sweep",
         )(nodes, coef, weight, *ghosts, full)
-        incoming = [passed_along(returned[p], "dom", offset_of(p)) for p in range(BLOCKS)]
+        incoming = []
+        for p, item in enumerate(returned):
+            incoming.append(passed_along(item, "dom", offset_of(p % BLOCKS)))
         if again:
             full, *outs = pl.pallas_call(
                 functools.partial(between_kernel, sub, lanes),
@@ -378,24 +405,26 @@
                 name="between",
             )(send, weight, *incoming, full)
 
-    _, *blocks = pl.pallas_call(
-        functools.partial(leave_kernel, sub, lanes, halves, spec_count),
-        out_shape=[full_shape] + [shape_of(row_count * halves, LANES)] * spec_count,
-        in_specs=[SM] * 2 + [VM] * (2 + BLOCKS),
-        out_specs=[VM] * (1 + spec_count),
-        input_output_aliases={3 + BLOCKS: 0},
-        scratch_shapes=[squares, stages],
-        cost_estimate=cost(2 * owned * row_count, 4 * moved),
-        compiler_params=limit(4),
-        name="leave",
-    )(place, send, weight, *incoming, full)
-    pieces = [blocks[0]] + [passed_along(blocks[d], "spec", d) for d in range(1, spec_count)]
+    pieces = []
+    for which, (start, size) in enumerate(groups):
+        full, *blocks = pl.pallas_call(
+            functools.partial(leave_kernel, sub, (start, size), lanes, halves, spec_count),
+            out_shape=[full_shape] + [shape_of(size * lanes * halves, LANES)] * spec_count,
+            in_specs=[SM] * 2 + [VM] * (2 + BLOCKS),
+            out_specs=[VM] * (1 + spec_count),
+            input_output_aliases={3 + BLOCKS: 0},
+            scratch_shapes=[squares, stages],
+            cost_estimate=cost(2 * owned * size * LANES, 3 * moved * size // sub),
+            compiler_params=limit(4),
+        )(place, send, weight, *incoming[which * BLOCKS : (which + 1) * BLOCKS], full)
+        pieces += [blocks[0]] + [passed_along(blocks[d], "spec", d) for d in range(1, spec_count)]
     return pl.pallas_call(
-        functools.partial(interact_kernel, halves, spec_count),
+        functools.partial(interact_kernel, row_count * halves, halves, spec_count, [s * lanes * halves for s, _ in groups]),
         out_shape=shape_of(bins, halves * LANES),
-        in_specs=[SM] * 4 + [VM] * spec_count,
-        out_specs=VM,
-        scratch_shapes=[pltpu.VMEM((bins * halves, LANES), jnp.float32)] * (2 + 2 * GROUPS),
+        in_specs=[SM] * 4 + [VM] * len(pieces),
+        out_specs=pl.BlockSpec(memory_space=pl.ANY),
+        scratch_shapes=[pltpu.VMEM((bins * halves, LANES), jnp.float32)] * (2 + 2 * GROUPS)
+        + [pltpu.VMEM((bins, halves * LANES), jnp.float32), pltpu.SemaphoreType.DMA((chunked(bins // 48, 4),))],
         cost_estimate=cost(16 * bins * halves * LANES, 8 * bins * halves * LANES),
         compiler_params=limit(12),
         name="interact",

time: 126 us -> 120 us (0.952)
  waiting for transfers between devices: 54 us -> 40.4 us
  starting transfers between devices: 23.5 us -> 29.8 us
    ppermute x19 -> x26, waiting for transfers between devices: 54 us -> 40.4 us  [passed_along(): lax.ppermute(value, axis, [(source, (source + steps) % count) for source...]
    ppermute x19 -> x26, starting transfers between devices: 23.5 us -> 29.8 us  [passed_along(): lax.ppermute(value, axis, [(source, (source + steps) % count) for source...]
    pallas_call x4 -> x5, Pallas kernels: 32.6 us -> 33.3 us  [the longest x2 22.5 us: on_device(): pl.pallas_call(functools.partial(sweep_kernel, sub, groups, lanes, shared...]
  transfers between devices with their start and end apart: 19 -> 26, of which waited for: 11 -> 14; matrix products, arithmetic and copies ran while one was open for 2% -> 2% of each run, Pallas kernels for 4% -> 8%
where the time goes in v4:
time: 120 us; the launch traced here: 119 us
  Pallas kernels  43.7 us (36%)
  waiting for transfers between devices  40.4 us (34%)
  starting transfers between devices  29.8 us (25%)
  local copies, waits for them, and re-layouts  2.88 us (2%)
  other arithmetic  2.42 us (2%)
    ppermute x26, waiting for transfers between devices, passed_along(): lax.ppermute(value, axis, [(source, (source + steps) % count) for source...  40.4 us
    ppermute x26, starting transfers between devices, passed_along(): lax.ppermute(value, axis, [(source, (source + steps) % count) for source...  29.8 us
    pallas_call x2, Pallas kernels, on_device(): pl.pallas_call(functools.partial(sweep_kernel, sub, groups, lanes, shared...  22.5 us
    pallas_call x1, Pallas kernels, on_device(): pl.pallas_call(functools.partial(interact_kernel, row_count * halves, hal...  6.72 us
    pallas_call x1, Pallas kernels, on_device(): pl.pallas_call(functools.partial(slope_kernel, sub, shared), out_shape=[s...  4.88 us
    pallas_call x2, Pallas kernels, on_device(): pl.pallas_call(functools.partial(leave_kernel, sub, (start, size), lanes,...  4.13 us
    pallas_call x1, Pallas kernels, on_device(): pl.pallas_call(functools.partial(between_kernel, sub, lanes), out_shape=[...  2.91 us
    unnamed x11, local copies, waits for them, and re-layouts  2.86 us
  transfers between devices with their start and end apart: 26, of which 14 were waited for; matrix products, arithmetic and copies ran while one was open for 2% of the time, Pallas kernels for 8%

profile of v4, /device:TPU:9, one launch (start us, length us, event | category | flops | bytes accessed | tf_op | source)
XLA Modules:
  0.0 119.5 jit_solution(13076712015656840162)
XLA Ops:
  2.0 2.6 %enter.1 = (f32[4608,128]{1,0:T(8,128)S(1)}, f32[324,128]{1,0:T(8,128)}, f32[324,128]{1,0:T(8,128)}, f32[324,128]{1,0:T(8,128)S(1)}, f32[324,128]{1,0:T(8,128)S(1)}) custom-call(s32[512]{0:T(512)S(1)} %multiply_bitcast_fusion.send, f32[324,1024]{1,0:T(8,128)S(1)} %copy-done), custom_call_target="tpu_custom_call" | custom-call | bytes 3145728 | tf_op jit(solution)/shard_map/enter/pallas_call | solution.py:355
  5.9 2.1 %collective-permute-start.1 = (f32[324,128]{1,0:T(8,128)}, f32[324,128]{1,0:T(8,128)S(1)}, u32[]{:S(2)}, u32[]{:S(2)}) collective-permute-start(f32[324,128]{1,0:T(8,128)} %get-tuple-element.43), channel_id=1, source_target_pairs={{0,4},{4,8},{8,12},{12,16},{16,20},{20,24},{24,28},{28,0},{1,5},{5... | collective-permute-start | bytes 497672 | tf_op jit(solution)/shard_map/ppermute | solution.py:34
  12.4 4.9 %slopes.1 = (f32[6144,128]{1,0:T(8,128)S(1)}, f32[3072,128]{1,0:T(8,128)S(1)}) custom-call(f32[2,3,2048]{2,1,0:T(4,128)S(1)} %copy.16.normals, f32[1,1024]{1,0:T(1,128)S(1)} %bitcast.4, f32[9,128]{1,0:T(8,128)S(1)} %pad_maximum_fusion.wave), custom_call_target="tpu_custom_call" | custom-call | flops 5242880 | bytes 4718592 | tf_op jit(solution)/shard_map/slopes/pallas_call | solution.py:366
  18.2 11.3 %sweep.2 = (f32[4608,128]{1,0:T(8,128)S(1)}, f32[324,128]{1,0:T(8,128)S(1)}, f32[324,128]{1,0:T(8,128)S(1)}, f32[324,128]{1,0:T(8,128)S(1)}, f32[324,128]{1,0:T(8,128)S(1)}) custom-call(s32[6144]{0:T(1024)S(1)} %reshape.51.conn, f32[6144,128]{1,0:T(8,128)S(1)} %get-tuple-element.41.coef, ...), custom_call_target="tpu_custom_call", output_to_operand_aliasing={{0}: (7, {})} | custom-call | flops 15925248 | bytes 12582912 | tf_op jit(solution)/shard_map/sweep/pallas_call | solution.py:381
  30.6 1.8 %collective-permute-start.5 = (f32[324,128]{1,0:T(8,128)S(1)}, f32[324,128]{1,0:T(8,128)S(1)}, u32[]{:S(2)}, u32[]{:S(2)}) collective-permute-start(f32[324,128]{1,0:T(8,128)S(1)} %get-tuple-element.48), channel_id=1, source_target_pairs={{0,28},{4,0},{8,4},{12,8},{16,12},{20,16},{24,20},{28,24},{1,29},{... | collective-permute-start | bytes 497672 | tf_op jit(solution)/shard_map/ppermute | solution.py:34
  32.7 2.1 %collective-permute-start.7 = (f32[324,128]{1,0:T(8,128)S(1)}, f32[324,128]{1,0:T(8,128)S(1)}, u32[]{:S(2)}, u32[]{:S(2)}) collective-permute-start(f32[324,128]{1,0:T(8,128)S(1)} %get-tuple-element.50), channel_id=1, source_target_pairs={{0,8},{4,12},{8,16},{12,20},{16,24},{20,28},{24,0},{28,4},{1,9},{5... | collective-permute-start | bytes 497672 | tf_op jit(solution)/shard_map/ppermute | solution.py:34
  34.8 4.8 %collective-permute-done.5.rest_1_ = f32[324,128]{1,0:T(8,128)S(1)} collective-permute-done((f32[324,128]{1,0:T(8,128)S(1)}, f32[324,128]{1,0:T(8,128)S(1)}, u32[]{:S(2)}, u32[]{:S(2)}) %collective-permute-start.5) | collective-permute-done | bytes 165920 | tf_op jit(solution)/shard_map/ppermute | solution.py:34
  39.6 3.5 %collective-permute-done.7.rest_3_ = f32[324,128]{1,0:T(8,128)S(1)} collective-permute-done((f32[324,128]{1,0:T(8,128)S(1)}, f32[324,128]{1,0:T(8,128)S(1)}, u32[]{:S(2)}, u32[]{:S(2)}) %collective-permute-start.7) | collective-permute-done | bytes 165920 | tf_op jit(solution)/shard_map/ppermute | solution.py:34
  43.1 2.9 %between.1 = (f32[4608,128]{1,0:T(8,128)S(1)}, f32[324,128]{1,0:T(8,128)S(1)}, f32[324,128]{1,0:T(8,128)S(1)}, f32[324,128]{1,0:T(8,128)S(1)}, f32[324,128]{1,0:T(8,128)S(1)}) custom-call(s32[512]{0:T(512)S(1)} %multiply_bitcast_fusion.send, f32[3072,128]{1,0:T(8,128)S(1)} %get-tuple-element.40.weight, ...), custom_call_target="tpu_custom_call", output_to_operand_aliasing={{0}: (6, {})} | custom-call | flops 663552 | bytes 6291456 | tf_op jit(solution)/shard_map/between/pallas_call | solution.py:396
  46.5 2.0 %collective-permute-start.11 = (f32[324,128]{1,0:T(8,128)S(1)}, f32[324,128]{1,0:T(8,128)S(1)}, u32[]{:S(2)}, u32[]{:S(2)}) collective-permute-start(f32[324,128]{1,0:T(8,128)S(1)} %get-tuple-element.55), channel_id=1, source_target_pairs={{0,24},{4,28},{8,0},{12,4},{16,8},{20,12},{24,16},{28,20},{1,25},{... | collective-permute-start | bytes 497672 | tf_op jit(solution)/shard_map/ppermute | solution.py:34
  48.5 2.3 %collective-permute-start.9 = (f32[324,128]{1,0:T(8,128)S(1)}, f32[324,128]{1,0:T(8,128)S(1)}, u32[]{:S(2)}, u32[]{:S(2)}) collective-permute-start(f32[324,128]{1,0:T(8,128)S(1)} %get-tuple-element.53), channel_id=1, source_target_pairs={{0,4},{4,8},{8,12},{12,16},{16,20},{20,24},{24,28},{28,0},{1,5},{5... | collective-permute-start | bytes 497672 | tf_op jit(solution)/shard_map/ppermute | solution.py:34
  50.7 1.9 %collective-permute-done.10.rest_2_ = f32[324,128]{1,0:T(8,128)S(1)} collective-permute-done((f32[324,128]{1,0:T(8,128)S(1)}, f32[324,128]{1,0:T(8,128)S(1)}, u32[]{:S(2)}, u32[]{:S(2)}) %collective-permute-start.10) | collective-permute-done | bytes 165920 | tf_op jit(solution)/shard_map/ppermute | solution.py:34
  52.7 4.2 %collective-permute-done.8.rest_0_ = f32[324,128]{1,0:T(8,128)S(1)} collective-permute-done((f32[324,128]{1,0:T(8,128)S(1)}, f32[324,128]{1,0:T(8,128)S(1)}, u32[]{:S(2)}, u32[]{:S(2)}) %collective-permute-start.8) | collective-permute-done | bytes 165920 | tf_op jit(solution)/shard_map/ppermute | solution.py:34
  58.0 11.2 %sweep.3 = (f32[4608,128]{1,0:T(8,128)S(1)}, f32[108,128]{1,0:T(8,128)S(1)}, f32[108,128]{1,0:T(8,128)S(1)}, f32[108,128]{1,0:T(8,128)S(1)}, f32[108,128]{1,0:T(...) custom-call(s32[6144]{0:T(1024)S(1)} %reshape.51.conn, ...), custom_call_target="tpu_custom_call", output_to_operand_aliasing={{0}: (7, {})} | custom-call | flops 15925248 | bytes 12582912 | tf_op jit(solution)/shard_map/sweep/pallas_call | solution.py:381
  69.2 2.1 %collective-permute-start.12 = (f32[108,128]{1,0:T(8,128)S(1)}, f32[108,128]{1,0:T(8,128)S(1)}, u32[]{:S(2)}, u32[]{:S(2)}) collective-permute-start(f32[108,128]{1,0:T(8,128)S(1)} %get-tuple-element.57), channel_id=1, source_target_pairs={{0,24},{4,28},{8,0},{12,4},{16,8},{20,12},{24,16},{28,20},{1,25},{... | collective-permute-start | bytes 165896 | tf_op jit(solution)/shard_map/ppermute | solution.py:34
  74.4 2.2 %collective-permute-start.19 = (f32[216,128]{1,0:T(8,128)S(1)}, f32[216,128]{1,0:T(8,128)S(1)}, u32[]{:S(2)}, u32[]{:S(2)}) collective-permute-start(f32[216,128]{1,0:T(8,128)S(1)} %get-tuple-element.66), channel_id=1, source_target_pairs={{0,24},{4,28},{8,0},{12,4},{16,8},{20,12},{24,16},{28,20},{1,25},{... | collective-permute-start | bytes 331784 | tf_op jit(solution)/shard_map/ppermute | solution.py:34
  78.8 2.0 %shard_map.91 = (f32[4608,128]{1,0:T(8,128)S(1)}, f32[216,128]{1,0:T(8,128)S(1)}, f32[216,128]{1,0:T(8,128)S(1)}, f32[216,128]{1,0:T(8,128)S(1)}, f32[216,128]{1,0:T(8,128)S(1)}) custom-call(s32[1]{0:T(128)} %bitcast.place, s32[512]{0:T(512)S(1)} %multiply_bitcast_fusion.send, ...), custom_call_target="tpu_custom_call", output_to_operand_aliasing={{0}: (7, {})} | custom-call | flops 262144 | bytes 1572864 | tf_op jit(solution)/shard_map/pallas_call | solution.py:410
  85.8 2.2 %shard_map.92 = (f32[4608,128]{1,0:T(8,128)S(1)}, f32[432,128]{1,0:T(8,128)S(1)}, f32[432,128]{1,0:T(8,128)S(1)}, f32[432,128]{1,0:T(8,128)S(1)}, f32[432,128]{1,0:T(8,128)S(1)}) custom-call(s32[1]{0:T(128)} %bitcast.place, s32[512]{0:T(512)S(1)} %multiply_bitcast_fusion.send, ...), custom_call_target="tpu_custom_call", output_to_operand_aliasing={{0}: (7, {})} | custom-call | flops 524288 | bytes 3145728 | tf_op jit(solution)/shard_map/pallas_call | solution.py:410
  89.3 2.5 %collective-permute-start.24 = (f32[432,128]{1,0:T(8,128)S(1)}, f32[432,128]{1,0:T(8,128)S(1)}, u32[]{:S(2)}, u32[]{:S(2)}) collective-permute-start(f32[432,128]{1,0:T(8,128)S(1)} %get-tuple-element.73), channel_id=1, source_target_pairs={{0,2},{1,3},{2,0},{3,1},{4,6},{5,7},{6,4},{7,5},{8,10},{9,11},{10,... | collective-permute-start | bytes 663560 | tf_op jit(solution)/shard_map/ppermute | solution.py:34
  91.9 11.4 %collective-permute-done.18.rest_3_ = f32[216,128]{1,0:T(8,128)S(1)} collective-permute-done((f32[216,128]{1,0:T(8,128)S(1)}, f32[216,128]{1,0:T(8,128)S(1)}, u32[]{:S(2)}, u32[]{:S(2)}) %collective-permute-start.18) | collective-permute-done | bytes 110624 | tf_op jit(solution)/shard_map/ppermute | solution.py:34
  103.2 2.3 %collective-permute-done.23.rest_5_ = f32[432,128]{1,0:T(8,128)S(1)} collective-permute-done((f32[432,128]{1,0:T(8,128)S(1)}, f32[432,128]{1,0:T(8,128)S(1)}, u32[]{:S(2)}, u32[]{:S(2)}) %collective-permute-start.23) | collective-permute-done | bytes 221216 | tf_op jit(solution)/shard_map/ppermute | solution.py:34
  105.6 4.7 %collective-permute-done.24.rest_6_ = f32[432,128]{1,0:T(8,128)S(1)} collective-permute-done((f32[432,128]{1,0:T(8,128)S(1)}, f32[432,128]{1,0:T(8,128)S(1)}, u32[]{:S(2)}, u32[]{:S(2)}) %collective-permute-start.24) | collective-permute-done | bytes 221216 | tf_op jit(solution)/shard_map/ppermute | solution.py:34
  110.3 2.4 %collective-permute-done.25.rest_7_ = f32[432,128]{1,0:T(8,128)S(1)} collective-permute-done((f32[432,128]{1,0:T(8,128)S(1)}, f32[432,128]{1,0:T(8,128)S(1)}, u32[]{:S(2)}, u32[]{:S(2)}) %collective-permute-start.25) | collective-permute-done | bytes 221216 | tf_op jit(solution)/shard_map/ppermute | solution.py:34
  112.7 6.7 %interact.1 = f32[1296,256]{1,0:T(8,128)} custom-call(s32[1]{0:T(128)} %bitcast.place, s32[1296]{0:T(1024)S(1)} %get-tuple-element.78.plus, s32[1296]{0:T(1024)S(1)} %get-tuple-element.77.minus, f32[1296]{0:T(1024)S(1)} %copy-done.1, f32[216,128]{1,0:T(8,128)S(1)} %get-tuple-element.62.rest_0_, f32[216,128]{1,0:T(8,128)S(1)} %collective-permute-done.16.rest_1_, ...), custom_call_target="tpu_custom_call" | custom-call | flops 5308416 | bytes 2654208 | tf_op jit(solution)/shard_map/interact/pallas_call | solution.py:421
  (56 shorter events, 23.2 us)
Async XLA Ops:
  4.6 12.6 %collective-permute-start = (f32[324,128]{1,0:T(8,128)}, f32[324,128]{1,0:T(8,128)S(1)}, u32[]{:S(2)}, u32[]{:S(2)}) collective-permute-start(f32[324,128]{1,0:T(8,128)} %get-tuple-element.42), channel_id=1, source_target_pairs={{0,8},{4,12},{8,16},{12,20},{16,24},{20,28},{24,0},{28,4},{1,9},{5... | collective-permute-start | bytes 497672 | tf_op jit(solution)/shard_map/ppermute | solution.py:34
  5.9 11.4 %collective-permute-start.1 = (f32[324,128]{1,0:T(8,128)}, f32[324,128]{1,0:T(8,128)S(1)}, u32[]{:S(2)}, u32[]{:S(2)}) collective-permute-start(f32[324,128]{1,0:T(8,128)} %get-tuple-element.43), channel_id=1, source_target_pairs={{0,4},{4,8},{8,12},{12,16},{16,20},{20,24},{24,28},{28,0},{1,5},{5... | collective-permute-start | bytes 497672 | tf_op jit(solution)/shard_map/ppermute | solution.py:34
  7.9 9.4 %collective-permute-start.2 = (f32[324,128]{1,0:T(8,128)S(1)}, f32[324,128]{1,0:T(8,128)S(1)}, u32[]{:S(2)}, u32[]{:S(2)}) collective-permute-start(f32[324,128]{1,0:T(8,128)S(1)} %get-tuple-element.44), channel_id=1, source_target_pairs={{0,28},{4,0},{8,4},{12,8},{16,12},{20,16},{24,20},{28,24},{1,29},{... | collective-permute-start | bytes 497672 | tf_op jit(solution)/shard_map/ppermute | solution.py:34
  7.9 10.3 %collective-permute-start.3 = (f32[324,128]{1,0:T(8,128)S(1)}, f32[324,128]{1,0:T(8,128)S(1)}, u32[]{:S(2)}, u32[]{:S(2)}) collective-permute-start(f32[324,128]{1,0:T(8,128)S(1)} %get-tuple-element.45), channel_id=1, source_target_pairs={{0,24},{4,28},{8,0},{12,4},{16,8},{20,12},{24,16},{28,20},{1,25},{... | collective-permute-start | bytes 497672 | tf_op jit(solution)/shard_map/ppermute | solution.py:34
  29.4 5.3 %collective-permute-start.4 = (f32[324,128]{1,0:T(8,128)S(1)}, f32[324,128]{1,0:T(8,128)S(1)}, u32[]{:S(2)}, u32[]{:S(2)}) collective-permute-start(f32[324,128]{1,0:T(8,128)S(1)} %get-tuple-element.47), channel_id=1, source_target_pairs={{0,24},{4,28},{8,0},{12,4},{16,8},{20,12},{24,16},{28,20},{1,25},{... | collective-permute-start | bytes 497672 | tf_op jit(solution)/shard_map/ppermute | solution.py:34
  30.6 8.9 %collective-permute-start.5 = (f32[324,128]{1,0:T(8,128)S(1)}, f32[324,128]{1,0:T(8,128)S(1)}, u32[]{:S(2)}, u32[]{:S(2)}) collective-permute-start(f32[324,128]{1,0:T(8,128)S(1)} %get-tuple-element.48), channel_id=1, source_target_pairs={{0,28},{4,0},{8,4},{12,8},{16,12},{20,16},{24,20},{28,24},{1,29},{... | collective-permute-start | bytes 497672 | tf_op jit(solution)/shard_map/ppermute | solution.py:34
  32.5 7.1 %collective-permute-start.6 = (f32[324,128]{1,0:T(8,128)S(1)}, f32[324,128]{1,0:T(8,128)S(1)}, u32[]{:S(2)}, u32[]{:S(2)}) collective-permute-start(f32[324,128]{1,0:T(8,128)S(1)} %get-tuple-element.49), channel_id=1, source_target_pairs={{0,4},{4,8},{8,12},{12,16},{16,20},{20,24},{24,28},{28,0},{1,5},{5... | collective-permute-start | bytes 497672 | tf_op jit(solution)/shard_map/ppermute | solution.py:34
  32.7 10.5 %collective-permute-start.7 = (f32[324,128]{1,0:T(8,128)S(1)}, f32[324,128]{1,0:T(8,128)S(1)}, u32[]{:S(2)}, u32[]{:S(2)}) collective-permute-start(f32[324,128]{1,0:T(8,128)S(1)} %get-tuple-element.50), channel_id=1, source_target_pairs={{0,8},{4,12},{8,16},{12,20},{16,24},{20,28},{24,0},{28,4},{1,9},{5... | collective-permute-start | bytes 497672 | tf_op jit(solution)/shard_map/ppermute | solution.py:34
  46.0 6.6 %collective-permute-start.10 = (f32[324,128]{1,0:T(8,128)S(1)}, f32[324,128]{1,0:T(8,128)S(1)}, u32[]{:S(2)}, u32[]{:S(2)}) collective-permute-start(f32[324,128]{1,0:T(8,128)S(1)} %get-tuple-element.54), channel_id=1, source_target_pairs={{0,28},{4,0},{8,4},{12,8},{16,12},{20,16},{24,20},{28,24},{1,29},{... | collective-permute-start | bytes 497672 | tf_op jit(solution)/shard_map/ppermute | solution.py:34
  46.5 6.2 %collective-permute-start.11 = (f32[324,128]{1,0:T(8,128)S(1)}, f32[324,128]{1,0:T(8,128)S(1)}, u32[]{:S(2)}, u32[]{:S(2)}) collective-permute-start(f32[324,128]{1,0:T(8,128)S(1)} %get-tuple-element.55), channel_id=1, source_target_pairs={{0,24},{4,28},{8,0},{12,4},{16,8},{20,12},{24,16},{28,20},{1,25},{... | collective-permute-start | bytes 497672 | tf_op jit(solution)/shard_map/ppermute | solution.py:34
  48.5 8.4 %collective-permute-start.8 = (f32[324,128]{1,0:T(8,128)S(1)}, f32[324,128]{1,0:T(8,128)S(1)}, u32[]{:S(2)}, u32[]{:S(2)}) collective-permute-start(f32[324,128]{1,0:T(8,128)S(1)} %get-tuple-element.52), channel_id=1, source_target_pairs={{0,8},{4,12},{8,16},{12,20},{16,24},{20,28},{24,0},{28,4},{1,9},{5... | collective-permute-start | bytes 497672 | tf_op jit(solution)/shard_map/ppermute | solution.py:34
  48.5 9.5 %collective-permute-start.9 = (f32[324,128]{1,0:T(8,128)S(1)}, f32[324,128]{1,0:T(8,128)S(1)}, u32[]{:S(2)}, u32[]{:S(2)}) collective-permute-start(f32[324,128]{1,0:T(8,128)S(1)} %get-tuple-element.53), channel_id=1, source_target_pairs={{0,4},{4,8},{8,12},{12,16},{16,20},{20,24},{24,28},{28,0},{1,5},{5... | collective-permute-start | bytes 497672 | tf_op jit(solution)/shard_map/ppermute | solution.py:34
  69.2 7.4 %collective-permute-start.12 = (f32[108,128]{1,0:T(8,128)S(1)}, f32[108,128]{1,0:T(8,128)S(1)}, u32[]{:S(2)}, u32[]{:S(2)}) collective-permute-start(f32[108,128]{1,0:T(8,128)S(1)} %get-tuple-element.57), channel_id=1, source_target_pairs={{0,24},{4,28},{8,0},{12,4},{16,8},{20,12},{24,16},{28,20},{1,25},{... | collective-permute-start | bytes 165896 | tf_op jit(solution)/shard_map/ppermute | solution.py:34
  71.3 6.8 %collective-permute-start.13 = (f32[108,128]{1,0:T(8,128)S(1)}, f32[108,128]{1,0:T(8,128)S(1)}, u32[]{:S(2)}, u32[]{:S(2)}) collective-permute-start(f32[108,128]{1,0:T(8,128)S(1)} %get-tuple-element.58), channel_id=1, source_target_pairs={{0,28},{4,0},{8,4},{12,8},{16,12},{20,16},{24,20},{28,24},{1,29},{... | collective-permute-start | bytes 165896 | tf_op jit(solution)/shard_map/ppermute | solution.py:34
  74.4 7.8 %collective-permute-start.19 = (f32[216,128]{1,0:T(8,128)S(1)}, f32[216,128]{1,0:T(8,128)S(1)}, u32[]{:S(2)}, u32[]{:S(2)}) collective-permute-start(f32[216,128]{1,0:T(8,128)S(1)} %get-tuple-element.66), channel_id=1, source_target_pairs={{0,24},{4,28},{8,0},{12,4},{16,8},{20,12},{24,16},{28,20},{1,25},{... | collective-permute-start | bytes 331784 | tf_op jit(solution)/shard_map/ppermute | solution.py:34
  76.6 7.4 %collective-permute-start.20 = (f32[216,128]{1,0:T(8,128)S(1)}, f32[216,128]{1,0:T(8,128)S(1)}, u32[]{:S(2)}, u32[]{:S(2)}) collective-permute-start(f32[216,128]{1,0:T(8,128)S(1)} %get-tuple-element.67), channel_id=1, source_target_pairs={{0,28},{4,0},{8,4},{12,8},{16,12},{20,16},{24,20},{28,24},{1,29},{... | collective-permute-start | bytes 331784 | tf_op jit(solution)/shard_map/ppermute | solution.py:34
  78.1 6.6 %collective-permute-start.21 = (f32[216,128]{1,0:T(8,128)S(1)}, f32[216,128]{1,0:T(8,128)S(1)}, u32[]{:S(2)}, u32[]{:S(2)}) collective-permute-start(f32[216,128]{1,0:T(8,128)S(1)} %get-tuple-element.68), channel_id=1, source_target_pairs={{0,4},{4,8},{8,12},{12,16},{16,20},{20,24},{24,28},{28,0},{1,5},{5... | collective-permute-start | bytes 331784 | tf_op jit(solution)/shard_map/ppermute | solution.py:34
  78.3 7.4 %collective-permute-start.22 = (f32[216,128]{1,0:T(8,128)S(1)}, f32[216,128]{1,0:T(8,128)S(1)}, u32[]{:S(2)}, u32[]{:S(2)}) collective-permute-start(f32[216,128]{1,0:T(8,128)S(1)} %get-tuple-element.69), channel_id=1, source_target_pairs={{0,8},{4,12},{8,16},{12,20},{16,24},{20,28},{24,0},{28,4},{1,9},{5... | collective-permute-start | bytes 331784 | tf_op jit(solution)/shard_map/ppermute | solution.py:34
  80.8 11.1 %collective-permute-start.16 = (f32[216,128]{1,0:T(8,128)S(1)}, f32[216,128]{1,0:T(8,128)S(1)}, u32[]{:S(2)}, u32[]{:S(2)}) collective-permute-start(f32[216,128]{1,0:T(8,128)S(1)} %get-tuple-element.63), channel_id=1, source_target_pairs={{0,1},{1,2},{2,3},{3,0},{4,5},{5,6},{6,7},{7,4},{8,9},{9,10},{10,1... | collective-permute-start | bytes 331784 | tf_op jit(solution)/shard_map/ppermute | solution.py:34
  82.1 9.7 %collective-permute-start.17 = (f32[216,128]{1,0:T(8,128)S(1)}, f32[216,128]{1,0:T(8,128)S(1)}, u32[]{:S(2)}, u32[]{:S(2)}) collective-permute-start(f32[216,128]{1,0:T(8,128)S(1)} %get-tuple-element.64), channel_id=1, source_target_pairs={{0,2},{1,3},{2,0},{3,1},{4,6},{5,7},{6,4},{7,5},{8,10},{9,11},{10,... | collective-permute-start | bytes 331784 | tf_op jit(solution)/shard_map/ppermute | solution.py:34
  84.0 19.2 %collective-permute-start.18 = (f32[216,128]{1,0:T(8,128)S(1)}, f32[216,128]{1,0:T(8,128)S(1)}, u32[]{:S(2)}, u32[]{:S(2)}) collective-permute-start(f32[216,128]{1,0:T(8,128)S(1)} %get-tuple-element.65), channel_id=1, source_target_pairs={{0,3},{1,0},{2,1},{3,2},{4,7},{5,4},{6,5},{7,6},{8,11},{9,8},{10,9... | collective-permute-start | bytes 331784 | tf_op jit(solution)/shard_map/ppermute | solution.py:34
  88.0 17.6 %collective-permute-start.23 = (f32[432,128]{1,0:T(8,128)S(1)}, f32[432,128]{1,0:T(8,128)S(1)}, u32[]{:S(2)}, u32[]{:S(2)}) collective-permute-start(f32[432,128]{1,0:T(8,128)S(1)} %get-tuple-element.72), channel_id=1, source_target_pairs={{0,1},{1,2},{2,3},{3,0},{4,5},{5,6},{6,7},{7,4},{8,9},{9,10},{10,1... | collective-permute-start | bytes 663560 | tf_op jit(solution)/shard_map/ppermute | solution.py:34
  89.3 21.0 %collective-permute-start.24 = (f32[432,128]{1,0:T(8,128)S(1)}, f32[432,128]{1,0:T(8,128)S(1)}, u32[]{:S(2)}, u32[]{:S(2)}) collective-permute-start(f32[432,128]{1,0:T(8,128)S(1)} %get-tuple-element.73), channel_id=1, source_target_pairs={{0,2},{1,3},{2,0},{3,1},{4,6},{5,7},{6,4},{7,5},{8,10},{9,11},{10,... | collective-permute-start | bytes 663560 | tf_op jit(solution)/shard_map/ppermute | solution.py:34
  91.8 20.9 %collective-permute-start.25 = (f32[432,128]{1,0:T(8,128)S(1)}, f32[432,128]{1,0:T(8,128)S(1)}, u32[]{:S(2)}, u32[]{:S(2)}) collective-permute-start(f32[432,128]{1,0:T(8,128)S(1)} %get-tuple-element.74), channel_id=1, source_target_pairs={{0,3},{1,0},{2,1},{3,2},{4,7},{5,4},{6,5},{7,6},{8,11},{9,8},{10,9... | collective-permute-start | bytes 663560 | tf_op jit(solution)/shard_map/ppermute | solution.py:34
  (7 other events, 66.0 us)

commit v5 on v4

--- a/solution.py
+++ b/solution.py
@@ -45,15 +45,16 @@
             block[part * lanes : (part + 1) * lanes, column * LANES : (column + 1) * LANES] = tile[:lanes]
 
 
-def block_to_rows(sub, lanes, block, square, rows, first):
+def block_to_rows(sub, lanes, block, square, rows, first, start=0):
     for column in range(block.shape[1] // LANES):
-        for part in range(sub):
+        for part in range(block.shape[0] // lanes):
             slot = square.at[(column * sub + part) % square.shape[0]]
             slot[:lanes, :] = block[part * lanes : (part + 1) * lanes, column * LANES : (column + 1) * LANES]
-            rows[pl.ds(first + column * LANES * sub + part, LANES, stride=sub), :] = slot[...].T
-
-
-def pack_rows(sub, lanes, send, energy, stages, outs):
+            rows[pl.ds(first + column * LANES * sub + start + part, LANES, stride=sub), :] = slot[...].T
+
+
+def pack_rows(parts, lanes, send, full, stages, outs):
+    start, size = parts
     slots = outs[0].shape[1]
     unroll = chunked(slots, 32)
     for position in range(BLOCKS):
@@ -64,16 +65,17 @@
             first = k * unroll
             listed = send.at[pl.ds((BLOCKS - 1 - position) * slots + first, unroll)]
             for u in range(unroll):
-                stage[pl.ds((first + u) * sub, sub), :] = energy[pl.ds(listed[u], sub), :]
-
-        rows_to_block(sub, lanes, stage, outs[position])
+                stage[pl.ds((first + u) * size, size), :] = full[pl.ds(listed[u] + start, size), :]
+
+    for position in range(BLOCKS):
+        rows_to_block(size, lanes, stages.at[position], outs[position])
 
 
 def enter_kernel(sub, lanes, send, spectrum, full, *rest):
     outs, square, stages = rest[:BLOCKS], rest[BLOCKS], rest[BLOCKS + 1]
     square[...] = jnp.zeros_like(square)
     block_to_rows(sub, lanes, spectrum, square, full, 0)
-    pack_rows(sub, lanes, send, full, stages, outs)
+    pack_rows((0, sub), lanes, send, full, stages, outs)
 
 
 def clear(items):
@@ -136,8 +138,9 @@
     return result
 
 
-def sweep_kernel(sub, groups, lanes, shared, own_rows, conn, coef, weight, *rest):
-    ghosts, full, rest = rest[:BLOCKS], rest[BLOCKS + 1], rest[BLOCKS + 2 :]
+def sweep_kernel(sub, inner, groups, lanes, shared, own_rows, conn, coef, weight, *rest):
+    ghosts, rest = rest[: BLOCKS * len(inner)], rest[BLOCKS * len(inner) + 1 :]
+    full, rest = rest[0], rest[1:]
     returned, rest = rest[: BLOCKS * len(groups)], rest[BLOCKS * len(groups) :]
     square, stages, sums = rest[0], rest[1], rest[2:]
     clear(sums)
@@ -145,8 +148,10 @@
     elements = conn.shape[0] // 3
     parts = 1 if shared else sub
     square[...] = jnp.zeros_like(square)
-    for position in range(BLOCKS):
-        block_to_rows(sub, lanes, ghosts[position], square, full, own_rows + position * ghost_rows)
+    for which, (start, _) in enumerate(inner):
+        for position in range(BLOCKS):
+            block = ghosts[which * BLOCKS + position]
+            block_to_rows(sub, lanes, block, square, full, own_rows + position * ghost_rows, start)
 
     share = elements // GROUPS
     unroll = chunked(share, 16)
@@ -223,11 +228,11 @@
                 full[row, :] = item
 
 
-def between_kernel(sub, lanes, send, weight, *rest):
+def between_kernel(parts, lanes, send, weight, *rest):
     incoming, rest = rest[:BLOCKS], rest[BLOCKS + 1 :]
     full, outs, square, stages = rest[0], rest[1 : 1 + BLOCKS], rest[1 + BLOCKS], rest[2 + BLOCKS]
-    add_returned((0, sub), lanes, send, weight, incoming, square, stages, full)
-    pack_rows(sub, lanes, send, full, stages, outs)
+    add_returned(parts, lanes, send, weight, incoming, square, stages, full)
+    pack_rows(parts, lanes, send, full, stages, outs)
 
 
 def leave_kernel(sub, parts, lanes, halves, count, place, send, weight, *rest):
@@ -374,16 +379,18 @@
         name="slopes",
     )(normals, step_weight.reshape(1, owned), wave)
 
+    groups = whole if sub == 1 else ((0, 1), (1, sub - 1))
+    inner = whole
     for sweep_index in range(STEPS):
-        again = sweep_index < STEPS - 1
-        groups = whole if again or sub == 1 else ((0, 1), (1, sub - 1))
-        ghosts = [passed_along(outs[p], "dom", -offset_of(p)) for p in range(BLOCKS)]
+        ghosts = []
+        for p, item in enumerate(outs):
+            ghosts.append(passed_along(item, "dom", -offset_of(p % BLOCKS)))
         full, *returned = pl.pallas_call(
-            functools.partial(sweep_kernel, sub, groups, lanes, shared, own_rows),
+            functools.partial(sweep_kernel, sub, inner, groups, lanes, shared, own_rows),
             out_shape=[full_shape] + blocks_of(groups),
-            in_specs=[SM] + [VM] * (3 + BLOCKS),
+            in_specs=[SM] + [VM] * (3 + len(ghosts)),
             out_specs=[VM] * (1 + BLOCKS * len(groups)),
-            input_output_aliases={3 + BLOCKS: 0},
+            input_output_aliases={3 + len(ghosts): 0},
             scratch_shapes=[squares, stages] + sums,
             cost_estimate=cost(elements * 24 * row_count, 4 * LANES * (3 * elements + 4 * rows)),
             compiler_params=limit(20),
@@ -392,18 +399,20 @@
         incoming = []
         for p, item in enumerate(returned):
             incoming.append(passed_along(item, "dom", offset_of(p % BLOCKS)))
-        if again:
-            full, *outs = pl.pallas_call(
-                functools.partial(between_kernel, sub, lanes),
-                out_shape=[full_shape] + block_shapes,
-                in_specs=[SM] + [VM] * (2 + BLOCKS),
-                out_specs=[VM] * (1 + BLOCKS),
-                input_output_aliases={2 + BLOCKS: 0},
-                scratch_shapes=[squares, stages],
-                cost_estimate=cost(2 * owned * row_count, 4 * moved),
-                compiler_params=limit(4),
-                name="between",
-            )(send, weight, *incoming, full)
+        if sweep_index < STEPS - 1:
+            outs, inner = [], groups
+            for which, parts in enumerate(groups):
+                full, *more = pl.pallas_call(
+                    functools.partial(between_kernel, parts, lanes),
+                    out_shape=[full_shape] + blocks_of((parts,)),
+                    in_specs=[SM] + [VM] * (2 + BLOCKS),
+                    out_specs=[VM] * (1 + BLOCKS),
+                    input_output_aliases={2 + BLOCKS: 0},
+                    scratch_shapes=[squares, stages],
+                    cost_estimate=cost(2 * owned * parts[1] * LANES, 4 * moved * parts[1] // sub),
+                    compiler_params=limit(4),
+                )(send, weight, *incoming[which * BLOCKS : (which + 1) * BLOCKS], full)
+                outs += more
 
     pieces = []
     for which, (start, size) in enumerate(groups):

time: 120 us -> 124 us (1.033)
  starting transfers between devices: 29.8 us -> 40.7 us
  waiting for transfers between devices: 40.4 us -> 32.2 us
  Pallas kernels: 43.7 us -> 45.5 us
    ppermute x26 -> x34, starting transfers between devices: 29.8 us -> 40.7 us  [passed_along(): lax.ppermute(value, axis, [(source, (source + steps) % count) for source...]
    ppermute x26 -> x34, waiting for transfers between devices: 40.4 us -> 32.2 us  [passed_along(): lax.ppermute(value, axis, [(source, (source + steps) % count) for source...]
    pallas_call x3 -> x4, Pallas kernels: 25.4 us -> 27.4 us  [the longest x2 22.5 us: on_device(): pl.pallas_call(functools.partial(sweep_kernel, sub, inner, groups, lanes,...]
  transfers between devices with their start and end apart: 26 -> 34, of which waited for: 14 -> 10; matrix products, arithmetic and copies ran while one was open for 2% -> 2% of each run, Pallas kernels for 8% -> 11%
where the time goes in v5:
time: 124 us
  Pallas kernels  45.5 us (37%)
  starting transfers between devices  40.7 us (33%)
  waiting for transfers between devices  32.2 us (26%)
  local copies, waits for them, and re-layouts  2.88 us (2%)
  other arithmetic  2.42 us (2%)
    ppermute x34, starting transfers between devices, passed_along(): lax.ppermute(value, axis, [(source, (source + steps) % count) for source...  40.7 us
    ppermute x34, waiting for transfers between devices, passed_along(): lax.ppermute(value, axis, [(source, (source + steps) % count) for source...  32.2 us
    pallas_call x2, Pallas kernels, on_device(): pl.pallas_call(functools.partial(sweep_kernel, sub, inner, groups, lanes,...  22.5 us
    pallas_call x1, Pallas kernels, on_device(): pl.pallas_call(functools.partial(interact_kernel, row_count * halves, hal...  6.72 us
    pallas_call x2, Pallas kernels, on_device(): pl.pallas_call(functools.partial(between_kernel, parts, lanes), out_shape...  4.91 us
    pallas_call x1, Pallas kernels, on_device(): pl.pallas_call(functools.partial(slope_kernel, sub, shared), out_shape=[s...  4.88 us
    pallas_call x2, Pallas kernels, on_device(): pl.pallas_call(functools.partial(leave_kernel, sub, (start, size), lanes,...  4.13 us
    unnamed x11, local copies, waits for them, and re-layouts  2.86 us
  transfers between devices with their start and end apart: 34, of which 10 were waited for; matrix products, arithmetic and copies ran while one was open for 2% of the time, Pallas kernels for 11%

profile of v5, /device:TPU:9, one launch (start us, length us, event | category | flops | bytes accessed | tf_op | source)
XLA Modules:
  0.0 123.9 jit_solution(10949388180186458502)
XLA Ops:
  2.0 2.4 %enter.1 = (f32[4608,128]{1,0:T(8,128)S(1)}, f32[324,128]{1,0:T(8,128)}, f32[324,128]{1,0:T(8,128)}, f32[324,128]{1,0:T(8,128)S(1)}, f32[324,128]{1,0:T(8,128)S(1)}) custom-call(s32[512]{0:T(512)S(1)} %multiply_bitcast_fusion.send, f32[324,1024]{1,0:T(8,128)S(1)} %copy-done), custom_call_target="tpu_custom_call" | custom-call | bytes 3145728 | tf_op jit(solution)/shard_map/enter/pallas_call | solution.py:360
  5.6 2.1 %collective-permute-start.1 = (f32[324,128]{1,0:T(8,128)}, f32[324,128]{1,0:T(8,128)S(1)}, u32[]{:S(2)}, u32[]{:S(2)}) collective-permute-start(f32[324,128]{1,0:T(8,128)} %get-tuple-element.52), channel_id=1, source_target_pairs={{0,4},{4,8},{8,12},{12,16},{16,20},{20,24},{24,28},{28,0},{1,5},{5... | collective-permute-start | bytes 497672 | tf_op jit(solution)/shard_map/ppermute | solution.py:34
  12.1 4.9 %slopes.1 = (f32[6144,128]{1,0:T(8,128)S(1)}, f32[3072,128]{1,0:T(8,128)S(1)}) custom-call(f32[2,3,2048]{2,1,0:T(4,128)S(1)} %copy.17.normals, f32[1,1024]{1,0:T(1,128)S(1)} %bitcast.4, f32[9,128]{1,0:T(8,128)S(1)} %pad_maximum_fusion.wave), custom_call_target="tpu_custom_call" | custom-call | flops 5242880 | bytes 4718592 | tf_op jit(solution)/shard_map/slopes/pallas_call | solution.py:371
  18.0 11.2 %sweep.2 = (f32[4608,128]{1,0:T(8,128)S(1)}, f32[108,128]{1,0:T(8,128)S(1)}, f32[108,128]{1,0:T(8,128)S(1)}, f32[108,128]{1,0:T(8,128)S(1)}, f32[108,128]{1,0:T(...) custom-call(s32[6144]{0:T(1024)S(1)} %reshape.51.conn, ...), custom_call_target="tpu_custom_call", output_to_operand_aliasing={{0}: (7, {})} | custom-call | flops 15925248 | bytes 12582912 | tf_op jit(solution)/shard_map/sweep/pallas_call | solution.py:388
  32.4 2.1 %collective-permute-start.12 = (f32[216,128]{1,0:T(8,128)S(1)}, f32[216,128]{1,0:T(8,128)S(1)}, u32[]{:S(2)}, u32[]{:S(2)}) collective-permute-start(f32[216,128]{1,0:T(8,128)S(1)} %get-tuple-element.65), channel_id=1, source_target_pairs={{0,24},{4,28},{8,0},{12,4},{16,8},{20,12},{24,16},{28,20},{1,25},{... | collective-permute-start | bytes 331784 | tf_op jit(solution)/shard_map/ppermute | solution.py:34
  34.5 2.9 %collective-permute-start.14 = (f32[216,128]{1,0:T(8,128)S(1)}, f32[216,128]{1,0:T(8,128)S(1)}, u32[]{:S(2)}, u32[]{:S(2)}) collective-permute-start(f32[216,128]{1,0:T(8,128)S(1)} %get-tuple-element.67), channel_id=1, source_target_pairs={{0,4},{4,8},{8,12},{12,16},{16,20},{20,24},{24,28},{28,0},{1,5},{5... | collective-permute-start | bytes 331784 | tf_op jit(solution)/shard_map/ppermute | solution.py:34
  39.0 5.6 %collective-permute-done.7.rest_3_ = f32[108,128]{1,0:T(8,128)S(1)} collective-permute-done((f32[108,128]{1,0:T(8,128)S(1)}, f32[108,128]{1,0:T(8,128)S(1)}, u32[]{:S(2)}, u32[]{:S(2)}) %collective-permute-start.7) | collective-permute-done | bytes 55328 | tf_op jit(solution)/shard_map/ppermute | solution.py:34
  44.6 2.4 %shard_map.91 = (f32[4608,128]{1,0:T(8,128)S(1)}, f32[108,128]{1,0:T(8,128)S(1)}, f32[108,128]{1,0:T(8,128)S(1)}, f32[108,128]{1,0:T(8,128)S(1)}, f32[108,128]{1,0:T(8,128)S(1)}) custom-call(s32[512]{0:T(512)S(1)} %multiply_bitcast_fusion.send, f32[3072,128]{1,0:T(8,128)S(1)} %get-tuple-element.49.weight, ...), custom_call_target="tpu_custom_call", output_to_operand_aliasing={{0}: (6, {})} | custom-call | flops 262144 | bytes 2097152 | tf_op jit(solution)/shard_map/pallas_call | solution.py:405
  49.0 2.5 %shard_map.92 = (f32[4608,128]{1,0:T(8,128)S(1)}, f32[216,128]{1,0:T(8,128)S(1)}, f32[216,128]{1,0:T(8,128)S(1)}, f32[216,128]{1,0:T(8,128)S(1)}, f32[216,128]{1,0:T(8,128)S(1)}) custom-call(s32[512]{0:T(512)S(1)} %multiply_bitcast_fusion.send, f32[3072,128]{1,0:T(8,128)S(1)} %get-tuple-element.49.weight, ...), custom_call_target="tpu_custom_call", output_to_operand_aliasing={{0}: (6, {})} | custom-call | flops 524288 | bytes 4194304 | tf_op jit(solution)/shard_map/pallas_call | solution.py:405
  52.5 2.5 %collective-permute-start.17 = (f32[216,128]{1,0:T(8,128)S(1)}, f32[216,128]{1,0:T(8,128)S(1)}, u32[]{:S(2)}, u32[]{:S(2)}) collective-permute-start(f32[216,128]{1,0:T(8,128)S(1)} %get-tuple-element.71), channel_id=1, source_target_pairs={{0,4},{4,8},{8,12},{12,16},{16,20},{20,24},{24,28},{28,0},{1,5},{5... | collective-permute-start | bytes 331784 | tf_op jit(solution)/shard_map/ppermute | solution.py:34
  55.0 2.0 %collective-permute-start.19 = (f32[216,128]{1,0:T(8,128)S(1)}, f32[216,128]{1,0:T(8,128)S(1)}, u32[]{:S(2)}, u32[]{:S(2)}) collective-permute-start(f32[216,128]{1,0:T(8,128)S(1)} %get-tuple-element.73), channel_id=1, source_target_pairs={{0,24},{4,28},{8,0},{12,4},{16,8},{20,12},{24,16},{28,20},{1,25},{... | collective-permute-start | bytes 331784 | tf_op jit(solution)/shard_map/ppermute | solution.py:34
  57.0 2.0 %collective-permute-start.9 = (f32[108,128]{1,0:T(8,128)S(1)}, f32[108,128]{1,0:T(8,128)S(1)}, u32[]{:S(2)}, u32[]{:S(2)}) collective-permute-start(f32[108,128]{1,0:T(8,128)S(1)} %get-tuple-element.62), channel_id=1, source_target_pairs={{0,4},{4,8},{8,12},{12,16},{16,20},{20,24},{24,28},{28,0},{1,5},{5... | collective-permute-start | bytes 165896 | tf_op jit(solution)/shard_map/ppermute | solution.py:34
  59.0 2.1 %collective-permute-done.9.rest_1_ = f32[108,128]{1,0:T(8,128)S(1)} collective-permute-done((f32[108,128]{1,0:T(8,128)S(1)}, f32[108,128]{1,0:T(8,128)S(1)}, u32[]{:S(2)}, u32[]{:S(2)}) %collective-permute-start.9) | collective-permute-done | bytes 55328 | tf_op jit(solution)/shard_map/ppermute | solution.py:34
  62.5 11.3 %sweep.3 = (f32[4608,128]{1,0:T(8,128)S(1)}, f32[108,128]{1,0:T(8,128)S(1)}, f32[108,128]{1,0:T(8,128)S(1)}, f32[108,128]{1,0:T(8,128)S(1)}, f32[108,128]{1,0:T(...) custom-call(s32[6144]{0:T(1024)S(1)} %reshape.51.conn, ...), custom_call_target="tpu_custom_call", output_to_operand_aliasing={{0}: (11, {})} | custom-call | flops 15925248 | bytes 12582912 | tf_op jit(solution)/shard_map/sweep/pallas_call | solution.py:388
  74.5 2.5 %collective-permute-start.21 = (f32[108,128]{1,0:T(8,128)S(1)}, f32[108,128]{1,0:T(8,128)S(1)}, u32[]{:S(2)}, u32[]{:S(2)}) collective-permute-start(f32[108,128]{1,0:T(8,128)S(1)} %get-tuple-element.76), channel_id=1, source_target_pairs={{0,28},{4,0},{8,4},{12,8},{16,12},{20,16},{24,20},{28,24},{1,29},{... | collective-permute-start | bytes 165896 | tf_op jit(solution)/shard_map/ppermute | solution.py:34
  77.2 1.9 %collective-permute-start.23 = (f32[108,128]{1,0:T(8,128)S(1)}, f32[108,128]{1,0:T(8,128)S(1)}, u32[]{:S(2)}, u32[]{:S(2)}) collective-permute-start(f32[108,128]{1,0:T(8,128)S(1)} %get-tuple-element.78), channel_id=1, source_target_pairs={{0,8},{4,12},{8,16},{12,20},{16,24},{20,28},{24,0},{28,4},{1,9},{5... | collective-permute-start | bytes 165896 | tf_op jit(solution)/shard_map/ppermute | solution.py:34
  83.2 2.0 %shard_map.93 = (f32[4608,128]{1,0:T(8,128)S(1)}, f32[216,128]{1,0:T(8,128)S(1)}, f32[216,128]{1,0:T(8,128)S(1)}, f32[216,128]{1,0:T(8,128)S(1)}, f32[216,128]{1,0:T(8,128)S(1)}) custom-call(s32[1]{0:T(128)} %bitcast.place, s32[512]{0:T(512)S(1)} %multiply_bitcast_fusion.send, ...), custom_call_target="tpu_custom_call", output_to_operand_aliasing={{0}: (7, {})} | custom-call | flops 262144 | bytes 1572864 | tf_op jit(solution)/shard_map/pallas_call | solution.py:419
  89.3 2.2 %shard_map.94 = (f32[4608,128]{1,0:T(8,128)S(1)}, f32[432,128]{1,0:T(8,128)S(1)}, f32[432,128]{1,0:T(8,128)S(1)}, f32[432,128]{1,0:T(8,128)S(1)}, f32[432,128]{1,0:T(8,128)S(1)}) custom-call(s32[1]{0:T(128)} %bitcast.place, s32[512]{0:T(512)S(1)} %multiply_bitcast_fusion.send, ...), custom_call_target="tpu_custom_call", output_to_operand_aliasing={{0}: (7, {})} | custom-call | flops 524288 | bytes 3145728 | tf_op jit(solution)/shard_map/pallas_call | solution.py:419
  92.9 1.9 %collective-permute-start.32 = (f32[432,128]{1,0:T(8,128)S(1)}, f32[432,128]{1,0:T(8,128)S(1)}, u32[]{:S(2)}, u32[]{:S(2)}) collective-permute-start(f32[432,128]{1,0:T(8,128)S(1)} %get-tuple-element.91), channel_id=1, source_target_pairs={{0,2},{1,3},{2,0},{3,1},{4,6},{5,7},{6,4},{7,5},{8,10},{9,11},{10,... | collective-permute-start | bytes 663560 | tf_op jit(solution)/shard_map/ppermute | solution.py:34
  96.2 11.6 %collective-permute-done.26.rest_3_ = f32[216,128]{1,0:T(8,128)S(1)} collective-permute-done((f32[216,128]{1,0:T(8,128)S(1)}, f32[216,128]{1,0:T(8,128)S(1)}, u32[]{:S(2)}, u32[]{:S(2)}) %collective-permute-start.26) | collective-permute-done | bytes 110624 | tf_op jit(solution)/shard_map/ppermute | solution.py:34
  107.7 2.7 %collective-permute-done.31.rest_5_ = f32[432,128]{1,0:T(8,128)S(1)} collective-permute-done((f32[432,128]{1,0:T(8,128)S(1)}, f32[432,128]{1,0:T(8,128)S(1)}, u32[]{:S(2)}, u32[]{:S(2)}) %collective-permute-start.31) | collective-permute-done | bytes 221216 | tf_op jit(solution)/shard_map/ppermute | solution.py:34
  110.4 4.7 %collective-permute-done.32.rest_6_ = f32[432,128]{1,0:T(8,128)S(1)} collective-permute-done((f32[432,128]{1,0:T(8,128)S(1)}, f32[432,128]{1,0:T(8,128)S(1)}, u32[]{:S(2)}, u32[]{:S(2)}) %collective-permute-start.32) | collective-permute-done | bytes 221216 | tf_op jit(solution)/shard_map/ppermute | solution.py:34
  115.1 2.1 %collective-permute-done.33.rest_7_ = f32[432,128]{1,0:T(8,128)S(1)} collective-permute-done((f32[432,128]{1,0:T(8,128)S(1)}, f32[432,128]{1,0:T(8,128)S(1)}, u32[]{:S(2)}, u32[]{:S(2)}) %collective-permute-start.33) | collective-permute-done | bytes 221216 | tf_op jit(solution)/shard_map/ppermute | solution.py:34
  117.2 6.7 %interact.1 = f32[1296,256]{1,0:T(8,128)} custom-call(s32[1]{0:T(128)} %bitcast.place, s32[1296]{0:T(1024)S(1)} %get-tuple-element.96.plus, s32[1296]{0:T(1024)S(1)} %get-tuple-element.95.minus, f32[1296]{0:T(1024)S(1)} %copy-done.1, f32[216,128]{1,0:T(8,128)S(1)} %get-tuple-element.80.rest_0_, f32[216,128]{1,0:T(8,128)S(1)} %collective-permute-done.24.rest_1_, ...), custom_call_target="tpu_custom_call" | custom-call | flops 5308416 | bytes 2654208 | tf_op jit(solution)/shard_map/interact/pallas_call | solution.py:430
  (73 shorter events, 29.7 us)
Async XLA Ops:
  4.4 12.6 %collective-permute-start = (f32[324,128]{1,0:T(8,128)}, f32[324,128]{1,0:T(8,128)S(1)}, u32[]{:S(2)}, u32[]{:S(2)}) collective-permute-start(f32[324,128]{1,0:T(8,128)} %get-tuple-element.51), channel_id=1, source_target_pairs={{0,8},{4,12},{8,16},{12,20},{16,24},{20,28},{24,0},{28,4},{1,9},{5... | collective-permute-start | bytes 497672 | tf_op jit(solution)/shard_map/ppermute | solution.py:34
  5.6 11.4 %collective-permute-start.1 = (f32[324,128]{1,0:T(8,128)}, f32[324,128]{1,0:T(8,128)S(1)}, u32[]{:S(2)}, u32[]{:S(2)}) collective-permute-start(f32[324,128]{1,0:T(8,128)} %get-tuple-element.52), channel_id=1, source_target_pairs={{0,4},{4,8},{8,12},{12,16},{16,20},{20,24},{24,28},{28,0},{1,5},{5... | collective-permute-start | bytes 497672 | tf_op jit(solution)/shard_map/ppermute | solution.py:34
  7.7 9.4 %collective-permute-start.2 = (f32[324,128]{1,0:T(8,128)S(1)}, f32[324,128]{1,0:T(8,128)S(1)}, u32[]{:S(2)}, u32[]{:S(2)}) collective-permute-start(f32[324,128]{1,0:T(8,128)S(1)} %get-tuple-element.53), channel_id=1, source_target_pairs={{0,28},{4,0},{8,4},{12,8},{16,12},{20,16},{24,20},{28,24},{1,29},{... | collective-permute-start | bytes 497672 | tf_op jit(solution)/shard_map/ppermute | solution.py:34
  7.7 10.3 %collective-permute-start.3 = (f32[324,128]{1,0:T(8,128)S(1)}, f32[324,128]{1,0:T(8,128)S(1)}, u32[]{:S(2)}, u32[]{:S(2)}) collective-permute-start(f32[324,128]{1,0:T(8,128)S(1)} %get-tuple-element.54), channel_id=1, source_target_pairs={{0,24},{4,28},{8,0},{12,4},{16,8},{20,12},{24,16},{28,20},{1,25},{... | collective-permute-start | bytes 497672 | tf_op jit(solution)/shard_map/ppermute | solution.py:34
  32.4 15.1 %collective-permute-start.12 = (f32[216,128]{1,0:T(8,128)S(1)}, f32[216,128]{1,0:T(8,128)S(1)}, u32[]{:S(2)}, u32[]{:S(2)}) collective-permute-start(f32[216,128]{1,0:T(8,128)S(1)} %get-tuple-element.65), channel_id=1, source_target_pairs={{0,24},{4,28},{8,0},{12,4},{16,8},{20,12},{24,16},{28,20},{1,25},{... | collective-permute-start | bytes 331784 | tf_op jit(solution)/shard_map/ppermute | solution.py:34
  34.4 14.0 %collective-permute-start.13 = (f32[216,128]{1,0:T(8,128)S(1)}, f32[216,128]{1,0:T(8,128)S(1)}, u32[]{:S(2)}, u32[]{:S(2)}) collective-permute-start(f32[216,128]{1,0:T(8,128)S(1)} %get-tuple-element.66), channel_id=1, source_target_pairs={{0,28},{4,0},{8,4},{12,8},{16,12},{20,16},{24,20},{28,24},{1,29},{... | collective-permute-start | bytes 331784 | tf_op jit(solution)/shard_map/ppermute | solution.py:34
  34.5 14.5 %collective-permute-start.14 = (f32[216,128]{1,0:T(8,128)S(1)}, f32[216,128]{1,0:T(8,128)S(1)}, u32[]{:S(2)}, u32[]{:S(2)}) collective-permute-start(f32[216,128]{1,0:T(8,128)S(1)} %get-tuple-element.67), channel_id=1, source_target_pairs={{0,4},{4,8},{8,12},{12,16},{16,20},{20,24},{24,28},{28,0},{1,5},{5... | collective-permute-start | bytes 331784 | tf_op jit(solution)/shard_map/ppermute | solution.py:34
  37.4 11.6 %collective-permute-start.15 = (f32[216,128]{1,0:T(8,128)S(1)}, f32[216,128]{1,0:T(8,128)S(1)}, u32[]{:S(2)}, u32[]{:S(2)}) collective-permute-start(f32[216,128]{1,0:T(8,128)S(1)} %get-tuple-element.68), channel_id=1, source_target_pairs={{0,8},{4,12},{8,16},{12,20},{16,24},{20,28},{24,0},{28,4},{1,9},{5... | collective-permute-start | bytes 331784 | tf_op jit(solution)/shard_map/ppermute | solution.py:34
  47.0 8.0 %collective-permute-start.10 = (f32[108,128]{1,0:T(8,128)S(1)}, f32[108,128]{1,0:T(8,128)S(1)}, u32[]{:S(2)}, u32[]{:S(2)}) collective-permute-start(f32[108,128]{1,0:T(8,128)S(1)} %get-tuple-element.63), channel_id=1, source_target_pairs={{0,28},{4,0},{8,4},{12,8},{16,12},{20,16},{24,20},{28,24},{1,29},{... | collective-permute-start | bytes 165896 | tf_op jit(solution)/shard_map/ppermute | solution.py:34
  47.5 7.5 %collective-permute-start.11 = (f32[108,128]{1,0:T(8,128)S(1)}, f32[108,128]{1,0:T(8,128)S(1)}, u32[]{:S(2)}, u32[]{:S(2)}) collective-permute-start(f32[108,128]{1,0:T(8,128)S(1)} %get-tuple-element.64), channel_id=1, source_target_pairs={{0,24},{4,28},{8,0},{12,4},{16,8},{20,12},{24,16},{28,20},{1,25},{... | collective-permute-start | bytes 165896 | tf_op jit(solution)/shard_map/ppermute | solution.py:34
  48.5 8.5 %collective-permute-start.8 = (f32[108,128]{1,0:T(8,128)S(1)}, f32[108,128]{1,0:T(8,128)S(1)}, u32[]{:S(2)}, u32[]{:S(2)}) collective-permute-start(f32[108,128]{1,0:T(8,128)S(1)} %get-tuple-element.61), channel_id=1, source_target_pairs={{0,8},{4,12},{8,16},{12,20},{16,24},{20,28},{24,0},{28,4},{1,9},{5... | collective-permute-start | bytes 165896 | tf_op jit(solution)/shard_map/ppermute | solution.py:34
  51.5 9.6 %collective-permute-start.16 = (f32[216,128]{1,0:T(8,128)S(1)}, f32[216,128]{1,0:T(8,128)S(1)}, u32[]{:S(2)}, u32[]{:S(2)}) collective-permute-start(f32[216,128]{1,0:T(8,128)S(1)} %get-tuple-element.70), channel_id=1, source_target_pairs={{0,8},{4,12},{8,16},{12,20},{16,24},{20,28},{24,0},{28,4},{1,9},{5... | collective-permute-start | bytes 331784 | tf_op jit(solution)/shard_map/ppermute | solution.py:34
  52.5 8.6 %collective-permute-start.17 = (f32[216,128]{1,0:T(8,128)S(1)}, f32[216,128]{1,0:T(8,128)S(1)}, u32[]{:S(2)}, u32[]{:S(2)}) collective-permute-start(f32[216,128]{1,0:T(8,128)S(1)} %get-tuple-element.71), channel_id=1, source_target_pairs={{0,4},{4,8},{8,12},{12,16},{16,20},{20,24},{24,28},{28,0},{1,5},{5... | collective-permute-start | bytes 331784 | tf_op jit(solution)/shard_map/ppermute | solution.py:34
  55.0 7.5 %collective-permute-start.19 = (f32[216,128]{1,0:T(8,128)S(1)}, f32[216,128]{1,0:T(8,128)S(1)}, u32[]{:S(2)}, u32[]{:S(2)}) collective-permute-start(f32[216,128]{1,0:T(8,128)S(1)} %get-tuple-element.73), channel_id=1, source_target_pairs={{0,24},{4,28},{8,0},{12,4},{16,8},{20,12},{24,16},{28,20},{1,25},{... | collective-permute-start | bytes 331784 | tf_op jit(solution)/shard_map/ppermute | solution.py:34
  79.1 7.5 %collective-permute-start.27 = (f32[216,128]{1,0:T(8,128)S(1)}, f32[216,128]{1,0:T(8,128)S(1)}, u32[]{:S(2)}, u32[]{:S(2)}) collective-permute-start(f32[216,128]{1,0:T(8,128)S(1)} %get-tuple-element.84), channel_id=1, source_target_pairs={{0,24},{4,28},{8,0},{12,4},{16,8},{20,12},{24,16},{28,20},{1,25},{... | collective-permute-start | bytes 331784 | tf_op jit(solution)/shard_map/ppermute | solution.py:34
  79.5 8.1 %collective-permute-start.28 = (f32[216,128]{1,0:T(8,128)S(1)}, f32[216,128]{1,0:T(8,128)S(1)}, u32[]{:S(2)}, u32[]{:S(2)}) collective-permute-start(f32[216,128]{1,0:T(8,128)S(1)} %get-tuple-element.85), channel_id=1, source_target_pairs={{0,28},{4,0},{8,4},{12,8},{16,12},{20,16},{24,20},{28,24},{1,29},{... | collective-permute-start | bytes 331784 | tf_op jit(solution)/shard_map/ppermute | solution.py:34
  80.4 8.6 %collective-permute-start.29 = (f32[216,128]{1,0:T(8,128)S(1)}, f32[216,128]{1,0:T(8,128)S(1)}, u32[]{:S(2)}, u32[]{:S(2)}) collective-permute-start(f32[216,128]{1,0:T(8,128)S(1)} %get-tuple-element.86), channel_id=1, source_target_pairs={{0,4},{4,8},{8,12},{12,16},{16,20},{20,24},{24,28},{28,0},{1,5},{5... | collective-permute-start | bytes 331784 | tf_op jit(solution)/shard_map/ppermute | solution.py:34
  81.9 7.4 %collective-permute-start.30 = (f32[216,128]{1,0:T(8,128)S(1)}, f32[216,128]{1,0:T(8,128)S(1)}, u32[]{:S(2)}, u32[]{:S(2)}) collective-permute-start(f32[216,128]{1,0:T(8,128)S(1)} %get-tuple-element.87), channel_id=1, source_target_pairs={{0,8},{4,12},{8,16},{12,20},{16,24},{20,28},{24,0},{28,4},{1,9},{5... | collective-permute-start | bytes 331784 | tf_op jit(solution)/shard_map/ppermute | solution.py:34
  85.2 9.6 %collective-permute-start.24 = (f32[216,128]{1,0:T(8,128)S(1)}, f32[216,128]{1,0:T(8,128)S(1)}, u32[]{:S(2)}, u32[]{:S(2)}) collective-permute-start(f32[216,128]{1,0:T(8,128)S(1)} %get-tuple-element.81), channel_id=1, source_target_pairs={{0,1},{1,2},{2,3},{3,0},{4,5},{5,6},{6,7},{7,4},{8,9},{9,10},{10,1... | collective-permute-start | bytes 331784 | tf_op jit(solution)/shard_map/ppermute | solution.py:34
  86.6 9.6 %collective-permute-start.25 = (f32[216,128]{1,0:T(8,128)S(1)}, f32[216,128]{1,0:T(8,128)S(1)}, u32[]{:S(2)}, u32[]{:S(2)}) collective-permute-start(f32[216,128]{1,0:T(8,128)S(1)} %get-tuple-element.82), channel_id=1, source_target_pairs={{0,2},{1,3},{2,0},{3,1},{4,6},{5,7},{6,4},{7,5},{8,10},{9,11},{10,... | collective-permute-start | bytes 331784 | tf_op jit(solution)/shard_map/ppermute | solution.py:34
  87.7 20.1 %collective-permute-start.26 = (f32[216,128]{1,0:T(8,128)S(1)}, f32[216,128]{1,0:T(8,128)S(1)}, u32[]{:S(2)}, u32[]{:S(2)}) collective-permute-start(f32[216,128]{1,0:T(8,128)S(1)} %get-tuple-element.83), channel_id=1, source_target_pairs={{0,3},{1,0},{2,1},{3,2},{4,7},{5,4},{6,5},{7,6},{8,11},{9,8},{10,9... | collective-permute-start | bytes 331784 | tf_op jit(solution)/shard_map/ppermute | solution.py:34
  91.5 18.9 %collective-permute-start.31 = (f32[432,128]{1,0:T(8,128)S(1)}, f32[432,128]{1,0:T(8,128)S(1)}, u32[]{:S(2)}, u32[]{:S(2)}) collective-permute-start(f32[432,128]{1,0:T(8,128)S(1)} %get-tuple-element.90), channel_id=1, source_target_pairs={{0,1},{1,2},{2,3},{3,0},{4,5},{5,6},{6,7},{7,4},{8,9},{9,10},{10,1... | collective-permute-start | bytes 663560 | tf_op jit(solution)/shard_map/ppermute | solution.py:34
  92.9 22.2 %collective-permute-start.32 = (f32[432,128]{1,0:T(8,128)S(1)}, f32[432,128]{1,0:T(8,128)S(1)}, u32[]{:S(2)}, u32[]{:S(2)}) collective-permute-start(f32[432,128]{1,0:T(8,128)S(1)} %get-tuple-element.91), channel_id=1, source_target_pairs={{0,2},{1,3},{2,0},{3,1},{4,6},{5,7},{6,4},{7,5},{8,10},{9,11},{10,... | collective-permute-start | bytes 663560 | tf_op jit(solution)/shard_map/ppermute | solution.py:34
  94.8 22.4 %collective-permute-start.33 = (f32[432,128]{1,0:T(8,128)S(1)}, f32[432,128]{1,0:T(8,128)S(1)}, u32[]{:S(2)}, u32[]{:S(2)}) collective-permute-start(f32[432,128]{1,0:T(8,128)S(1)} %get-tuple-element.92), channel_id=1, source_target_pairs={{0,3},{1,0},{2,1},{3,2},{4,7},{5,4},{6,5},{7,6},{8,11},{9,8},{10,9... | collective-permute-start | bytes 663560 | tf_op jit(solution)/shard_map/ppermute | solution.py:34
  (15 other events, 111.9 us)

commit v6 on v5

--- a/solution.py
+++ b/solution.py
@@ -154,7 +154,7 @@
             block_to_rows(sub, lanes, block, square, full, own_rows + position * ghost_rows, start)
 
     share = elements // GROUPS
-    unroll = chunked(share, 16)
+    unroll = chunked(share, 32)
 
     @pl.loop(0, share // unroll)
     def _(k):
@@ -235,13 +235,14 @@
     pack_rows(parts, lanes, send, full, stages, outs)
 
 
-def leave_kernel(sub, parts, lanes, halves, count, place, send, weight, *rest):
+def leave_kernel(sub, parts, lanes, halves, count, send, weight, *rest):
     incoming, rest = rest[:BLOCKS], rest[BLOCKS + 1 :]
     full, outs, square, stages = rest[0], rest[1 : 1 + count], rest[1 + count], rest[2 + count]
     add_returned(parts, lanes, send, weight, incoming, square, stages, full)
     start, size = parts
+    place = send[send.shape[0] - 1]
     for distance in range(count):
-        target = lax.rem(place[0] + distance, count)
+        target = lax.rem(place + distance, count)
         for half in range(halves):
             first = (target * halves + half) * LANES * sub + start
             for part in range(size):
@@ -249,27 +250,28 @@
                 outs[distance][pl.ds(part * lanes * halves + half, lanes, stride=halves), :] = tile[:lanes]
 
 
-def interact_kernel(per_source, halves, count, starts, place, plus, minus, rate, *rest):
+def interact_kernel(per_source, halves, count, starts, partner, rate, *rest):
     pieces, rest = rest[: count * len(starts)], rest[count * len(starts) :]
     target, energy, kept, added, out, done = rest[0], rest[1], rest[2], rest[3:-2], rest[-2], rest[-1]
+    bins = rate.shape[0]
+    place = partner[2 * bins]
     clear(added)
     for which, start in enumerate(starts):
         for distance in range(count):
             piece = pieces[which * count + distance]
-            first = lax.rem(place[0] + count - distance, count) * per_source + start
+            first = lax.rem(place + count - distance, count) * per_source + start
             if per_source % 8 == 0 and start % 8 == 0:
                 first = pl.multiple_of(first, 8)
             energy[pl.ds(first, piece.shape[0]), :] = piece[...]
-    bins = plus.shape[0]
     share = bins // GROUPS
-    unroll = chunked(share, 12)
+    unroll = chunked(share, 18)
 
     @pl.loop(0, share // unroll)
     def _(k):
         for u in range(unroll):
             for group in range(GROUPS):
                 index = group * share + k * unroll + u
-                up, down = plus[index], minus[index]
+                up, down = partner[index], partner[bins + index]
                 here = pl.ds(index * halves, halves)
                 own = energy[here, :]
                 upper = energy[pl.ds(up, halves), :]
@@ -331,9 +333,10 @@
     rows = own_rows + BLOCKS * ghost_rows
     halves = owned // (spec_count * LANES)
 
-    send = (send_nodes[0] * sub).reshape(-1)
     nodes = (conn * sub).reshape(-1)
     place = lax.axis_index("spec").reshape(1)
+    send = (send_nodes[0] * sub).reshape(-1)
+    listing = jnp.concatenate([send, place])
 
     bin_of = (
         lax.axis_index("spec") * row_count
@@ -419,25 +422,25 @@
         full, *blocks = pl.pallas_call(
             functools.partial(leave_kernel, sub, (start, size), lanes, halves, spec_count),
             out_shape=[full_shape] + [shape_of(size * lanes * halves, LANES)] * spec_count,
-            in_specs=[SM] * 2 + [VM] * (2 + BLOCKS),
+            in_specs=[SM] + [VM] * (2 + BLOCKS),
             out_specs=[VM] * (1 + spec_count),
-            input_output_aliases={3 + BLOCKS: 0},
+            input_output_aliases={2 + BLOCKS: 0},
             scratch_shapes=[squares, stages],
             cost_estimate=cost(2 * owned * size * LANES, 3 * moved * size // sub),
             compiler_params=limit(4),
-        )(place, send, weight, *incoming[which * BLOCKS : (which + 1) * BLOCKS], full)
+        )(listing, weight, *incoming[which * BLOCKS : (which + 1) * BLOCKS], full)
         pieces += [blocks[0]] + [passed_along(blocks[d], "spec", d) for d in range(1, spec_count)]
     return pl.pallas_call(
         functools.partial(interact_kernel, row_count * halves, halves, spec_count, [s * lanes * halves for s, _ in groups]),
         out_shape=shape_of(bins, halves * LANES),
-        in_specs=[SM] * 4 + [VM] * len(pieces),
+        in_specs=[SM] * 2 + [VM] * len(pieces),
         out_specs=pl.BlockSpec(memory_space=pl.ANY),
         scratch_shapes=[pltpu.VMEM((bins * halves, LANES), jnp.float32)] * (2 + 2 * GROUPS)
         + [pltpu.VMEM((bins, halves * LANES), jnp.float32), pltpu.SemaphoreType.DMA((chunked(bins // 48, 4),))],
         cost_estimate=cost(16 * bins * halves * LANES, 8 * bins * halves * LANES),
         compiler_params=limit(12),
         name="interact",
-    )(place, dia_plus * halves, dia_minus * halves, dia_coeff, *pieces)
+    )(jnp.concatenate([dia_plus * halves, dia_minus * halves, place]), dia_coeff, *pieces)
 
 
 def solution(mesh):

time: 124 us -> 124 us (level)
    pallas_call x2, Pallas kernels: 4.13 us -> 5.38 us  [on_device(): pl.pallas_call(functools.partial(leave_kernel, sub, (start, size), lanes,...]
  transfers between devices with their start and end apart: 34 -> 34, of which waited for: 10 -> 9; matrix products, arithmetic and copies ran while one was open for 2% -> 2% of each run, Pallas kernels for 11% -> 12%
where the time goes in v6:
time: 124 us
  Pallas kernels  46.3 us (37%)
  starting transfers between devices  40.3 us (32%)
  waiting for transfers between devices  32 us (26%)
  local copies, waits for them, and re-layouts  2.95 us (2%)
  other arithmetic  2.42 us (2%)
    ppermute x34, starting transfers between devices, passed_along(): lax.ppermute(value, axis, [(source, (source + steps) % count) for source...  40.3 us
    ppermute x34, waiting for transfers between devices, passed_along(): lax.ppermute(value, axis, [(source, (source + steps) % count) for source...  32 us
    pallas_call x2, Pallas kernels, on_device(): pl.pallas_call(functools.partial(sweep_kernel, sub, inner, groups, lanes,...  22 us
    pallas_call x1, Pallas kernels, on_device(): pl.pallas_call(functools.partial(interact_kernel, row_count * halves, hal...  6.71 us
    pallas_call x2, Pallas kernels, on_device(): pl.pallas_call(functools.partial(leave_kernel, sub, (start, size), lanes,...  5.38 us
    pallas_call x2, Pallas kernels, on_device(): pl.pallas_call(functools.partial(between_kernel, parts, lanes), out_shape...  4.91 us
    pallas_call x1, Pallas kernels, on_device(): pl.pallas_call(functools.partial(slope_kernel, sub, shared), out_shape=[s...  4.88 us
    unnamed x11, local copies, waits for them, and re-layouts  2.85 us
  transfers between devices with their start and end apart: 34, of which 9 were waited for; matrix products, arithmetic and copies ran while one was open for 2% of the time, Pallas kernels for 12%

profile of v6, /device:TPU:9, one launch (start us, length us, event | category | flops | bytes accessed | tf_op | source)
XLA Modules:
  0.0 124.1 jit_solution(12919258948196725375)
XLA Ops:
  2.0 2.4 %enter.1 = (f32[4608,128]{1,0:T(8,128)S(1)}, f32[324,128]{1,0:T(8,128)}, f32[324,128]{1,0:T(8,128)}, f32[324,128]{1,0:T(8,128)S(1)}, f32[324,128]{1,0:T(8,128)S(1)}) custom-call(s32[512]{0:T(512)S(1)} %multiply_bitcast_fusion.send, f32[324,1024]{1,0:T(8,128)S(1)} %copy-done), custom_call_target="tpu_custom_call" | custom-call | bytes 3145728 | tf_op jit(solution)/shard_map/enter/pallas_call | solution.py:363
  5.6 2.1 %collective-permute-start.1 = (f32[324,128]{1,0:T(8,128)}, f32[324,128]{1,0:T(8,128)S(1)}, u32[]{:S(2)}, u32[]{:S(2)}) collective-permute-start(f32[324,128]{1,0:T(8,128)} %get-tuple-element.52), channel_id=1, source_target_pairs={{0,4},{4,8},{8,12},{12,16},{16,20},{20,24},{24,28},{28,0},{1,5},{5... | collective-permute-start | bytes 497672 | tf_op jit(solution)/shard_map/ppermute | solution.py:34
  12.1 4.9 %slopes.1 = (f32[6144,128]{1,0:T(8,128)S(1)}, f32[3072,128]{1,0:T(8,128)S(1)}) custom-call(f32[2,3,2048]{2,1,0:T(4,128)S(1)} %copy.17.normals, f32[1,1024]{1,0:T(1,128)S(1)} %bitcast.4, f32[9,128]{1,0:T(8,128)S(1)} %pad_maximum_fusion.wave), custom_call_target="tpu_custom_call" | custom-call | flops 5242880 | bytes 4718592 | tf_op jit(solution)/shard_map/slopes/pallas_call | solution.py:374
  18.0 11.0 %sweep.2 = (f32[4608,128]{1,0:T(8,128)S(1)}, f32[108,128]{1,0:T(8,128)S(1)}, f32[108,128]{1,0:T(8,128)S(1)}, f32[108,128]{1,0:T(8,128)S(1)}, f32[108,128]{1,0:T(...) custom-call(s32[6144]{0:T(1024)S(1)} %reshape.51.conn, ...), custom_call_target="tpu_custom_call", output_to_operand_aliasing={{0}: (7, {})} | custom-call | flops 15925248 | bytes 12582912 | tf_op jit(solution)/shard_map/sweep/pallas_call | solution.py:391
  32.1 2.1 %collective-permute-start.12 = (f32[216,128]{1,0:T(8,128)S(1)}, f32[216,128]{1,0:T(8,128)S(1)}, u32[]{:S(2)}, u32[]{:S(2)}) collective-permute-start(f32[216,128]{1,0:T(8,128)S(1)} %get-tuple-element.65), channel_id=1, source_target_pairs={{0,24},{4,28},{8,0},{12,4},{16,8},{20,12},{24,16},{28,20},{1,25},{... | collective-permute-start | bytes 331784 | tf_op jit(solution)/shard_map/ppermute | solution.py:34
  34.2 2.9 %collective-permute-start.14 = (f32[216,128]{1,0:T(8,128)S(1)}, f32[216,128]{1,0:T(8,128)S(1)}, u32[]{:S(2)}, u32[]{:S(2)}) collective-permute-start(f32[216,128]{1,0:T(8,128)S(1)} %get-tuple-element.67), channel_id=1, source_target_pairs={{0,4},{4,8},{8,12},{12,16},{16,20},{20,24},{24,28},{28,0},{1,5},{5... | collective-permute-start | bytes 331784 | tf_op jit(solution)/shard_map/ppermute | solution.py:34
  38.7 5.6 %collective-permute-done.7.rest_3_ = f32[108,128]{1,0:T(8,128)S(1)} collective-permute-done((f32[108,128]{1,0:T(8,128)S(1)}, f32[108,128]{1,0:T(8,128)S(1)}, u32[]{:S(2)}, u32[]{:S(2)}) %collective-permute-start.7) | collective-permute-done | bytes 55328 | tf_op jit(solution)/shard_map/ppermute | solution.py:34
  44.3 2.4 %shard_map.91 = (f32[4608,128]{1,0:T(8,128)S(1)}, f32[108,128]{1,0:T(8,128)S(1)}, f32[108,128]{1,0:T(8,128)S(1)}, f32[108,128]{1,0:T(8,128)S(1)}, f32[108,128]{1,0:T(8,128)S(1)}) custom-call(s32[512]{0:T(512)S(1)} %multiply_bitcast_fusion.send, f32[3072,128]{1,0:T(8,128)S(1)} %get-tuple-element.49.weight, ...), custom_call_target="tpu_custom_call", output_to_operand_aliasing={{0}: (6, {})} | custom-call | flops 262144 | bytes 2097152 | tf_op jit(solution)/shard_map/pallas_call | solution.py:408
  48.7 2.5 %shard_map.92 = (f32[4608,128]{1,0:T(8,128)S(1)}, f32[216,128]{1,0:T(8,128)S(1)}, f32[216,128]{1,0:T(8,128)S(1)}, f32[216,128]{1,0:T(8,128)S(1)}, f32[216,128]{1,0:T(8,128)S(1)}) custom-call(s32[512]{0:T(512)S(1)} %multiply_bitcast_fusion.send, f32[3072,128]{1,0:T(8,128)S(1)} %get-tuple-element.49.weight, ...), custom_call_target="tpu_custom_call", output_to_operand_aliasing={{0}: (6, {})} | custom-call | flops 524288 | bytes 4194304 | tf_op jit(solution)/shard_map/pallas_call | solution.py:408
  52.2 2.5 %collective-permute-start.17 = (f32[216,128]{1,0:T(8,128)S(1)}, f32[216,128]{1,0:T(8,128)S(1)}, u32[]{:S(2)}, u32[]{:S(2)}) collective-permute-start(f32[216,128]{1,0:T(8,128)S(1)} %get-tuple-element.71), channel_id=1, source_target_pairs={{0,4},{4,8},{8,12},{12,16},{16,20},{20,24},{24,28},{28,0},{1,5},{5... | collective-permute-start | bytes 331784 | tf_op jit(solution)/shard_map/ppermute | solution.py:34
  54.7 2.0 %collective-permute-start.19 = (f32[216,128]{1,0:T(8,128)S(1)}, f32[216,128]{1,0:T(8,128)S(1)}, u32[]{:S(2)}, u32[]{:S(2)}) collective-permute-start(f32[216,128]{1,0:T(8,128)S(1)} %get-tuple-element.73), channel_id=1, source_target_pairs={{0,24},{4,28},{8,0},{12,4},{16,8},{20,12},{24,16},{28,20},{1,25},{... | collective-permute-start | bytes 331784 | tf_op jit(solution)/shard_map/ppermute | solution.py:34
  56.8 2.0 %collective-permute-start.9 = (f32[108,128]{1,0:T(8,128)S(1)}, f32[108,128]{1,0:T(8,128)S(1)}, u32[]{:S(2)}, u32[]{:S(2)}) collective-permute-start(f32[108,128]{1,0:T(8,128)S(1)} %get-tuple-element.62), channel_id=1, source_target_pairs={{0,4},{4,8},{8,12},{12,16},{16,20},{20,24},{24,28},{28,0},{1,5},{5... | collective-permute-start | bytes 165896 | tf_op jit(solution)/shard_map/ppermute | solution.py:34
  58.7 2.1 %collective-permute-done.9.rest_1_ = f32[108,128]{1,0:T(8,128)S(1)} collective-permute-done((f32[108,128]{1,0:T(8,128)S(1)}, f32[108,128]{1,0:T(8,128)S(1)}, u32[]{:S(2)}, u32[]{:S(2)}) %collective-permute-start.9) | collective-permute-done | bytes 55328 | tf_op jit(solution)/shard_map/ppermute | solution.py:34
  62.3 11.0 %sweep.3 = (f32[4608,128]{1,0:T(8,128)S(1)}, f32[108,128]{1,0:T(8,128)S(1)}, f32[108,128]{1,0:T(8,128)S(1)}, f32[108,128]{1,0:T(8,128)S(1)}, f32[108,128]{1,0:T(...) custom-call(s32[6144]{0:T(1024)S(1)} %reshape.51.conn, ...), custom_call_target="tpu_custom_call", output_to_operand_aliasing={{0}: (11, {})} | custom-call | flops 15925248 | bytes 12582912 | tf_op jit(solution)/shard_map/sweep/pallas_call | solution.py:391
  74.0 2.5 %collective-permute-start.21 = (f32[108,128]{1,0:T(8,128)S(1)}, f32[108,128]{1,0:T(8,128)S(1)}, u32[]{:S(2)}, u32[]{:S(2)}) collective-permute-start(f32[108,128]{1,0:T(8,128)S(1)} %get-tuple-element.76), channel_id=1, source_target_pairs={{0,28},{4,0},{8,4},{12,8},{16,12},{20,16},{24,20},{28,24},{1,29},{... | collective-permute-start | bytes 165896 | tf_op jit(solution)/shard_map/ppermute | solution.py:34
  76.7 1.9 %collective-permute-start.23 = (f32[108,128]{1,0:T(8,128)S(1)}, f32[108,128]{1,0:T(8,128)S(1)}, u32[]{:S(2)}, u32[]{:S(2)}) collective-permute-start(f32[108,128]{1,0:T(8,128)S(1)} %get-tuple-element.78), channel_id=1, source_target_pairs={{0,8},{4,12},{8,16},{12,20},{16,24},{20,28},{24,0},{28,4},{1,9},{5... | collective-permute-start | bytes 165896 | tf_op jit(solution)/shard_map/ppermute | solution.py:34
  82.8 2.6 %shard_map.93 = (f32[4608,128]{1,0:T(8,128)S(1)}, f32[216,128]{1,0:T(8,128)S(1)}, f32[216,128]{1,0:T(8,128)S(1)}, f32[216,128]{1,0:T(8,128)}, f32[216,128]{1,0:T(8,128)}) custom-call(s32[513]{0:T(1024)S(1)} %pad_add_fusion.send, f32[3072,128]{1,0:T(8,128)S(1)} %get-tuple-element.49.weight, ...), custom_call_target="tpu_custom_call", output_to_operand_aliasing={{0}: (6, {})} | custom-call | flops 262144 | bytes 1572864 | tf_op jit(solution)/shard_map/pallas_call | solution.py:422
  89.2 2.7 %shard_map.94 = (f32[4608,128]{1,0:T(8,128)S(1)}, f32[432,128]{1,0:T(8,128)S(1)}, f32[432,128]{1,0:T(8,128)}, f32[432,128]{1,0:T(8,128)S(1)}, f32[432,128]{1,0:T(8,128)S(1)}) custom-call(s32[513]{0:T(1024)S(1)} %pad_add_fusion.send, f32[3072,128]{1,0:T(8,128)S(1)} %get-tuple-element.49.weight, ...), custom_call_target="tpu_custom_call", output_to_operand_aliasing={{0}: (6, {})} | custom-call | flops 524288 | bytes 3145728 | tf_op jit(solution)/shard_map/pallas_call | solution.py:422
  92.9 2.2 %collective-permute-start.32 = (f32[432,128]{1,0:T(8,128)S(1)}, f32[432,128]{1,0:T(8,128)S(1)}, u32[]{:S(2)}, u32[]{:S(2)}) collective-permute-start(f32[432,128]{1,0:T(8,128)S(1)} %get-tuple-element.91), channel_id=1, source_target_pairs={{0,2},{1,3},{2,0},{3,1},{4,6},{5,7},{6,4},{7,5},{8,10},{9,11},{10,... | collective-permute-start | bytes 663560 | tf_op jit(solution)/shard_map/ppermute | solution.py:34
  96.5 11.4 %collective-permute-done.26.rest_3_ = f32[216,128]{1,0:T(8,128)S(1)} collective-permute-done((f32[216,128]{1,0:T(8,128)}, f32[216,128]{1,0:T(8,128)S(1)}, u32[]{:S(2)}, u32[]{:S(2)}) %collective-permute-start.26) | collective-permute-done | bytes 110624 | tf_op jit(solution)/shard_map/ppermute | solution.py:34
  107.9 2.8 %collective-permute-done.31.rest_5_ = f32[432,128]{1,0:T(8,128)S(1)} collective-permute-done((f32[432,128]{1,0:T(8,128)}, f32[432,128]{1,0:T(8,128)S(1)}, u32[]{:S(2)}, u32[]{:S(2)}) %collective-permute-start.31) | collective-permute-done | bytes 221216 | tf_op jit(solution)/shard_map/ppermute | solution.py:34
  110.7 4.6 %collective-permute-done.32.rest_6_ = f32[432,128]{1,0:T(8,128)S(1)} collective-permute-done((f32[432,128]{1,0:T(8,128)S(1)}, f32[432,128]{1,0:T(8,128)S(1)}, u32[]{:S(2)}, u32[]{:S(2)}) %collective-permute-start.32) | collective-permute-done | bytes 221216 | tf_op jit(solution)/shard_map/ppermute | solution.py:34
  115.3 2.0 %collective-permute-done.33.rest_7_ = f32[432,128]{1,0:T(8,128)S(1)} collective-permute-done((f32[432,128]{1,0:T(8,128)S(1)}, f32[432,128]{1,0:T(8,128)S(1)}, u32[]{:S(2)}, u32[]{:S(2)}) %collective-permute-start.33) | collective-permute-done | bytes 221216 | tf_op jit(solution)/shard_map/ppermute | solution.py:34
  117.4 6.7 %interact.1 = f32[1296,256]{1,0:T(8,128)} custom-call(s32[2593]{0:T(1024)S(1)} %concatenate.9.partner, f32[1296]{0:T(1024)S(1)} %copy-done.1, f32[216,128]{1,0:T(8,128)S(1)} %get-tuple-element.80.rest_0_, f32[216,128]{1,0:T(8,128)S(1)} %collective-permute-done.24.rest_1_, f32[216,128]{1,0:T(8,128)S(1)} %collective-permute-done.25.rest_2_, ...), custom_call_target="tpu_custom_call" | custom-call | flops 5308416 | bytes 2654208 | tf_op jit(solution)/shard_map/interact/pallas_call | solution.py:433
  (75 shorter events, 28.9 us)
Async XLA Ops:
  4.4 12.6 %collective-permute-start = (f32[324,128]{1,0:T(8,128)}, f32[324,128]{1,0:T(8,128)S(1)}, u32[]{:S(2)}, u32[]{:S(2)}) collective-permute-start(f32[324,128]{1,0:T(8,128)} %get-tuple-element.51), channel_id=1, source_target_pairs={{0,8},{4,12},{8,16},{12,20},{16,24},{20,28},{24,0},{28,4},{1,9},{5... | collective-permute-start | bytes 497672 | tf_op jit(solution)/shard_map/ppermute | solution.py:34
  5.6 11.4 %collective-permute-start.1 = (f32[324,128]{1,0:T(8,128)}, f32[324,128]{1,0:T(8,128)S(1)}, u32[]{:S(2)}, u32[]{:S(2)}) collective-permute-start(f32[324,128]{1,0:T(8,128)} %get-tuple-element.52), channel_id=1, source_target_pairs={{0,4},{4,8},{8,12},{12,16},{16,20},{20,24},{24,28},{28,0},{1,5},{5... | collective-permute-start | bytes 497672 | tf_op jit(solution)/shard_map/ppermute | solution.py:34
  7.7 9.4 %collective-permute-start.2 = (f32[324,128]{1,0:T(8,128)S(1)}, f32[324,128]{1,0:T(8,128)S(1)}, u32[]{:S(2)}, u32[]{:S(2)}) collective-permute-start(f32[324,128]{1,0:T(8,128)S(1)} %get-tuple-element.53), channel_id=1, source_target_pairs={{0,28},{4,0},{8,4},{12,8},{16,12},{20,16},{24,20},{28,24},{1,29},{... | collective-permute-start | bytes 497672 | tf_op jit(solution)/shard_map/ppermute | solution.py:34
  7.7 10.3 %collective-permute-start.3 = (f32[324,128]{1,0:T(8,128)S(1)}, f32[324,128]{1,0:T(8,128)S(1)}, u32[]{:S(2)}, u32[]{:S(2)}) collective-permute-start(f32[324,128]{1,0:T(8,128)S(1)} %get-tuple-element.54), channel_id=1, source_target_pairs={{0,24},{4,28},{8,0},{12,4},{16,8},{20,12},{24,16},{28,20},{1,25},{... | collective-permute-start | bytes 497672 | tf_op jit(solution)/shard_map/ppermute | solution.py:34
  32.1 15.1 %collective-permute-start.12 = (f32[216,128]{1,0:T(8,128)S(1)}, f32[216,128]{1,0:T(8,128)S(1)}, u32[]{:S(2)}, u32[]{:S(2)}) collective-permute-start(f32[216,128]{1,0:T(8,128)S(1)} %get-tuple-element.65), channel_id=1, source_target_pairs={{0,24},{4,28},{8,0},{12,4},{16,8},{20,12},{24,16},{28,20},{1,25},{... | collective-permute-start | bytes 331784 | tf_op jit(solution)/shard_map/ppermute | solution.py:34
  34.2 14.0 %collective-permute-start.13 = (f32[216,128]{1,0:T(8,128)S(1)}, f32[216,128]{1,0:T(8,128)S(1)}, u32[]{:S(2)}, u32[]{:S(2)}) collective-permute-start(f32[216,128]{1,0:T(8,128)S(1)} %get-tuple-element.66), channel_id=1, source_target_pairs={{0,28},{4,0},{8,4},{12,8},{16,12},{20,16},{24,20},{28,24},{1,29},{... | collective-permute-start | bytes 331784 | tf_op jit(solution)/shard_map/ppermute | solution.py:34
  34.2 14.5 %collective-permute-start.14 = (f32[216,128]{1,0:T(8,128)S(1)}, f32[216,128]{1,0:T(8,128)S(1)}, u32[]{:S(2)}, u32[]{:S(2)}) collective-permute-start(f32[216,128]{1,0:T(8,128)S(1)} %get-tuple-element.67), channel_id=1, source_target_pairs={{0,4},{4,8},{8,12},{12,16},{16,20},{20,24},{24,28},{28,0},{1,5},{5... | collective-permute-start | bytes 331784 | tf_op jit(solution)/shard_map/ppermute | solution.py:34
  37.1 11.6 %collective-permute-start.15 = (f32[216,128]{1,0:T(8,128)S(1)}, f32[216,128]{1,0:T(8,128)S(1)}, u32[]{:S(2)}, u32[]{:S(2)}) collective-permute-start(f32[216,128]{1,0:T(8,128)S(1)} %get-tuple-element.68), channel_id=1, source_target_pairs={{0,8},{4,12},{8,16},{12,20},{16,24},{20,28},{24,0},{28,4},{1,9},{5... | collective-permute-start | bytes 331784 | tf_op jit(solution)/shard_map/ppermute | solution.py:34
  46.7 8.0 %collective-permute-start.10 = (f32[108,128]{1,0:T(8,128)S(1)}, f32[108,128]{1,0:T(8,128)S(1)}, u32[]{:S(2)}, u32[]{:S(2)}) collective-permute-start(f32[108,128]{1,0:T(8,128)S(1)} %get-tuple-element.63), channel_id=1, source_target_pairs={{0,28},{4,0},{8,4},{12,8},{16,12},{20,16},{24,20},{28,24},{1,29},{... | collective-permute-start | bytes 165896 | tf_op jit(solution)/shard_map/ppermute | solution.py:34
  47.2 7.5 %collective-permute-start.11 = (f32[108,128]{1,0:T(8,128)S(1)}, f32[108,128]{1,0:T(8,128)S(1)}, u32[]{:S(2)}, u32[]{:S(2)}) collective-permute-start(f32[108,128]{1,0:T(8,128)S(1)} %get-tuple-element.64), channel_id=1, source_target_pairs={{0,24},{4,28},{8,0},{12,4},{16,8},{20,12},{24,16},{28,20},{1,25},{... | collective-permute-start | bytes 165896 | tf_op jit(solution)/shard_map/ppermute | solution.py:34
  48.2 8.5 %collective-permute-start.8 = (f32[108,128]{1,0:T(8,128)S(1)}, f32[108,128]{1,0:T(8,128)S(1)}, u32[]{:S(2)}, u32[]{:S(2)}) collective-permute-start(f32[108,128]{1,0:T(8,128)S(1)} %get-tuple-element.61), channel_id=1, source_target_pairs={{0,8},{4,12},{8,16},{12,20},{16,24},{20,28},{24,0},{28,4},{1,9},{5... | collective-permute-start | bytes 165896 | tf_op jit(solution)/shard_map/ppermute | solution.py:34
  51.2 9.6 %collective-permute-start.16 = (f32[216,128]{1,0:T(8,128)S(1)}, f32[216,128]{1,0:T(8,128)S(1)}, u32[]{:S(2)}, u32[]{:S(2)}) collective-permute-start(f32[216,128]{1,0:T(8,128)S(1)} %get-tuple-element.70), channel_id=1, source_target_pairs={{0,8},{4,12},{8,16},{12,20},{16,24},{20,28},{24,0},{28,4},{1,9},{5... | collective-permute-start | bytes 331784 | tf_op jit(solution)/shard_map/ppermute | solution.py:34
  52.2 8.6 %collective-permute-start.17 = (f32[216,128]{1,0:T(8,128)S(1)}, f32[216,128]{1,0:T(8,128)S(1)}, u32[]{:S(2)}, u32[]{:S(2)}) collective-permute-start(f32[216,128]{1,0:T(8,128)S(1)} %get-tuple-element.71), channel_id=1, source_target_pairs={{0,4},{4,8},{8,12},{12,16},{16,20},{20,24},{24,28},{28,0},{1,5},{5... | collective-permute-start | bytes 331784 | tf_op jit(solution)/shard_map/ppermute | solution.py:34
  54.7 7.5 %collective-permute-start.19 = (f32[216,128]{1,0:T(8,128)S(1)}, f32[216,128]{1,0:T(8,128)S(1)}, u32[]{:S(2)}, u32[]{:S(2)}) collective-permute-start(f32[216,128]{1,0:T(8,128)S(1)} %get-tuple-element.73), channel_id=1, source_target_pairs={{0,24},{4,28},{8,0},{12,4},{16,8},{20,12},{24,16},{28,20},{1,25},{... | collective-permute-start | bytes 331784 | tf_op jit(solution)/shard_map/ppermute | solution.py:34
  78.6 8.1 %collective-permute-start.27 = (f32[216,128]{1,0:T(8,128)S(1)}, f32[216,128]{1,0:T(8,128)S(1)}, u32[]{:S(2)}, u32[]{:S(2)}) collective-permute-start(f32[216,128]{1,0:T(8,128)S(1)} %get-tuple-element.84), channel_id=1, source_target_pairs={{0,24},{4,28},{8,0},{12,4},{16,8},{20,12},{24,16},{28,20},{1,25},{... | collective-permute-start | bytes 331784 | tf_op jit(solution)/shard_map/ppermute | solution.py:34
  79.1 8.7 %collective-permute-start.28 = (f32[216,128]{1,0:T(8,128)S(1)}, f32[216,128]{1,0:T(8,128)S(1)}, u32[]{:S(2)}, u32[]{:S(2)}) collective-permute-start(f32[216,128]{1,0:T(8,128)S(1)} %get-tuple-element.85), channel_id=1, source_target_pairs={{0,28},{4,0},{8,4},{12,8},{16,12},{20,16},{24,20},{28,24},{1,29},{... | collective-permute-start | bytes 331784 | tf_op jit(solution)/shard_map/ppermute | solution.py:34
  80.0 9.2 %collective-permute-start.29 = (f32[216,128]{1,0:T(8,128)S(1)}, f32[216,128]{1,0:T(8,128)S(1)}, u32[]{:S(2)}, u32[]{:S(2)}) collective-permute-start(f32[216,128]{1,0:T(8,128)S(1)} %get-tuple-element.86), channel_id=1, source_target_pairs={{0,4},{4,8},{8,12},{12,16},{16,20},{20,24},{24,28},{28,0},{1,5},{5... | collective-permute-start | bytes 331784 | tf_op jit(solution)/shard_map/ppermute | solution.py:34
  81.5 7.7 %collective-permute-start.30 = (f32[216,128]{1,0:T(8,128)S(1)}, f32[216,128]{1,0:T(8,128)S(1)}, u32[]{:S(2)}, u32[]{:S(2)}) collective-permute-start(f32[216,128]{1,0:T(8,128)S(1)} %get-tuple-element.87), channel_id=1, source_target_pairs={{0,8},{4,12},{8,16},{12,20},{16,24},{20,28},{24,0},{28,4},{1,9},{5... | collective-permute-start | bytes 331784 | tf_op jit(solution)/shard_map/ppermute | solution.py:34
  85.4 9.7 %collective-permute-start.24 = (f32[216,128]{1,0:T(8,128)S(1)}, f32[216,128]{1,0:T(8,128)S(1)}, u32[]{:S(2)}, u32[]{:S(2)}) collective-permute-start(f32[216,128]{1,0:T(8,128)S(1)} %get-tuple-element.81), channel_id=1, source_target_pairs={{0,1},{1,2},{2,3},{3,0},{4,5},{5,6},{6,7},{7,4},{8,9},{9,10},{10,1... | collective-permute-start | bytes 331784 | tf_op jit(solution)/shard_map/ppermute | solution.py:34
  86.7 9.7 %collective-permute-start.25 = (f32[216,128]{1,0:T(8,128)}, f32[216,128]{1,0:T(8,128)S(1)}, u32[]{:S(2)}, u32[]{:S(2)}) collective-permute-start(f32[216,128]{1,0:T(8,128)} %get-tuple-element.82), channel_id=1, source_target_pairs={{0,2},{1,3},{2,0},{3,1},{4,6},{5,7},{6,4},{7,5},{8,10},{9,11},{10,... | collective-permute-start | bytes 331784 | tf_op jit(solution)/shard_map/ppermute | solution.py:34
  87.8 20.1 %collective-permute-start.26 = (f32[216,128]{1,0:T(8,128)}, f32[216,128]{1,0:T(8,128)S(1)}, u32[]{:S(2)}, u32[]{:S(2)}) collective-permute-start(f32[216,128]{1,0:T(8,128)} %get-tuple-element.83), channel_id=1, source_target_pairs={{0,3},{1,0},{2,1},{3,2},{4,7},{5,4},{6,5},{7,6},{8,11},{9,8},{10,9... | collective-permute-start | bytes 331784 | tf_op jit(solution)/shard_map/ppermute | solution.py:34
  92.0 18.7 %collective-permute-start.31 = (f32[432,128]{1,0:T(8,128)}, f32[432,128]{1,0:T(8,128)S(1)}, u32[]{:S(2)}, u32[]{:S(2)}) collective-permute-start(f32[432,128]{1,0:T(8,128)} %get-tuple-element.90), channel_id=1, source_target_pairs={{0,1},{1,2},{2,3},{3,0},{4,5},{5,6},{6,7},{7,4},{8,9},{9,10},{10,1... | collective-permute-start | bytes 663560 | tf_op jit(solution)/shard_map/ppermute | solution.py:34
  92.9 22.4 %collective-permute-start.32 = (f32[432,128]{1,0:T(8,128)S(1)}, f32[432,128]{1,0:T(8,128)S(1)}, u32[]{:S(2)}, u32[]{:S(2)}) collective-permute-start(f32[432,128]{1,0:T(8,128)S(1)} %get-tuple-element.91), channel_id=1, source_target_pairs={{0,2},{1,3},{2,0},{3,1},{4,6},{5,7},{6,4},{7,5},{8,10},{9,11},{10,... | collective-permute-start | bytes 663560 | tf_op jit(solution)/shard_map/ppermute | solution.py:34
  95.1 22.3 %collective-permute-start.33 = (f32[432,128]{1,0:T(8,128)S(1)}, f32[432,128]{1,0:T(8,128)S(1)}, u32[]{:S(2)}, u32[]{:S(2)}) collective-permute-start(f32[432,128]{1,0:T(8,128)S(1)} %get-tuple-element.92), channel_id=1, source_target_pairs={{0,3},{1,0},{2,1},{3,2},{4,7},{5,4},{6,5},{7,6},{8,11},{9,8},{10,9... | collective-permute-start | bytes 663560 | tf_op jit(solution)/shard_map/ppermute | solution.py:34
  (15 other events, 111.6 us)

commit v7 on v6

--- a/solution.py
+++ b/solution.py
@@ -22,7 +22,7 @@
 weight_both = 0.9375 ** (-4)
 
 VM = pl.BlockSpec(memory_space=pltpu.VMEM)
-SM = pl.BlockSpec(memory_space=pltpu.SMEM)
+ANY = pl.BlockSpec(memory_space=pl.ANY)
 
 
 def offset_of(position):
@@ -36,6 +36,16 @@
 
 def chunked(total, limit):
     return max(size for size in range(1, limit + 1) if total % size == 0)
+
+
+def listed_in(source, scratch, done):
+    copy = pltpu.make_async_copy(source, scratch, done)
+    copy.start()
+    return copy
+
+
+def list_scratch(length, dtype=jnp.int32):
+    return [pltpu.SMEM((length,), dtype), pltpu.SemaphoreType.DMA(())]
 
 
 def rows_to_block(sub, lanes, stage, block, start=0):
@@ -71,10 +81,12 @@
         rows_to_block(size, lanes, stages.at[position], outs[position])
 
 
-def enter_kernel(sub, lanes, send, spectrum, full, *rest):
-    outs, square, stages = rest[:BLOCKS], rest[BLOCKS], rest[BLOCKS + 1]
+def enter_kernel(sub, lanes, source, spectrum, full, *rest):
+    outs, (square, stages, send, done) = rest[:BLOCKS], rest[BLOCKS:]
+    pending = listed_in(source, send, done)
     square[...] = jnp.zeros_like(square)
     block_to_rows(sub, lanes, spectrum, square, full, 0)
+    pending.wait()
     pack_rows((0, sub), lanes, send, full, stages, outs)
 
 
@@ -138,11 +150,12 @@
     return result
 
 
-def sweep_kernel(sub, inner, groups, lanes, shared, own_rows, conn, coef, weight, *rest):
+def sweep_kernel(sub, inner, groups, lanes, shared, own_rows, source, coef, weight, *rest):
     ghosts, rest = rest[: BLOCKS * len(inner)], rest[BLOCKS * len(inner) + 1 :]
     full, rest = rest[0], rest[1:]
     returned, rest = rest[: BLOCKS * len(groups)], rest[BLOCKS * len(groups) :]
-    square, stages, sums = rest[0], rest[1], rest[2:]
+    square, stages, conn, done, sums = rest[0], rest[1], rest[2], rest[3], rest[4:]
+    pending = listed_in(source, conn, done)
     clear(sums)
     ghost_rows = (full.shape[0] - own_rows) // BLOCKS
     elements = conn.shape[0] // 3
@@ -153,6 +166,7 @@
             block = ghosts[which * BLOCKS + position]
             block_to_rows(sub, lanes, block, square, full, own_rows + position * ghost_rows, start)
 
+    pending.wait()
     share = elements // GROUPS
     unroll = chunked(share, 32)
 
@@ -205,13 +219,14 @@
         full[at, :] = full[at, :] - weight[at, :] * total(sums, at)
 
 
-def add_returned(parts, lanes, send, weight, incoming, square, stages, full):
+def add_returned(parts, lanes, pending, send, weight, incoming, square, stages, full):
     start, size = parts
     slots = incoming[0].shape[1]
     square[...] = jnp.zeros_like(square)
     unroll = chunked(slots, 16)
     for position in range(BLOCKS):
         block_to_rows(size, lanes, incoming[position], square, stages.at[position], 0)
+    pending.wait()
     for position in range(BLOCKS):
         stage = stages.at[position]
 
@@ -228,19 +243,21 @@
                 full[row, :] = item
 
 
-def between_kernel(parts, lanes, send, weight, *rest):
+def between_kernel(parts, lanes, source, weight, *rest):
     incoming, rest = rest[:BLOCKS], rest[BLOCKS + 1 :]
-    full, outs, square, stages = rest[0], rest[1 : 1 + BLOCKS], rest[1 + BLOCKS], rest[2 + BLOCKS]
-    add_returned(parts, lanes, send, weight, incoming, square, stages, full)
+    full, outs, (square, stages, send, done) = rest[0], rest[1 : 1 + BLOCKS], rest[1 + BLOCKS :]
+    pending = listed_in(source, send, done)
+    add_returned(parts, lanes, pending, send, weight, incoming, square, stages, full)
     pack_rows(parts, lanes, send, full, stages, outs)
 
 
-def leave_kernel(sub, parts, lanes, halves, count, send, weight, *rest):
+def leave_kernel(sub, parts, lanes, halves, count, source, weight, *rest):
     incoming, rest = rest[:BLOCKS], rest[BLOCKS + 1 :]
-    full, outs, square, stages = rest[0], rest[1 : 1 + count], rest[1 + count], rest[2 + count]
-    add_returned(parts, lanes, send, weight, incoming, square, stages, full)
+    full, outs, (square, stages, send, done) = rest[0], rest[1 : 1 + count], rest[1 + count :]
+    pending = listed_in(source, send, done)
+    add_returned(parts, lanes, pending, send, weight, incoming, square, stages, full)
     start, size = parts
-    place = send[send.shape[0] - 1]
+    place = lax.axis_index("spec")
     for distance in range(count):
         target = lax.rem(place + distance, count)
         for half in range(halves):
@@ -250,11 +267,13 @@
                 outs[distance][pl.ds(part * lanes * halves + half, lanes, stride=halves), :] = tile[:lanes]
 
 
-def interact_kernel(per_source, halves, count, starts, partner, rate, *rest):
+def interact_kernel(per_source, halves, count, starts, partner_source, rate_source, *rest):
     pieces, rest = rest[: count * len(starts)], rest[count * len(starts) :]
-    target, energy, kept, added, out, done = rest[0], rest[1], rest[2], rest[3:-2], rest[-2], rest[-1]
+    target, energy, kept, added = rest[0], rest[1], rest[2], rest[3:-6]
+    out, done, partner, partner_done, rate, rate_done = rest[-6:]
+    pending = listed_in(partner_source, partner, partner_done), listed_in(rate_source, rate, rate_done)
     bins = rate.shape[0]
-    place = partner[2 * bins]
+    place = lax.axis_index("spec")
     clear(added)
     for which, start in enumerate(starts):
         for distance in range(count):
@@ -263,6 +282,8 @@
             if per_source % 8 == 0 and start % 8 == 0:
                 first = pl.multiple_of(first, 8)
             energy[pl.ds(first, piece.shape[0]), :] = piece[...]
+    for item in pending:
+        item.wait()
     share = bins // GROUPS
     unroll = chunked(share, 18)
 
@@ -334,9 +355,7 @@
     halves = owned // (spec_count * LANES)
 
     nodes = (conn * sub).reshape(-1)
-    place = lax.axis_index("spec").reshape(1)
     send = (send_nodes[0] * sub).reshape(-1)
-    listing = jnp.concatenate([send, place])
 
     bin_of = (
         lax.axis_index("spec") * row_count
@@ -363,9 +382,9 @@
     full, *outs = pl.pallas_call(
         functools.partial(enter_kernel, sub, lanes),
         out_shape=[full_shape] + block_shapes,
-        in_specs=[SM, VM],
+        in_specs=[ANY, VM],
         out_specs=[VM] * (1 + BLOCKS),
-        scratch_shapes=[squares, stages],
+        scratch_shapes=[squares, stages] + list_scratch(BLOCKS * slots),
         cost_estimate=cost(0, 2 * moved),
         compiler_params=limit(4),
         name="enter",
@@ -391,10 +410,10 @@
         full, *returned = pl.pallas_call(
             functools.partial(sweep_kernel, sub, inner, groups, lanes, shared, own_rows),
             out_shape=[full_shape] + blocks_of(groups),
-            in_specs=[SM] + [VM] * (3 + len(ghosts)),
+            in_specs=[ANY] + [VM] * (3 + len(ghosts)),
             out_specs=[VM] * (1 + BLOCKS * len(groups)),
             input_output_aliases={3 + len(ghosts): 0},
-            scratch_shapes=[squares, stages] + sums,
+            scratch_shapes=[squares, stages] + list_scratch(3 * elements) + sums,
             cost_estimate=cost(elements * 24 * row_count, 4 * LANES * (3 * elements + 4 * rows)),
             compiler_params=limit(20),
             name="sweep",
@@ -408,10 +427,10 @@
                 full, *more = pl.pallas_call(
                     functools.partial(between_kernel, parts, lanes),
                     out_shape=[full_shape] + blocks_of((parts,)),
-                    in_specs=[SM] + [VM] * (2 + BLOCKS),
+                    in_specs=[ANY] + [VM] * (2 + BLOCKS),
                     out_specs=[VM] * (1 + BLOCKS),
                     input_output_aliases={2 + BLOCKS: 0},
-                    scratch_shapes=[squares, stages],
+                    scratch_shapes=[squares, stages] + list_scratch(BLOCKS * slots),
                     cost_estimate=cost(2 * owned * parts[1] * LANES, 4 * moved * parts[1] // sub),
                     compiler_params=limit(4),
                 )(send, weight, *incoming[which * BLOCKS : (which + 1) * BLOCKS], full)
@@ -422,25 +441,29 @@
         full, *blocks = pl.pallas_call(
             functools.partial(leave_kernel, sub, (start, size), lanes, halves, spec_count),
             out_shape=[full_shape] + [shape_of(size * lanes * halves, LANES)] * spec_count,
-            in_specs=[SM] + [VM] * (2 + BLOCKS),
+            in_specs=[ANY] + [VM] * (2 + BLOCKS),
             out_specs=[VM] * (1 + spec_count),
             input_output_aliases={2 + BLOCKS: 0},
-            scratch_shapes=[squares, stages],
+            scratch_shapes=[squares, stages] + list_scratch(BLOCKS * slots),
             cost_estimate=cost(2 * owned * size * LANES, 3 * moved * size // sub),
             compiler_params=limit(4),
-        )(listing, weight, *incoming[which * BLOCKS : (which + 1) * BLOCKS], full)
-        pieces += [blocks[0]] + [passed_along(blocks[d], "spec", d) for d in range(1, spec_count)]
+        )(send, weight, *incoming[which * BLOCKS : (which + 1) * BLOCKS], full)
+        pieces.append(blocks[0])
+        for distance in range(1, spec_count):
+            pieces.append(passed_along(blocks[distance], "spec", distance))
     return pl.pallas_call(
         functools.partial(interact_kernel, row_count * halves, halves, spec_count, [s * lanes * halves for s, _ in groups]),
         out_shape=shape_of(bins, halves * LANES),
-        in_specs=[SM] * 2 + [VM] * len(pieces),
+        in_specs=[ANY] * 2 + [VM] * len(pieces),
         out_specs=pl.BlockSpec(memory_space=pl.ANY),
         scratch_shapes=[pltpu.VMEM((bins * halves, LANES), jnp.float32)] * (2 + 2 * GROUPS)
-        + [pltpu.VMEM((bins, halves * LANES), jnp.float32), pltpu.SemaphoreType.DMA((chunked(bins // 48, 4),))],
+        + [pltpu.VMEM((bins, halves * LANES), jnp.float32), pltpu.SemaphoreType.DMA((chunked(bins // 48, 4),))]
+        + list_scratch(2 * bins)
+        + list_scratch(bins, jnp.float32),
         cost_estimate=cost(16 * bins * halves * LANES, 8 * bins * halves * LANES),
         compiler_params=limit(12),
         name="interact",
-    )(jnp.concatenate([dia_plus * halves, dia_minus * halves, place]), dia_coeff, *pieces)
+    )(jnp.concatenate([dia_plus, dia_minus]) * halves, dia_coeff, *pieces)
 
 
 def solution(mesh):

time: 124 us -> 128 us (1.032)
  the two profiles are of different devices: /device:TPU:9 before, /device:TPU:4 now
where the time goes in v7:
time: 128 us; the launch traced here: 126 us
  waiting for transfers between devices  42.7 us (33%)
  Pallas kernels  41.7 us (33%)
  starting transfers between devices  35.7 us (28%)
  local copies, waits for them, and re-layouts  2.88 us (2%)
  other arithmetic  2.49 us (2%)
    ppermute x34, waiting for transfers between devices, passed_along(): lax.ppermute(value, axis, [(source, (source + steps) % count) for source...  42.7 us
    ppermute x34, starting transfers between devices, passed_along(): lax.ppermute(value, axis, [(source, (source + steps) % count) for source...  35.7 us
    pallas_call x2, Pallas kernels, on_device(): pl.pallas_call(functools.partial(sweep_kernel, sub, inner, groups, lanes,...  20.1 us
    pallas_call x1, Pallas kernels, on_device(): pl.pallas_call(functools.partial(interact_kernel, row_count * halves, hal...  6.24 us
    pallas_call x1, Pallas kernels, on_device(): pl.pallas_call(functools.partial(slope_kernel, sub, shared), out_shape=[s...  4.88 us
    pallas_call x2, Pallas kernels, on_device(): pl.pallas_call(functools.partial(between_kernel, parts, lanes), out_shape...  4.63 us
    pallas_call x2, Pallas kernels, on_device(): pl.pallas_call(functools.partial(leave_kernel, sub, (start, size), lanes,...  3.87 us
    unnamed x11, local copies, waits for them, and re-layouts  2.86 us
  transfers between devices with their start and end apart: 34, of which 6 were waited for; matrix products, arithmetic and copies ran while one was open for 2% of the time, Pallas kernels for 11%

profile of v7, /device:TPU:4, one launch (start us, length us, event | category | flops | bytes accessed | tf_op | source)
XLA Modules:
  0.0 125.7 jit_solution(296924109067400639)
XLA Ops:
  2.0 2.0 %enter.1 = (f32[4608,128]{1,0:T(8,128)S(1)}, f32[324,128]{1,0:T(8,128)}, f32[324,128]{1,0:T(8,128)}, f32[324,128]{1,0:T(8,128)S(1)}, f32[324,128]{1,0:T(8,128)S(1)}) custom-call(s32[512]{0:T(512)S(1)} %multiply_bitcast_fusion.source, f32[324,1024]{1,0:T(8,128)S(1)} %copy-done), custom_call_target="tpu_custom_call" | custom-call | bytes 3145728 | tf_op jit(solution)/shard_map/enter/pallas_call | solution.py:382
  5.5 2.6 %collective-permute-start.2 = (f32[324,128]{1,0:T(8,128)S(1)}, f32[324,128]{1,0:T(8,128)S(1)}, u32[]{:S(2)}, u32[]{:S(2)}) collective-permute-start(f32[324,128]{1,0:T(8,128)S(1)} %get-tuple-element.53), channel_id=1, source_target_pairs={{0,28},{4,0},{8,4},{12,8},{16,12},{20,16},{24,20},{28,24},{1,29},{... | collective-permute-start | bytes 497672 | tf_op jit(solution)/shard_map/ppermute | solution.py:34
  12.0 4.9 %slopes.1 = (f32[6144,128]{1,0:T(8,128)S(1)}, f32[3072,128]{1,0:T(8,128)S(1)}) custom-call(f32[2,3,2048]{2,1,0:T(4,128)S(1)} %copy.17.normals, f32[1,1024]{1,0:T(1,128)S(1)} %bitcast.3, f32[9,128]{1,0:T(8,128)S(1)} %pad_maximum_fusion.wave), custom_call_target="tpu_custom_call" | custom-call | flops 5242880 | bytes 4718592 | tf_op jit(solution)/shard_map/slopes/pallas_call | solution.py:393
  17.2 10.0 %sweep.2 = (f32[4608,128]{1,0:T(8,128)S(1)}, f32[108,128]{1,0:T(8,128)S(1)}, f32[108,128]{1,0:T(8,128)S(1)}, f32[108,128]{1,0:T(8,128)S(1)}, f32[108,128]{1,0:T(...) custom-call(s32[6144]{0:T(1024)S(1)} %reshape.47.source, ...), custom_call_target="tpu_custom_call", output_to_operand_aliasing={{0}: (7, {})} | custom-call | flops 15925248 | bytes 12582912 | tf_op jit(solution)/shard_map/sweep/pallas_call | solution.py:410
  27.3 2.7 %collective-permute-start.4 = (f32[108,128]{1,0:T(8,128)S(1)}, f32[108,128]{1,0:T(8,128)S(1)}, u32[]{:S(2)}, u32[]{:S(2)}) collective-permute-start(f32[108,128]{1,0:T(8,128)S(1)} %get-tuple-element.56), channel_id=1, source_target_pairs={{0,24},{4,28},{8,0},{12,4},{16,8},{20,12},{24,16},{28,20},{1,25},{... | collective-permute-start | bytes 165896 | tf_op jit(solution)/shard_map/ppermute | solution.py:34
  31.0 1.6 %collective-permute-start.13 = (f32[216,128]{1,0:T(8,128)S(1)}, f32[216,128]{1,0:T(8,128)S(1)}, u32[]{:S(2)}, u32[]{:S(2)}) collective-permute-start(f32[216,128]{1,0:T(8,128)S(1)} %get-tuple-element.66), channel_id=1, source_target_pairs={{0,28},{4,0},{8,4},{12,8},{16,12},{20,16},{24,20},{28,24},{1,29},{... | collective-permute-start | bytes 331784 | tf_op jit(solution)/shard_map/ppermute | solution.py:34
  32.7 2.0 %collective-permute-start.15 = (f32[216,128]{1,0:T(8,128)S(1)}, f32[216,128]{1,0:T(8,128)S(1)}, u32[]{:S(2)}, u32[]{:S(2)}) collective-permute-start(f32[216,128]{1,0:T(8,128)S(1)} %get-tuple-element.68), channel_id=1, source_target_pairs={{0,8},{4,12},{8,16},{12,20},{16,24},{20,28},{24,0},{28,4},{1,9},{5... | collective-permute-start | bytes 331784 | tf_op jit(solution)/shard_map/ppermute | solution.py:34
  34.9 7.4 %collective-permute-done.7.rest_3_ = f32[108,128]{1,0:T(8,128)S(1)} collective-permute-done((f32[108,128]{1,0:T(8,128)S(1)}, f32[108,128]{1,0:T(8,128)S(1)}, u32[]{:S(2)}, u32[]{:S(2)}) %collective-permute-start.7) | collective-permute-done | bytes 55328 | tf_op jit(solution)/shard_map/ppermute | solution.py:34
  42.3 2.3 %shard_map.91 = (f32[4608,128]{1,0:T(8,128)S(1)}, f32[108,128]{1,0:T(8,128)S(1)}, f32[108,128]{1,0:T(8,128)S(1)}, f32[108,128]{1,0:T(8,128)S(1)}, f32[108,128]{1,0:T(8,128)S(1)}) custom-call(s32[512]{0:T(512)S(1)} %multiply_bitcast_fusion.source, f32[3072,128]{1,0:T(8,128)S(1)} %get-tuple-element.49.weight, ...), custom_call_target="tpu_custom_call", output_to_operand_aliasing={{0}: (6, {})} | custom-call | flops 262144 | bytes 2097152 | tf_op jit(solution)/shard_map/pallas_call | solution.py:427
  47.5 2.4 %shard_map.92 = (f32[4608,128]{1,0:T(8,128)S(1)}, f32[216,128]{1,0:T(8,128)S(1)}, f32[216,128]{1,0:T(8,128)S(1)}, f32[216,128]{1,0:T(8,128)S(1)}, f32[216,128]{1,0:T(8,128)S(1)}) custom-call(s32[512]{0:T(512)S(1)} %multiply_bitcast_fusion.source, f32[3072,128]{1,0:T(8,128)S(1)} %get-tuple-element.49.weight, ...), custom_call_target="tpu_custom_call", output_to_operand_aliasing={{0}: (6, {})} | custom-call | flops 524288 | bytes 4194304 | tf_op jit(solution)/shard_map/pallas_call | solution.py:427
  49.8 2.1 %collective-permute-start.16 = (f32[216,128]{1,0:T(8,128)S(1)}, f32[216,128]{1,0:T(8,128)S(1)}, u32[]{:S(2)}, u32[]{:S(2)}) collective-permute-start(f32[216,128]{1,0:T(8,128)S(1)} %get-tuple-element.70), channel_id=1, source_target_pairs={{0,8},{4,12},{8,16},{12,20},{16,24},{20,28},{24,0},{28,4},{1,9},{5... | collective-permute-start | bytes 331784 | tf_op jit(solution)/shard_map/ppermute | solution.py:34
  51.9 2.6 %collective-permute-start.18 = (f32[216,128]{1,0:T(8,128)S(1)}, f32[216,128]{1,0:T(8,128)S(1)}, u32[]{:S(2)}, u32[]{:S(2)}) collective-permute-start(f32[216,128]{1,0:T(8,128)S(1)} %get-tuple-element.72), channel_id=1, source_target_pairs={{0,28},{4,0},{8,4},{12,8},{16,12},{20,16},{24,20},{28,24},{1,29},{... | collective-permute-start | bytes 331784 | tf_op jit(solution)/shard_map/ppermute | solution.py:34
  54.8 6.4 %collective-permute-done.9.rest_1_ = f32[108,128]{1,0:T(8,128)S(1)} collective-permute-done((f32[108,128]{1,0:T(8,128)S(1)}, f32[108,128]{1,0:T(8,128)S(1)}, u32[]{:S(2)}, u32[]{:S(2)}) %collective-permute-start.9) | collective-permute-done | bytes 55328 | tf_op jit(solution)/shard_map/ppermute | solution.py:34
  61.2 10.1 %sweep.3 = (f32[4608,128]{1,0:T(8,128)S(1)}, f32[108,128]{1,0:T(8,128)S(1)}, f32[108,128]{1,0:T(8,128)S(1)}, f32[108,128]{1,0:T(8,128)S(1)}, f32[108,128]{1,0:T(...) custom-call(s32[6144]{0:T(1024)S(1)} %reshape.47.source, ...), custom_call_target="tpu_custom_call", output_to_operand_aliasing={{0}: (11, {})} | custom-call | flops 15925248 | bytes 12582912 | tf_op jit(solution)/shard_map/sweep/pallas_call | solution.py:410
  71.3 1.8 %collective-permute-start.20 = (f32[108,128]{1,0:T(8,128)S(1)}, f32[108,128]{1,0:T(8,128)S(1)}, u32[]{:S(2)}, u32[]{:S(2)}) collective-permute-start(f32[108,128]{1,0:T(8,128)S(1)} %get-tuple-element.75), channel_id=1, source_target_pairs={{0,24},{4,28},{8,0},{12,4},{16,8},{20,12},{24,16},{28,20},{1,25},{... | collective-permute-start | bytes 165896 | tf_op jit(solution)/shard_map/ppermute | solution.py:34
  75.8 2.2 %collective-permute-start.30 = (f32[216,128]{1,0:T(8,128)S(1)}, f32[216,128]{1,0:T(8,128)S(1)}, u32[]{:S(2)}, u32[]{:S(2)}) collective-permute-start(f32[216,128]{1,0:T(8,128)S(1)} %get-tuple-element.87), channel_id=1, source_target_pairs={{0,8},{4,12},{8,16},{12,20},{16,24},{20,28},{24,0},{28,4},{1,9},{5... | collective-permute-start | bytes 331784 | tf_op jit(solution)/shard_map/ppermute | solution.py:34
  78.2 7.5 %collective-permute-done.23.rest_3_ = f32[108,128]{1,0:T(8,128)S(1)} collective-permute-done((f32[108,128]{1,0:T(8,128)S(1)}, f32[108,128]{1,0:T(8,128)S(1)}, u32[]{:S(2)}, u32[]{:S(2)}) %collective-permute-start.23) | collective-permute-done | bytes 55328 | tf_op jit(solution)/shard_map/ppermute | solution.py:34
  85.7 1.9 %shard_map.93 = (f32[4608,128]{1,0:T(8,128)S(1)}, f32[216,128]{1,0:T(8,128)S(1)}, f32[216,128]{1,0:T(8,128)S(1)}, f32[216,128]{1,0:T(8,128)S(1)}, f32[216,128]{1,0:T(8,128)S(1)}) custom-call(s32[512]{0:T(512)S(1)} %multiply_bitcast_fusion.source, f32[3072,128]{1,0:T(8,128)S(1)} %get-tuple-element.49.weight, ...), custom_call_target="tpu_custom_call", output_to_operand_aliasing={{0}: (6, {})} | custom-call | flops 262144 | bytes 1572864 | tf_op jit(solution)/shard_map/pallas_call | solution.py:441
  87.6 1.6 %collective-permute-start.24 = (f32[216,128]{1,0:T(8,128)S(1)}, f32[216,128]{1,0:T(8,128)S(1)}, u32[]{:S(2)}, u32[]{:S(2)}) collective-permute-start(f32[216,128]{1,0:T(8,128)S(1)} %get-tuple-element.81), channel_id=1, source_target_pairs={{0,1},{1,2},{2,3},{3,0},{4,5},{5,6},{6,7},{7,4},{8,9},{9,10},{10,1... | collective-permute-start | bytes 331784 | tf_op jit(solution)/shard_map/ppermute | solution.py:34
  89.2 2.0 %shard_map.94 = (f32[4608,128]{1,0:T(8,128)S(1)}, f32[432,128]{1,0:T(8,128)S(1)}, f32[432,128]{1,0:T(8,128)S(1)}, f32[432,128]{1,0:T(8,128)S(1)}, f32[432,128]{1,0:T(8,128)S(1)}) custom-call(s32[512]{0:T(512)S(1)} %multiply_bitcast_fusion.source, f32[3072,128]{1,0:T(8,128)S(1)} %get-tuple-element.49.weight, ...), custom_call_target="tpu_custom_call", output_to_operand_aliasing={{0}: (6, {})} | custom-call | flops 524288 | bytes 3145728 | tf_op jit(solution)/shard_map/pallas_call | solution.py:441
  91.2 1.6 %collective-permute-start.31 = (f32[432,128]{1,0:T(8,128)S(1)}, f32[432,128]{1,0:T(8,128)S(1)}, u32[]{:S(2)}, u32[]{:S(2)}) collective-permute-start(f32[432,128]{1,0:T(8,128)S(1)} %get-tuple-element.90), channel_id=1, source_target_pairs={{0,1},{1,2},{2,3},{3,0},{4,5},{5,6},{6,7},{7,4},{8,9},{9,10},{10,1... | collective-permute-start | bytes 663560 | tf_op jit(solution)/shard_map/ppermute | solution.py:34
  94.1 2.7 %collective-permute-start.33 = (f32[432,128]{1,0:T(8,128)S(1)}, f32[432,128]{1,0:T(8,128)S(1)}, u32[]{:S(2)}, u32[]{:S(2)}) collective-permute-start(f32[432,128]{1,0:T(8,128)S(1)} %get-tuple-element.92), channel_id=1, source_target_pairs={{0,3},{1,0},{2,1},{3,2},{4,7},{5,4},{6,5},{7,6},{8,11},{9,8},{10,9... | collective-permute-start | bytes 663560 | tf_op jit(solution)/shard_map/ppermute | solution.py:34
  98.6 20.8 %collective-permute-done.25.rest_2_ = f32[216,128]{1,0:T(8,128)S(1)} collective-permute-done((f32[216,128]{1,0:T(8,128)S(1)}, f32[216,128]{1,0:T(8,128)S(1)}, u32[]{:S(2)}, u32[]{:S(2)}) %collective-permute-start.25) | collective-permute-done | bytes 110624 | tf_op jit(solution)/shard_map/ppermute | solution.py:34
  119.4 6.2 %interact.1 = f32[1296,256]{1,0:T(8,128)} custom-call(s32[2592]{0:T(1024)S(1)} %add_multiply_fusion.partner_source, f32[1296]{0:T(1024)S(1)} %copy-done.1, f32[216,128]{1,0:T(8,128)S(1)} %get-tuple-element.80.rest_0_, f32[216,128]{1,0:T(8,128)S(1)} %collective-permute-done.24.rest_1_, f32[216,128]{1,0:T(8,128)S(1)} %collective-permute-done.25.rest_2_, ...), custom_call_target="tpu_custom_call" | custom-call | flops 5308416 | bytes 2654208 | tf_op jit(solution)/shard_map/interact/pallas_call | solution.py:454
  (73 shorter events, 18.1 us)
Async XLA Ops:
  4.0 12.9 %collective-permute-start = (f32[324,128]{1,0:T(8,128)}, f32[324,128]{1,0:T(8,128)S(1)}, u32[]{:S(2)}, u32[]{:S(2)}) collective-permute-start(f32[324,128]{1,0:T(8,128)} %get-tuple-element.51), channel_id=1, source_target_pairs={{0,8},{4,12},{8,16},{12,20},{16,24},{20,28},{24,0},{28,4},{1,9},{5... | collective-permute-start | bytes 497672 | tf_op jit(solution)/shard_map/ppermute | solution.py:34
  5.5 11.4 %collective-permute-start.1 = (f32[324,128]{1,0:T(8,128)}, f32[324,128]{1,0:T(8,128)S(1)}, u32[]{:S(2)}, u32[]{:S(2)}) collective-permute-start(f32[324,128]{1,0:T(8,128)} %get-tuple-element.52), channel_id=1, source_target_pairs={{0,4},{4,8},{8,12},{12,16},{16,20},{20,24},{24,28},{28,0},{1,5},{5... | collective-permute-start | bytes 497672 | tf_op jit(solution)/shard_map/ppermute | solution.py:34
  5.5 11.4 %collective-permute-start.2 = (f32[324,128]{1,0:T(8,128)S(1)}, f32[324,128]{1,0:T(8,128)S(1)}, u32[]{:S(2)}, u32[]{:S(2)}) collective-permute-start(f32[324,128]{1,0:T(8,128)S(1)} %get-tuple-element.53), channel_id=1, source_target_pairs={{0,28},{4,0},{8,4},{12,8},{16,12},{20,16},{24,20},{28,24},{1,29},{... | collective-permute-start | bytes 497672 | tf_op jit(solution)/shard_map/ppermute | solution.py:34
  8.2 9.0 %collective-permute-start.3 = (f32[324,128]{1,0:T(8,128)S(1)}, f32[324,128]{1,0:T(8,128)S(1)}, u32[]{:S(2)}, u32[]{:S(2)}) collective-permute-start(f32[324,128]{1,0:T(8,128)S(1)} %get-tuple-element.54), channel_id=1, source_target_pairs={{0,24},{4,28},{8,0},{12,4},{16,8},{20,12},{24,16},{28,20},{1,25},{... | collective-permute-start | bytes 497672 | tf_op jit(solution)/shard_map/ppermute | solution.py:34
  30.5 15.0 %collective-permute-start.12 = (f32[216,128]{1,0:T(8,128)S(1)}, f32[216,128]{1,0:T(8,128)S(1)}, u32[]{:S(2)}, u32[]{:S(2)}) collective-permute-start(f32[216,128]{1,0:T(8,128)S(1)} %get-tuple-element.65), channel_id=1, source_target_pairs={{0,24},{4,28},{8,0},{12,4},{16,8},{20,12},{24,16},{28,20},{1,25},{... | collective-permute-start | bytes 331784 | tf_op jit(solution)/shard_map/ppermute | solution.py:34
  31.0 15.8 %collective-permute-start.13 = (f32[216,128]{1,0:T(8,128)S(1)}, f32[216,128]{1,0:T(8,128)S(1)}, u32[]{:S(2)}, u32[]{:S(2)}) collective-permute-start(f32[216,128]{1,0:T(8,128)S(1)} %get-tuple-element.66), channel_id=1, source_target_pairs={{0,28},{4,0},{8,4},{12,8},{16,12},{20,16},{24,20},{28,24},{1,29},{... | collective-permute-start | bytes 331784 | tf_op jit(solution)/shard_map/ppermute | solution.py:34
  32.6 14.8 %collective-permute-start.14 = (f32[216,128]{1,0:T(8,128)S(1)}, f32[216,128]{1,0:T(8,128)S(1)}, u32[]{:S(2)}, u32[]{:S(2)}) collective-permute-start(f32[216,128]{1,0:T(8,128)S(1)} %get-tuple-element.67), channel_id=1, source_target_pairs={{0,4},{4,8},{8,12},{12,16},{16,20},{20,24},{24,28},{28,0},{1,5},{5... | collective-permute-start | bytes 331784 | tf_op jit(solution)/shard_map/ppermute | solution.py:34
  32.7 14.7 %collective-permute-start.15 = (f32[216,128]{1,0:T(8,128)S(1)}, f32[216,128]{1,0:T(8,128)S(1)}, u32[]{:S(2)}, u32[]{:S(2)}) collective-permute-start(f32[216,128]{1,0:T(8,128)S(1)} %get-tuple-element.68), channel_id=1, source_target_pairs={{0,8},{4,12},{8,16},{12,20},{16,24},{20,28},{24,0},{28,4},{1,9},{5... | collective-permute-start | bytes 331784 | tf_op jit(solution)/shard_map/ppermute | solution.py:34
  45.4 9.2 %collective-permute-start.11 = (f32[108,128]{1,0:T(8,128)S(1)}, f32[108,128]{1,0:T(8,128)S(1)}, u32[]{:S(2)}, u32[]{:S(2)}) collective-permute-start(f32[108,128]{1,0:T(8,128)S(1)} %get-tuple-element.64), channel_id=1, source_target_pairs={{0,24},{4,28},{8,0},{12,4},{16,8},{20,12},{24,16},{28,20},{1,25},{... | collective-permute-start | bytes 165896 | tf_op jit(solution)/shard_map/ppermute | solution.py:34
  46.8 7.8 %collective-permute-start.8 = (f32[108,128]{1,0:T(8,128)S(1)}, f32[108,128]{1,0:T(8,128)S(1)}, u32[]{:S(2)}, u32[]{:S(2)}) collective-permute-start(f32[108,128]{1,0:T(8,128)S(1)} %get-tuple-element.61), channel_id=1, source_target_pairs={{0,8},{4,12},{8,16},{12,20},{16,24},{20,28},{24,0},{28,4},{1,9},{5... | collective-permute-start | bytes 165896 | tf_op jit(solution)/shard_map/ppermute | solution.py:34
  49.8 11.4 %collective-permute-start.16 = (f32[216,128]{1,0:T(8,128)S(1)}, f32[216,128]{1,0:T(8,128)S(1)}, u32[]{:S(2)}, u32[]{:S(2)}) collective-permute-start(f32[216,128]{1,0:T(8,128)S(1)} %get-tuple-element.70), channel_id=1, source_target_pairs={{0,8},{4,12},{8,16},{12,20},{16,24},{20,28},{24,0},{28,4},{1,9},{5... | collective-permute-start | bytes 331784 | tf_op jit(solution)/shard_map/ppermute | solution.py:34
  51.9 9.2 %collective-permute-start.17 = (f32[216,128]{1,0:T(8,128)S(1)}, f32[216,128]{1,0:T(8,128)S(1)}, u32[]{:S(2)}, u32[]{:S(2)}) collective-permute-start(f32[216,128]{1,0:T(8,128)S(1)} %get-tuple-element.71), channel_id=1, source_target_pairs={{0,4},{4,8},{8,12},{12,16},{16,20},{20,24},{24,28},{28,0},{1,5},{5... | collective-permute-start | bytes 331784 | tf_op jit(solution)/shard_map/ppermute | solution.py:34
  51.9 9.2 %collective-permute-start.18 = (f32[216,128]{1,0:T(8,128)S(1)}, f32[216,128]{1,0:T(8,128)S(1)}, u32[]{:S(2)}, u32[]{:S(2)}) collective-permute-start(f32[216,128]{1,0:T(8,128)S(1)} %get-tuple-element.72), channel_id=1, source_target_pairs={{0,28},{4,0},{8,4},{12,8},{16,12},{20,16},{24,20},{28,24},{1,29},{... | collective-permute-start | bytes 331784 | tf_op jit(solution)/shard_map/ppermute | solution.py:34
  73.6 15.6 %collective-permute-start.27 = (f32[216,128]{1,0:T(8,128)S(1)}, f32[216,128]{1,0:T(8,128)S(1)}, u32[]{:S(2)}, u32[]{:S(2)}) collective-permute-start(f32[216,128]{1,0:T(8,128)S(1)} %get-tuple-element.84), channel_id=1, source_target_pairs={{0,24},{4,28},{8,0},{12,4},{16,8},{20,12},{24,16},{28,20},{1,25},{... | collective-permute-start | bytes 331784 | tf_op jit(solution)/shard_map/ppermute | solution.py:34
  74.4 14.9 %collective-permute-start.28 = (f32[216,128]{1,0:T(8,128)S(1)}, f32[216,128]{1,0:T(8,128)S(1)}, u32[]{:S(2)}, u32[]{:S(2)}) collective-permute-start(f32[216,128]{1,0:T(8,128)S(1)} %get-tuple-element.85), channel_id=1, source_target_pairs={{0,28},{4,0},{8,4},{12,8},{16,12},{20,16},{24,20},{28,24},{1,29},{... | collective-permute-start | bytes 331784 | tf_op jit(solution)/shard_map/ppermute | solution.py:34
  75.7 13.5 %collective-permute-start.29 = (f32[216,128]{1,0:T(8,128)S(1)}, f32[216,128]{1,0:T(8,128)S(1)}, u32[]{:S(2)}, u32[]{:S(2)}) collective-permute-start(f32[216,128]{1,0:T(8,128)S(1)} %get-tuple-element.86), channel_id=1, source_target_pairs={{0,4},{4,8},{8,12},{12,16},{16,20},{20,24},{24,28},{28,0},{1,5},{5... | collective-permute-start | bytes 331784 | tf_op jit(solution)/shard_map/ppermute | solution.py:34
  75.8 13.4 %collective-permute-start.30 = (f32[216,128]{1,0:T(8,128)S(1)}, f32[216,128]{1,0:T(8,128)S(1)}, u32[]{:S(2)}, u32[]{:S(2)}) collective-permute-start(f32[216,128]{1,0:T(8,128)S(1)} %get-tuple-element.87), channel_id=1, source_target_pairs={{0,8},{4,12},{8,16},{12,20},{16,24},{20,28},{24,0},{28,4},{1,9},{5... | collective-permute-start | bytes 331784 | tf_op jit(solution)/shard_map/ppermute | solution.py:34
  78.0 7.6 %collective-permute-start.23 = (f32[108,128]{1,0:T(8,128)S(1)}, f32[108,128]{1,0:T(8,128)S(1)}, u32[]{:S(2)}, u32[]{:S(2)}) collective-permute-start(f32[108,128]{1,0:T(8,128)S(1)} %get-tuple-element.78), channel_id=1, source_target_pairs={{0,8},{4,12},{8,16},{12,20},{16,24},{20,28},{24,0},{28,4},{1,9},{5... | collective-permute-start | bytes 165896 | tf_op jit(solution)/shard_map/ppermute | solution.py:34
  87.6 9.6 %collective-permute-start.24 = (f32[216,128]{1,0:T(8,128)S(1)}, f32[216,128]{1,0:T(8,128)S(1)}, u32[]{:S(2)}, u32[]{:S(2)}) collective-permute-start(f32[216,128]{1,0:T(8,128)S(1)} %get-tuple-element.81), channel_id=1, source_target_pairs={{0,1},{1,2},{2,3},{3,0},{4,5},{5,6},{6,7},{7,4},{8,9},{9,10},{10,1... | collective-permute-start | bytes 331784 | tf_op jit(solution)/shard_map/ppermute | solution.py:34
  91.2 28.2 %collective-permute-start.31 = (f32[432,128]{1,0:T(8,128)S(1)}, f32[432,128]{1,0:T(8,128)S(1)}, u32[]{:S(2)}, u32[]{:S(2)}) collective-permute-start(f32[432,128]{1,0:T(8,128)S(1)} %get-tuple-element.90), channel_id=1, source_target_pairs={{0,1},{1,2},{2,3},{3,0},{4,5},{5,6},{6,7},{7,4},{8,9},{9,10},{10,1... | collective-permute-start | bytes 663560 | tf_op jit(solution)/shard_map/ppermute | solution.py:34
  92.9 26.5 %collective-permute-start.32 = (f32[432,128]{1,0:T(8,128)S(1)}, f32[432,128]{1,0:T(8,128)S(1)}, u32[]{:S(2)}, u32[]{:S(2)}) collective-permute-start(f32[432,128]{1,0:T(8,128)S(1)} %get-tuple-element.91), channel_id=1, source_target_pairs={{0,2},{1,3},{2,0},{3,1},{4,6},{5,7},{6,4},{7,5},{8,10},{9,11},{10,... | collective-permute-start | bytes 663560 | tf_op jit(solution)/shard_map/ppermute | solution.py:34
  94.1 25.3 %collective-permute-start.33 = (f32[432,128]{1,0:T(8,128)S(1)}, f32[432,128]{1,0:T(8,128)S(1)}, u32[]{:S(2)}, u32[]{:S(2)}) collective-permute-start(f32[432,128]{1,0:T(8,128)S(1)} %get-tuple-element.92), channel_id=1, source_target_pairs={{0,3},{1,0},{2,1},{3,2},{4,7},{5,4},{6,5},{7,6},{8,11},{9,8},{10,9... | collective-permute-start | bytes 663560 | tf_op jit(solution)/shard_map/ppermute | solution.py:34
  96.8 22.6 %collective-permute-start.25 = (f32[216,128]{1,0:T(8,128)S(1)}, f32[216,128]{1,0:T(8,128)S(1)}, u32[]{:S(2)}, u32[]{:S(2)}) collective-permute-start(f32[216,128]{1,0:T(8,128)S(1)} %get-tuple-element.82), channel_id=1, source_target_pairs={{0,2},{1,3},{2,0},{3,1},{4,6},{5,7},{6,4},{7,5},{8,10},{9,11},{10,... | collective-permute-start | bytes 331784 | tf_op jit(solution)/shard_map/ppermute | solution.py:34
  97.1 22.3 %collective-permute-start.26 = (f32[216,128]{1,0:T(8,128)S(1)}, f32[216,128]{1,0:T(8,128)S(1)}, u32[]{:S(2)}, u32[]{:S(2)}) collective-permute-start(f32[216,128]{1,0:T(8,128)S(1)} %get-tuple-element.83), channel_id=1, source_target_pairs={{0,3},{1,0},{2,1},{3,2},{4,7},{5,4},{6,5},{7,6},{8,11},{9,8},{10,9... | collective-permute-start | bytes 331784 | tf_op jit(solution)/shard_map/ppermute | solution.py:34
  (15 other events, 108.9 us)

commit v8 on v7

--- a/solution.py
+++ b/solution.py
@@ -55,12 +55,15 @@
             block[part * lanes : (part + 1) * lanes, column * LANES : (column + 1) * LANES] = tile[:lanes]
 
 
-def block_to_rows(sub, lanes, block, square, rows, first, start=0):
+def block_to_rows(sub, lanes, block, square, rows, first, start=0, factor=None):
     for column in range(block.shape[1] // LANES):
         for part in range(block.shape[0] // lanes):
             slot = square.at[(column * sub + part) % square.shape[0]]
             slot[:lanes, :] = block[part * lanes : (part + 1) * lanes, column * LANES : (column + 1) * LANES]
-            rows[pl.ds(first + column * LANES * sub + start + part, LANES, stride=sub), :] = slot[...].T
+            tile = slot[...].T
+            if factor is not None:
+                tile = tile * factor(column, part)
+            rows[pl.ds(first + column * LANES * sub + start + part, LANES, stride=sub), :] = tile
 
 
 def pack_rows(parts, lanes, send, full, stages, outs):
@@ -101,7 +104,8 @@
             item[pl.ds(pl.multiple_of(k * step, step), step), :] = zero
 
 
-def slope_kernel(sub, shared, normals, step_weight, wave, coef, weight, lines):
+def slope_kernel(sub, shared, source, normals, step_weight, wave, coef, weight, listed_weight, lines, send, done):
+    pending = listed_in(source, send, done)
     elements = normals.shape[2]
     parts = 1 if shared else sub
     plane = elements * parts
@@ -141,6 +145,15 @@
             for part in range(sub):
                 at = pl.ds((block * LANES + group * 8) * sub + part, 8, stride=sub)
                 weight[at, :] = value * wave[2 * sub + part : 2 * sub + part + 1, :]
+
+    pending.wait()
+    unroll = chunked(send.shape[0], 32)
+
+    @pl.loop(0, send.shape[0] // unroll)
+    def _(k):
+        listed = send.at[pl.ds(k * unroll, unroll)]
+        for u in range(unroll):
+            listed_weight[pl.ds((k * unroll + u) * sub, sub), :] = weight[pl.ds(listed[u], sub), :]
 
 
 def total(sums, at):
@@ -219,13 +232,18 @@
         full[at, :] = full[at, :] - weight[at, :] * total(sums, at)
 
 
-def add_returned(parts, lanes, pending, send, weight, incoming, square, stages, full):
+def add_returned(sub, parts, lanes, pending, send, listed_weight, incoming, square, stages, full):
     start, size = parts
     slots = incoming[0].shape[1]
     square[...] = jnp.zeros_like(square)
     unroll = chunked(slots, 16)
     for position in range(BLOCKS):
-        block_to_rows(size, lanes, incoming[position], square, stages.at[position], 0)
+        base = (BLOCKS - 1 - position) * slots * sub + start
+
+        def factor(column, part):
+            return listed_weight[pl.ds(base + column * LANES * sub + part, LANES, stride=sub), :]
+
+        block_to_rows(size, lanes, incoming[position], square, stages.at[position], 0, 0, factor)
     pending.wait()
     for position in range(BLOCKS):
         stage = stages.at[position]
@@ -235,27 +253,24 @@
             first = k * unroll
             listed = send.at[pl.ds((BLOCKS - 1 - position) * slots + first, unroll)]
             rows = [pl.ds(listed[u] + start, size) for u in range(unroll)]
-            fresh = [
-                full[row, :] - weight[row, :] * stage[pl.ds((first + u) * size, size), :]
-                for u, row in enumerate(rows)
-            ]
+            fresh = [full[row, :] - stage[pl.ds((first + u) * size, size), :] for u, row in enumerate(rows)]
             for row, item in zip(rows, fresh):
                 full[row, :] = item
 
 
-def between_kernel(parts, lanes, source, weight, *rest):
+def between_kernel(sub, parts, lanes, source, listed_weight, *rest):
     incoming, rest = rest[:BLOCKS], rest[BLOCKS + 1 :]
     full, outs, (square, stages, send, done) = rest[0], rest[1 : 1 + BLOCKS], rest[1 + BLOCKS :]
     pending = listed_in(source, send, done)
-    add_returned(parts, lanes, pending, send, weight, incoming, square, stages, full)
+    add_returned(sub, parts, lanes, pending, send, listed_weight, incoming, square, stages, full)
     pack_rows(parts, lanes, send, full, stages, outs)
 
 
-def leave_kernel(sub, parts, lanes, halves, count, source, weight, *rest):
+def leave_kernel(sub, parts, lanes, halves, count, source, listed_weight, *rest):
     incoming, rest = rest[:BLOCKS], rest[BLOCKS + 1 :]
     full, outs, (square, stages, send, done) = rest[0], rest[1 : 1 + count], rest[1 + count :]
     pending = listed_in(source, send, done)
-    add_returned(parts, lanes, pending, send, weight, incoming, square, stages, full)
+    add_returned(sub, parts, lanes, pending, send, listed_weight, incoming, square, stages, full)
     start, size = parts
     place = lax.axis_index("spec")
     for distance in range(count):
@@ -390,16 +405,16 @@
         name="enter",
     )(send, spectrum)
     pitch = 3 if shared else 3 * sub
-    coef, weight = pl.pallas_call(
+    coef, weight, listed_weight = pl.pallas_call(
         functools.partial(slope_kernel, sub, shared),
-        out_shape=[shape_of(elements * pitch, LANES), shape_of(own_rows, LANES)],
-        in_specs=[VM] * 3,
-        out_specs=[VM] * 2,
-        scratch_shapes=[pltpu.VMEM((LANES, elements), jnp.float32)],
+        out_shape=[shape_of(elements * pitch, LANES), shape_of(own_rows, LANES), shape_of(BLOCKS * ghost_rows, LANES)],
+        in_specs=[ANY] + [VM] * 3,
+        out_specs=[VM] * 3,
+        scratch_shapes=[pltpu.VMEM((LANES, elements), jnp.float32)] + list_scratch(BLOCKS * slots),
         cost_estimate=cost(20 * elements * LANES, 4 * LANES * (elements * pitch + own_rows)),
         compiler_params=limit(4),
         name="slopes",
-    )(normals, step_weight.reshape(1, owned), wave)
+    )(send, normals, step_weight.reshape(1, owned), wave)
 
     groups = whole if sub == 1 else ((0, 1), (1, sub - 1))
     inner = whole
@@ -425,7 +440,7 @@
             outs, inner = [], groups
             for which, parts in enumerate(groups):
                 full, *more = pl.pallas_call(
-                    functools.partial(between_kernel, parts, lanes),
+                    functools.partial(between_kernel, sub, parts, lanes),
                     out_shape=[full_shape] + blocks_of((parts,)),
                     in_specs=[ANY] + [VM] * (2 + BLOCKS),
                     out_specs=[VM] * (1 + BLOCKS),
@@ -433,7 +448,7 @@
                     scratch_shapes=[squares, stages] + list_scratch(BLOCKS * slots),
                     cost_estimate=cost(2 * owned * parts[1] * LANES, 4 * moved * parts[1] // sub),
                     compiler_params=limit(4),
-                )(send, weight, *incoming[which * BLOCKS : (which + 1) * BLOCKS], full)
+                )(send, listed_weight, *incoming[which * BLOCKS : (which + 1) * BLOCKS], full)
                 outs += more
 
     pieces = []
@@ -447,7 +462,7 @@
             scratch_shapes=[squares, stages] + list_scratch(BLOCKS * slots),
             cost_estimate=cost(2 * owned * size * LANES, 3 * moved * size // sub),
             compiler_params=limit(4),
-        )(send, weight, *incoming[which * BLOCKS : (which + 1) * BLOCKS], full)
+        )(send, listed_weight, *incoming[which * BLOCKS : (which + 1) * BLOCKS], full)
         pieces.append(blocks[0])
         for distance in range(1, spec_count):
             pieces.append(passed_along(blocks[distance], "spec", distance))

time: 128 us -> 127 us (level)
  transfers between devices with their start and end apart: 34 -> 34, of which waited for: 6 -> 5; matrix products, arithmetic and copies ran while one was open for 2% -> 2% of each run, Pallas kernels for 11% -> 10%
where the time goes in v8:
time: 127 us; the launch traced here: 125 us
  waiting for transfers between devices  42.4 us (33%)
  Pallas kernels  41.3 us (33%)
  starting transfers between devices  35.5 us (28%)
  local copies, waits for them, and re-layouts  2.88 us (2%)
  other arithmetic  2.49 us (2%)
    ppermute x34, waiting for transfers between devices, passed_along(): lax.ppermute(value, axis, [(source, (source + steps) % count) for source...  42.4 us
    ppermute x34, starting transfers between devices, passed_along(): lax.ppermute(value, axis, [(source, (source + steps) % count) for source...  35.5 us
    pallas_call x2, Pallas kernels, on_device(): pl.pallas_call(functools.partial(sweep_kernel, sub, inner, groups, lanes,...  20.1 us
    pallas_call x1, Pallas kernels, on_device(): pl.pallas_call(functools.partial(interact_kernel, row_count * halves, hal...  6.24 us
    pallas_call x1, Pallas kernels, on_device(): pl.pallas_call(functools.partial(slope_kernel, sub, shared), out_shape=[s...  5.38 us
    pallas_call x2, Pallas kernels, on_device(): pl.pallas_call(functools.partial(between_kernel, sub, parts, lanes), out_...  4.18 us
    pallas_call x2, Pallas kernels, on_device(): pl.pallas_call(functools.partial(leave_kernel, sub, (start, size), lanes,...  3.42 us
    unnamed x11, local copies, waits for them, and re-layouts  2.86 us
  transfers between devices with their start and end apart: 34, of which 5 were waited for; matrix products, arithmetic and copies ran while one was open for 2% of the time, Pallas kernels for 10%

profile of v8, /device:TPU:4, one launch (start us, length us, event | category | flops | bytes accessed | tf_op | source)
XLA Modules:
  0.0 124.8 jit_solution(5149144373957299121)
XLA Ops:
  2.0 2.0 %enter.1 = (f32[4608,128]{1,0:T(8,128)S(1)}, f32[324,128]{1,0:T(8,128)}, f32[324,128]{1,0:T(8,128)}, f32[324,128]{1,0:T(8,128)S(1)}, f32[324,128]{1,0:T(8,128)S(1)}) custom-call(s32[512]{0:T(512)S(1)} %multiply_bitcast_fusion.source, f32[324,1024]{1,0:T(8,128)S(1)} %copy-done), custom_call_target="tpu_custom_call" | custom-call | bytes 3145728 | tf_op jit(solution)/shard_map/enter/pallas_call | solution.py:397
  5.5 2.6 %collective-permute-start.2 = (f32[324,128]{1,0:T(8,128)S(1)}, f32[324,128]{1,0:T(8,128)S(1)}, u32[]{:S(2)}, u32[]{:S(2)}) collective-permute-start(f32[324,128]{1,0:T(8,128)S(1)} %get-tuple-element.55), channel_id=1, source_target_pairs={{0,28},{4,0},{8,4},{12,8},{16,12},{20,16},{24,20},{28,24},{1,29},{... | collective-permute-start | bytes 497672 | tf_op jit(solution)/shard_map/ppermute | solution.py:34
  12.0 5.4 %slopes.1 = (f32[6144,128]{1,0:T(8,128)S(1)}, f32[3072,128]{1,0:T(8,128)S(1)}, f32[1536,128]{1,0:T(8,128)S(1)}) custom-call(s32[512]{0:T(512)S(1)} %multiply_bitcast_fusion.source, f32[2,3,2048]{2,1,0:T(4,128)S(1)} %copy.17.normals, f32[1,1024]{1,0:T(1,128)S(1)} %bitcast.3, f32[9,128]{1,0:T(8,128)S(1)} %pad_maximum_fusion.wave), custom_call_target="tpu_custom_call" | custom-call | flops 5242880 | bytes 4718592 | tf_op jit(solution)/shard_map/slopes/pallas_call | solution.py:408
  17.4 10.0 %sweep.2 = (f32[4608,128]{1,0:T(8,128)S(1)}, f32[108,128]{1,0:T(8,128)S(1)}, f32[108,128]{1,0:T(8,128)S(1)}, f32[108,128]{1,0:T(8,128)S(1)}, f32[108,128]{1,0:T(...) custom-call(s32[6144]{0:T(1024)S(1)} %reshape.47.source, ...), custom_call_target="tpu_custom_call", output_to_operand_aliasing={{0}: (7, {})} | custom-call | flops 15925248 | bytes 12582912 | tf_op jit(solution)/shard_map/sweep/pallas_call | solution.py:425
  27.5 2.5 %collective-permute-start.4 = (f32[108,128]{1,0:T(8,128)S(1)}, f32[108,128]{1,0:T(8,128)S(1)}, u32[]{:S(2)}, u32[]{:S(2)}) collective-permute-start(f32[108,128]{1,0:T(8,128)S(1)} %get-tuple-element.58), channel_id=1, source_target_pairs={{0,24},{4,28},{8,0},{12,4},{16,8},{20,12},{24,16},{28,20},{1,25},{... | collective-permute-start | bytes 165896 | tf_op jit(solution)/shard_map/ppermute | solution.py:34
  31.0 1.6 %collective-permute-start.13 = (f32[216,128]{1,0:T(8,128)S(1)}, f32[216,128]{1,0:T(8,128)S(1)}, u32[]{:S(2)}, u32[]{:S(2)}) collective-permute-start(f32[216,128]{1,0:T(8,128)S(1)} %get-tuple-element.68), channel_id=1, source_target_pairs={{0,28},{4,0},{8,4},{12,8},{16,12},{20,16},{24,20},{28,24},{1,29},{... | collective-permute-start | bytes 331784 | tf_op jit(solution)/shard_map/ppermute | solution.py:34
  32.7 2.0 %collective-permute-start.15 = (f32[216,128]{1,0:T(8,128)S(1)}, f32[216,128]{1,0:T(8,128)S(1)}, u32[]{:S(2)}, u32[]{:S(2)}) collective-permute-start(f32[216,128]{1,0:T(8,128)S(1)} %get-tuple-element.70), channel_id=1, source_target_pairs={{0,8},{4,12},{8,16},{12,20},{16,24},{20,28},{24,0},{28,4},{1,9},{5... | collective-permute-start | bytes 331784 | tf_op jit(solution)/shard_map/ppermute | solution.py:34
  34.9 7.5 %collective-permute-done.7.rest_3_ = f32[108,128]{1,0:T(8,128)S(1)} collective-permute-done((f32[108,128]{1,0:T(8,128)S(1)}, f32[108,128]{1,0:T(8,128)S(1)}, u32[]{:S(2)}, u32[]{:S(2)}) %collective-permute-start.7) | collective-permute-done | bytes 55328 | tf_op jit(solution)/shard_map/ppermute | solution.py:34
  42.3 2.0 %shard_map.91 = (f32[4608,128]{1,0:T(8,128)S(1)}, f32[108,128]{1,0:T(8,128)S(1)}, f32[108,128]{1,0:T(8,128)S(1)}, f32[108,128]{1,0:T(8,128)S(1)}, f32[108,128]{1,0:T(8,128)S(1)}) custom-call(s32[512]{0:T(512)S(1)} %multiply_bitcast_fusion.source, f32[1536,128]{1,0:T(8,128)S(1)} %get-tuple-element.50.listed_weight, ...), custom_call_target="tpu_custom_call", output_to_operand_aliasing={{0}: (6, {})} | custom-call | flops 262144 | bytes 2097152 | tf_op jit(solution)/shard_map/pallas_call | solution.py:442
  47.2 2.1 %shard_map.92 = (f32[4608,128]{1,0:T(8,128)S(1)}, f32[216,128]{1,0:T(8,128)S(1)}, f32[216,128]{1,0:T(8,128)S(1)}, f32[216,128]{1,0:T(8,128)S(1)}, f32[216,128]{1,0:T(8,128)S(1)}) custom-call(s32[512]{0:T(512)S(1)} %multiply_bitcast_fusion.source, f32[1536,128]{1,0:T(8,128)S(1)} %get-tuple-element.50.listed_weight, ...), custom_call_target="tpu_custom_call", output_to_operand_aliasing={{0}: (6, {})} | custom-call | flops 524288 | bytes 4194304 | tf_op jit(solution)/shard_map/pallas_call | solution.py:442
  49.4 2.1 %collective-permute-start.16 = (f32[216,128]{1,0:T(8,128)S(1)}, f32[216,128]{1,0:T(8,128)S(1)}, u32[]{:S(2)}, u32[]{:S(2)}) collective-permute-start(f32[216,128]{1,0:T(8,128)S(1)} %get-tuple-element.72), channel_id=1, source_target_pairs={{0,8},{4,12},{8,16},{12,20},{16,24},{20,28},{24,0},{28,4},{1,9},{5... | collective-permute-start | bytes 331784 | tf_op jit(solution)/shard_map/ppermute | solution.py:34
  51.5 2.6 %collective-permute-start.18 = (f32[216,128]{1,0:T(8,128)S(1)}, f32[216,128]{1,0:T(8,128)S(1)}, u32[]{:S(2)}, u32[]{:S(2)}) collective-permute-start(f32[216,128]{1,0:T(8,128)S(1)} %get-tuple-element.74), channel_id=1, source_target_pairs={{0,28},{4,0},{8,4},{12,8},{16,12},{20,16},{24,20},{28,24},{1,29},{... | collective-permute-start | bytes 331784 | tf_op jit(solution)/shard_map/ppermute | solution.py:34
  54.3 6.4 %collective-permute-done.9.rest_1_ = f32[108,128]{1,0:T(8,128)S(1)} collective-permute-done((f32[108,128]{1,0:T(8,128)S(1)}, f32[108,128]{1,0:T(8,128)S(1)}, u32[]{:S(2)}, u32[]{:S(2)}) %collective-permute-start.9) | collective-permute-done | bytes 55328 | tf_op jit(solution)/shard_map/ppermute | solution.py:34
  60.7 10.1 %sweep.3 = (f32[4608,128]{1,0:T(8,128)S(1)}, f32[108,128]{1,0:T(8,128)S(1)}, f32[108,128]{1,0:T(8,128)S(1)}, f32[108,128]{1,0:T(8,128)S(1)}, f32[108,128]{1,0:T(...) custom-call(s32[6144]{0:T(1024)S(1)} %reshape.47.source, ...), custom_call_target="tpu_custom_call", output_to_operand_aliasing={{0}: (11, {})} | custom-call | flops 15925248 | bytes 12582912 | tf_op jit(solution)/shard_map/sweep/pallas_call | solution.py:425
  70.8 1.8 %collective-permute-start.20 = (f32[108,128]{1,0:T(8,128)S(1)}, f32[108,128]{1,0:T(8,128)S(1)}, u32[]{:S(2)}, u32[]{:S(2)}) collective-permute-start(f32[108,128]{1,0:T(8,128)S(1)} %get-tuple-element.77), channel_id=1, source_target_pairs={{0,24},{4,28},{8,0},{12,4},{16,8},{20,12},{24,16},{28,20},{1,25},{... | collective-permute-start | bytes 165896 | tf_op jit(solution)/shard_map/ppermute | solution.py:34
  75.4 2.2 %collective-permute-start.30 = (f32[216,128]{1,0:T(8,128)S(1)}, f32[216,128]{1,0:T(8,128)S(1)}, u32[]{:S(2)}, u32[]{:S(2)}) collective-permute-start(f32[216,128]{1,0:T(8,128)S(1)} %get-tuple-element.89), channel_id=1, source_target_pairs={{0,8},{4,12},{8,16},{12,20},{16,24},{20,28},{24,0},{28,4},{1,9},{5... | collective-permute-start | bytes 331784 | tf_op jit(solution)/shard_map/ppermute | solution.py:34
  77.8 7.5 %collective-permute-done.23.rest_3_ = f32[108,128]{1,0:T(8,128)S(1)} collective-permute-done((f32[108,128]{1,0:T(8,128)S(1)}, f32[108,128]{1,0:T(8,128)S(1)}, u32[]{:S(2)}, u32[]{:S(2)}) %collective-permute-start.23) | collective-permute-done | bytes 55328 | tf_op jit(solution)/shard_map/ppermute | solution.py:34
  85.2 1.6 %shard_map.93 = (f32[4608,128]{1,0:T(8,128)S(1)}, f32[216,128]{1,0:T(8,128)S(1)}, f32[216,128]{1,0:T(8,128)S(1)}, f32[216,128]{1,0:T(8,128)S(1)}, f32[216,128]{1,0:T(8,128)S(1)}) custom-call(s32[512]{0:T(512)S(1)} %multiply_bitcast_fusion.source, f32[1536,128]{1,0:T(8,128)S(1)} %get-tuple-element.50.listed_weight, ...), custom_call_target="tpu_custom_call", output_to_operand_aliasing={{0}: (6, {})} | custom-call | flops 262144 | bytes 1572864 | tf_op jit(solution)/shard_map/pallas_call | solution.py:456
  86.9 1.6 %collective-permute-start.24 = (f32[216,128]{1,0:T(8,128)S(1)}, f32[216,128]{1,0:T(8,128)S(1)}, u32[]{:S(2)}, u32[]{:S(2)}) collective-permute-start(f32[216,128]{1,0:T(8,128)S(1)} %get-tuple-element.83), channel_id=1, source_target_pairs={{0,1},{1,2},{2,3},{3,0},{4,5},{5,6},{6,7},{7,4},{8,9},{9,10},{10,1... | collective-permute-start | bytes 331784 | tf_op jit(solution)/shard_map/ppermute | solution.py:34
  88.5 1.8 %shard_map.94 = (f32[4608,128]{1,0:T(8,128)S(1)}, f32[432,128]{1,0:T(8,128)S(1)}, f32[432,128]{1,0:T(8,128)S(1)}, f32[432,128]{1,0:T(8,128)S(1)}, f32[432,128]{1,0:T(8,128)S(1)}) custom-call(s32[512]{0:T(512)S(1)} %multiply_bitcast_fusion.source, f32[1536,128]{1,0:T(8,128)S(1)} %get-tuple-element.50.listed_weight, ...), custom_call_target="tpu_custom_call", output_to_operand_aliasing={{0}: (6, {})} | custom-call | flops 524288 | bytes 3145728 | tf_op jit(solution)/shard_map/pallas_call | solution.py:456
  90.3 1.6 %collective-permute-start.31 = (f32[432,128]{1,0:T(8,128)S(1)}, f32[432,128]{1,0:T(8,128)S(1)}, u32[]{:S(2)}, u32[]{:S(2)}) collective-permute-start(f32[432,128]{1,0:T(8,128)S(1)} %get-tuple-element.92), channel_id=1, source_target_pairs={{0,1},{1,2},{2,3},{3,0},{4,5},{5,6},{6,7},{7,4},{8,9},{9,10},{10,1... | collective-permute-start | bytes 663560 | tf_op jit(solution)/shard_map/ppermute | solution.py:34
  93.2 2.7 %collective-permute-start.33 = (f32[432,128]{1,0:T(8,128)S(1)}, f32[432,128]{1,0:T(8,128)S(1)}, u32[]{:S(2)}, u32[]{:S(2)}) collective-permute-start(f32[432,128]{1,0:T(8,128)S(1)} %get-tuple-element.94), channel_id=1, source_target_pairs={{0,3},{1,0},{2,1},{3,2},{4,7},{5,4},{6,5},{7,6},{8,11},{9,8},{10,9... | collective-permute-start | bytes 663560 | tf_op jit(solution)/shard_map/ppermute | solution.py:34
  97.7 20.8 %collective-permute-done.25.rest_2_ = f32[216,128]{1,0:T(8,128)S(1)} collective-permute-done((f32[216,128]{1,0:T(8,128)S(1)}, f32[216,128]{1,0:T(8,128)S(1)}, u32[]{:S(2)}, u32[]{:S(2)}) %collective-permute-start.25) | collective-permute-done | bytes 110624 | tf_op jit(solution)/shard_map/ppermute | solution.py:34
  118.5 6.2 %interact.1 = f32[1296,256]{1,0:T(8,128)} custom-call(s32[2592]{0:T(1024)S(1)} %add_multiply_fusion.partner_source, f32[1296]{0:T(1024)S(1)} %copy-done.1, f32[216,128]{1,0:T(8,128)S(1)} %get-tuple-element.82.rest_0_, f32[216,128]{1,0:T(8,128)S(1)} %collective-permute-done.24.rest_1_, f32[216,128]{1,0:T(8,128)S(1)} %collective-permute-done.25.rest_2_, ...), custom_call_target="tpu_custom_call" | custom-call | flops 5308416 | bytes 2654208 | tf_op jit(solution)/shard_map/interact/pallas_call | solution.py:469
  (73 shorter events, 17.7 us)
Async XLA Ops:
  4.0 13.4 %collective-permute-start = (f32[324,128]{1,0:T(8,128)}, f32[324,128]{1,0:T(8,128)S(1)}, u32[]{:S(2)}, u32[]{:S(2)}) collective-permute-start(f32[324,128]{1,0:T(8,128)} %get-tuple-element.53), channel_id=1, source_target_pairs={{0,8},{4,12},{8,16},{12,20},{16,24},{20,28},{24,0},{28,4},{1,9},{5... | collective-permute-start | bytes 497672 | tf_op jit(solution)/shard_map/ppermute | solution.py:34
  5.5 11.9 %collective-permute-start.1 = (f32[324,128]{1,0:T(8,128)}, f32[324,128]{1,0:T(8,128)S(1)}, u32[]{:S(2)}, u32[]{:S(2)}) collective-permute-start(f32[324,128]{1,0:T(8,128)} %get-tuple-element.54), channel_id=1, source_target_pairs={{0,4},{4,8},{8,12},{12,16},{16,20},{20,24},{24,28},{28,0},{1,5},{5... | collective-permute-start | bytes 497672 | tf_op jit(solution)/shard_map/ppermute | solution.py:34
  5.5 11.9 %collective-permute-start.2 = (f32[324,128]{1,0:T(8,128)S(1)}, f32[324,128]{1,0:T(8,128)S(1)}, u32[]{:S(2)}, u32[]{:S(2)}) collective-permute-start(f32[324,128]{1,0:T(8,128)S(1)} %get-tuple-element.55), channel_id=1, source_target_pairs={{0,28},{4,0},{8,4},{12,8},{16,12},{20,16},{24,20},{28,24},{1,29},{... | collective-permute-start | bytes 497672 | tf_op jit(solution)/shard_map/ppermute | solution.py:34
  8.2 9.3 %collective-permute-start.3 = (f32[324,128]{1,0:T(8,128)S(1)}, f32[324,128]{1,0:T(8,128)S(1)}, u32[]{:S(2)}, u32[]{:S(2)}) collective-permute-start(f32[324,128]{1,0:T(8,128)S(1)} %get-tuple-element.56), channel_id=1, source_target_pairs={{0,24},{4,28},{8,0},{12,4},{16,8},{20,12},{24,16},{28,20},{1,25},{... | collective-permute-start | bytes 497672 | tf_op jit(solution)/shard_map/ppermute | solution.py:34
  30.5 14.7 %collective-permute-start.12 = (f32[216,128]{1,0:T(8,128)S(1)}, f32[216,128]{1,0:T(8,128)S(1)}, u32[]{:S(2)}, u32[]{:S(2)}) collective-permute-start(f32[216,128]{1,0:T(8,128)S(1)} %get-tuple-element.67), channel_id=1, source_target_pairs={{0,24},{4,28},{8,0},{12,4},{16,8},{20,12},{24,16},{28,20},{1,25},{... | collective-permute-start | bytes 331784 | tf_op jit(solution)/shard_map/ppermute | solution.py:34
  31.0 15.5 %collective-permute-start.13 = (f32[216,128]{1,0:T(8,128)S(1)}, f32[216,128]{1,0:T(8,128)S(1)}, u32[]{:S(2)}, u32[]{:S(2)}) collective-permute-start(f32[216,128]{1,0:T(8,128)S(1)} %get-tuple-element.68), channel_id=1, source_target_pairs={{0,28},{4,0},{8,4},{12,8},{16,12},{20,16},{24,20},{28,24},{1,29},{... | collective-permute-start | bytes 331784 | tf_op jit(solution)/shard_map/ppermute | solution.py:34
  32.6 14.6 %collective-permute-start.14 = (f32[216,128]{1,0:T(8,128)S(1)}, f32[216,128]{1,0:T(8,128)S(1)}, u32[]{:S(2)}, u32[]{:S(2)}) collective-permute-start(f32[216,128]{1,0:T(8,128)S(1)} %get-tuple-element.69), channel_id=1, source_target_pairs={{0,4},{4,8},{8,12},{12,16},{16,20},{20,24},{24,28},{28,0},{1,5},{5... | collective-permute-start | bytes 331784 | tf_op jit(solution)/shard_map/ppermute | solution.py:34
  32.7 14.5 %collective-permute-start.15 = (f32[216,128]{1,0:T(8,128)S(1)}, f32[216,128]{1,0:T(8,128)S(1)}, u32[]{:S(2)}, u32[]{:S(2)}) collective-permute-start(f32[216,128]{1,0:T(8,128)S(1)} %get-tuple-element.70), channel_id=1, source_target_pairs={{0,8},{4,12},{8,16},{12,20},{16,24},{20,28},{24,0},{28,4},{1,9},{5... | collective-permute-start | bytes 331784 | tf_op jit(solution)/shard_map/ppermute | solution.py:34
  45.2 8.9 %collective-permute-start.11 = (f32[108,128]{1,0:T(8,128)S(1)}, f32[108,128]{1,0:T(8,128)S(1)}, u32[]{:S(2)}, u32[]{:S(2)}) collective-permute-start(f32[108,128]{1,0:T(8,128)S(1)} %get-tuple-element.66), channel_id=1, source_target_pairs={{0,24},{4,28},{8,0},{12,4},{16,8},{20,12},{24,16},{28,20},{1,25},{... | collective-permute-start | bytes 165896 | tf_op jit(solution)/shard_map/ppermute | solution.py:34
  46.5 7.6 %collective-permute-start.8 = (f32[108,128]{1,0:T(8,128)S(1)}, f32[108,128]{1,0:T(8,128)S(1)}, u32[]{:S(2)}, u32[]{:S(2)}) collective-permute-start(f32[108,128]{1,0:T(8,128)S(1)} %get-tuple-element.63), channel_id=1, source_target_pairs={{0,8},{4,12},{8,16},{12,20},{16,24},{20,28},{24,0},{28,4},{1,9},{5... | collective-permute-start | bytes 165896 | tf_op jit(solution)/shard_map/ppermute | solution.py:34
  49.4 11.4 %collective-permute-start.16 = (f32[216,128]{1,0:T(8,128)S(1)}, f32[216,128]{1,0:T(8,128)S(1)}, u32[]{:S(2)}, u32[]{:S(2)}) collective-permute-start(f32[216,128]{1,0:T(8,128)S(1)} %get-tuple-element.72), channel_id=1, source_target_pairs={{0,8},{4,12},{8,16},{12,20},{16,24},{20,28},{24,0},{28,4},{1,9},{5... | collective-permute-start | bytes 331784 | tf_op jit(solution)/shard_map/ppermute | solution.py:34
  51.5 9.2 %collective-permute-start.17 = (f32[216,128]{1,0:T(8,128)S(1)}, f32[216,128]{1,0:T(8,128)S(1)}, u32[]{:S(2)}, u32[]{:S(2)}) collective-permute-start(f32[216,128]{1,0:T(8,128)S(1)} %get-tuple-element.73), channel_id=1, source_target_pairs={{0,4},{4,8},{8,12},{12,16},{16,20},{20,24},{24,28},{28,0},{1,5},{5... | collective-permute-start | bytes 331784 | tf_op jit(solution)/shard_map/ppermute | solution.py:34
  51.5 9.2 %collective-permute-start.18 = (f32[216,128]{1,0:T(8,128)S(1)}, f32[216,128]{1,0:T(8,128)S(1)}, u32[]{:S(2)}, u32[]{:S(2)}) collective-permute-start(f32[216,128]{1,0:T(8,128)S(1)} %get-tuple-element.74), channel_id=1, source_target_pairs={{0,28},{4,0},{8,4},{12,8},{16,12},{20,16},{24,20},{28,24},{1,29},{... | collective-permute-start | bytes 331784 | tf_op jit(solution)/shard_map/ppermute | solution.py:34
  73.1 15.4 %collective-permute-start.27 = (f32[216,128]{1,0:T(8,128)S(1)}, f32[216,128]{1,0:T(8,128)S(1)}, u32[]{:S(2)}, u32[]{:S(2)}) collective-permute-start(f32[216,128]{1,0:T(8,128)S(1)} %get-tuple-element.86), channel_id=1, source_target_pairs={{0,24},{4,28},{8,0},{12,4},{16,8},{20,12},{24,16},{28,20},{1,25},{... | collective-permute-start | bytes 331784 | tf_op jit(solution)/shard_map/ppermute | solution.py:34
  73.9 14.6 %collective-permute-start.28 = (f32[216,128]{1,0:T(8,128)S(1)}, f32[216,128]{1,0:T(8,128)S(1)}, u32[]{:S(2)}, u32[]{:S(2)}) collective-permute-start(f32[216,128]{1,0:T(8,128)S(1)} %get-tuple-element.87), channel_id=1, source_target_pairs={{0,28},{4,0},{8,4},{12,8},{16,12},{20,16},{24,20},{28,24},{1,29},{... | collective-permute-start | bytes 331784 | tf_op jit(solution)/shard_map/ppermute | solution.py:34
  75.3 13.3 %collective-permute-start.29 = (f32[216,128]{1,0:T(8,128)S(1)}, f32[216,128]{1,0:T(8,128)S(1)}, u32[]{:S(2)}, u32[]{:S(2)}) collective-permute-start(f32[216,128]{1,0:T(8,128)S(1)} %get-tuple-element.88), channel_id=1, source_target_pairs={{0,4},{4,8},{8,12},{12,16},{16,20},{20,24},{24,28},{28,0},{1,5},{5... | collective-permute-start | bytes 331784 | tf_op jit(solution)/shard_map/ppermute | solution.py:34
  75.4 13.1 %collective-permute-start.30 = (f32[216,128]{1,0:T(8,128)S(1)}, f32[216,128]{1,0:T(8,128)S(1)}, u32[]{:S(2)}, u32[]{:S(2)}) collective-permute-start(f32[216,128]{1,0:T(8,128)S(1)} %get-tuple-element.89), channel_id=1, source_target_pairs={{0,8},{4,12},{8,16},{12,20},{16,24},{20,28},{24,0},{28,4},{1,9},{5... | collective-permute-start | bytes 331784 | tf_op jit(solution)/shard_map/ppermute | solution.py:34
  77.6 7.6 %collective-permute-start.23 = (f32[108,128]{1,0:T(8,128)S(1)}, f32[108,128]{1,0:T(8,128)S(1)}, u32[]{:S(2)}, u32[]{:S(2)}) collective-permute-start(f32[108,128]{1,0:T(8,128)S(1)} %get-tuple-element.80), channel_id=1, source_target_pairs={{0,8},{4,12},{8,16},{12,20},{16,24},{20,28},{24,0},{28,4},{1,9},{5... | collective-permute-start | bytes 165896 | tf_op jit(solution)/shard_map/ppermute | solution.py:34
  86.9 9.4 %collective-permute-start.24 = (f32[216,128]{1,0:T(8,128)S(1)}, f32[216,128]{1,0:T(8,128)S(1)}, u32[]{:S(2)}, u32[]{:S(2)}) collective-permute-start(f32[216,128]{1,0:T(8,128)S(1)} %get-tuple-element.83), channel_id=1, source_target_pairs={{0,1},{1,2},{2,3},{3,0},{4,5},{5,6},{6,7},{7,4},{8,9},{9,10},{10,1... | collective-permute-start | bytes 331784 | tf_op jit(solution)/shard_map/ppermute | solution.py:34
  90.3 28.2 %collective-permute-start.31 = (f32[432,128]{1,0:T(8,128)S(1)}, f32[432,128]{1,0:T(8,128)S(1)}, u32[]{:S(2)}, u32[]{:S(2)}) collective-permute-start(f32[432,128]{1,0:T(8,128)S(1)} %get-tuple-element.92), channel_id=1, source_target_pairs={{0,1},{1,2},{2,3},{3,0},{4,5},{5,6},{6,7},{7,4},{8,9},{9,10},{10,1... | collective-permute-start | bytes 663560 | tf_op jit(solution)/shard_map/ppermute | solution.py:34
  92.0 26.5 %collective-permute-start.32 = (f32[432,128]{1,0:T(8,128)S(1)}, f32[432,128]{1,0:T(8,128)S(1)}, u32[]{:S(2)}, u32[]{:S(2)}) collective-permute-start(f32[432,128]{1,0:T(8,128)S(1)} %get-tuple-element.93), channel_id=1, source_target_pairs={{0,2},{1,3},{2,0},{3,1},{4,6},{5,7},{6,4},{7,5},{8,10},{9,11},{10,... | collective-permute-start | bytes 663560 | tf_op jit(solution)/shard_map/ppermute | solution.py:34
  93.2 25.3 %collective-permute-start.33 = (f32[432,128]{1,0:T(8,128)S(1)}, f32[432,128]{1,0:T(8,128)S(1)}, u32[]{:S(2)}, u32[]{:S(2)}) collective-permute-start(f32[432,128]{1,0:T(8,128)S(1)} %get-tuple-element.94), channel_id=1, source_target_pairs={{0,3},{1,0},{2,1},{3,2},{4,7},{5,4},{6,5},{7,6},{8,11},{9,8},{10,9... | collective-permute-start | bytes 663560 | tf_op jit(solution)/shard_map/ppermute | solution.py:34
  95.9 22.6 %collective-permute-start.25 = (f32[216,128]{1,0:T(8,128)S(1)}, f32[216,128]{1,0:T(8,128)S(1)}, u32[]{:S(2)}, u32[]{:S(2)}) collective-permute-start(f32[216,128]{1,0:T(8,128)S(1)} %get-tuple-element.84), channel_id=1, source_target_pairs={{0,2},{1,3},{2,0},{3,1},{4,6},{5,7},{6,4},{7,5},{8,10},{9,11},{10,... | collective-permute-start | bytes 331784 | tf_op jit(solution)/shard_map/ppermute | solution.py:34
  96.2 22.3 %collective-permute-start.26 = (f32[216,128]{1,0:T(8,128)S(1)}, f32[216,128]{1,0:T(8,128)S(1)}, u32[]{:S(2)}, u32[]{:S(2)}) collective-permute-start(f32[216,128]{1,0:T(8,128)S(1)} %get-tuple-element.85), channel_id=1, source_target_pairs={{0,3},{1,0},{2,1},{3,2},{4,7},{5,4},{6,5},{7,6},{8,11},{9,8},{10,9... | collective-permute-start | bytes 331784 | tf_op jit(solution)/shard_map/ppermute | solution.py:34
  (15 other events, 107.9 us)

commit v9 on v8

--- a/solution.py
+++ b/solution.py
@@ -211,7 +211,7 @@
                     at = pl.ds(index[corner], sub)
                     item[at, :] = item[at, :] + residual[corner]
 
-    step = chunked(ghost_rows, 64)
+    step = chunked(ghost_rows, 128)
     for position in range(BLOCKS):
         stage = stages.at[position]
 
@@ -224,7 +224,7 @@
         for position in range(BLOCKS):
             rows_to_block(sub, lanes, stages.at[position], returned[which * BLOCKS + position], start)
 
-    own_step = chunked(own_rows, 64)
+    own_step = chunked(own_rows, 128)
 
     @pl.loop(0, own_rows // own_step)
     def _(k):
@@ -322,7 +322,7 @@
 
     copies = done.shape[0]
     share = bins // copies
-    step = chunked(share, 48)
+    step = chunked(share, 144)
     for which in range(copies):
 
         @pl.loop(which * share // step, (which + 1) * share // step)

time: 127 us -> 126 us (level)
  no operation moved by 1% of the time
where the time goes in v9:
time: 126 us; the launch traced here: 124 us
  waiting for transfers between devices  42.4 us (34%)
  Pallas kernels  40.8 us (32%)
  starting transfers between devices  35.5 us (28%)
  local copies, waits for them, and re-layouts  2.88 us (2%)
  other arithmetic  2.49 us (2%)
    ppermute x34, waiting for transfers between devices, passed_along(): lax.ppermute(value, axis, [(source, (source + steps) % count) for source...  42.4 us
    ppermute x34, starting transfers between devices, passed_along(): lax.ppermute(value, axis, [(source, (source + steps) % count) for source...  35.5 us
    pallas_call x2, Pallas kernels, on_device(): pl.pallas_call(functools.partial(sweep_kernel, sub, inner, groups, lanes,...  19.7 us
    pallas_call x1, Pallas kernels, on_device(): pl.pallas_call(functools.partial(interact_kernel, row_count * halves, hal...  6.21 us
    pallas_call x1, Pallas kernels, on_device(): pl.pallas_call(functools.partial(slope_kernel, sub, shared), out_shape=[s...  5.38 us
    pallas_call x2, Pallas kernels, on_device(): pl.pallas_call(functools.partial(between_kernel, sub, parts, lanes), out_...  4.18 us
    pallas_call x2, Pallas kernels, on_device(): pl.pallas_call(functools.partial(leave_kernel, sub, (start, size), lanes,...  3.42 us
    unnamed x11, local copies, waits for them, and re-layouts  2.86 us
  transfers between devices with their start and end apart: 34, of which 5 were waited for; matrix products, arithmetic and copies ran while one was open for 2% of the time, Pallas kernels for 10%

profile of v9, /device:TPU:4, one launch (start us, length us, event | category | flops | bytes accessed | tf_op | source)
XLA Modules:
  0.0 124.3 jit_solution(8771699334324040436)
XLA Ops:
  2.0 2.0 %enter.1 = (f32[4608,128]{1,0:T(8,128)S(1)}, f32[324,128]{1,0:T(8,128)}, f32[324,128]{1,0:T(8,128)}, f32[324,128]{1,0:T(8,128)S(1)}, f32[324,128]{1,0:T(8,128)S(1)}) custom-call(s32[512]{0:T(512)S(1)} %multiply_bitcast_fusion.source, f32[324,1024]{1,0:T(8,128)S(1)} %copy-done), custom_call_target="tpu_custom_call" | custom-call | bytes 3145728 | tf_op jit(solution)/shard_map/enter/pallas_call | solution.py:397
  5.5 2.6 %collective-permute-start.2 = (f32[324,128]{1,0:T(8,128)S(1)}, f32[324,128]{1,0:T(8,128)S(1)}, u32[]{:S(2)}, u32[]{:S(2)}) collective-permute-start(f32[324,128]{1,0:T(8,128)S(1)} %get-tuple-element.55), channel_id=1, source_target_pairs={{0,28},{4,0},{8,4},{12,8},{16,12},{20,16},{24,20},{28,24},{1,29},{... | collective-permute-start | bytes 497672 | tf_op jit(solution)/shard_map/ppermute | solution.py:34
  12.0 5.4 %slopes.1 = (f32[6144,128]{1,0:T(8,128)S(1)}, f32[3072,128]{1,0:T(8,128)S(1)}, f32[1536,128]{1,0:T(8,128)S(1)}) custom-call(s32[512]{0:T(512)S(1)} %multiply_bitcast_fusion.source, f32[2,3,2048]{2,1,0:T(4,128)S(1)} %copy.17.normals, f32[1,1024]{1,0:T(1,128)S(1)} %bitcast.3, f32[9,128]{1,0:T(8,128)S(1)} %pad_maximum_fusion.wave), custom_call_target="tpu_custom_call" | custom-call | flops 5242880 | bytes 4718592 | tf_op jit(solution)/shard_map/slopes/pallas_call | solution.py:408
  17.4 9.8 %sweep.2 = (f32[4608,128]{1,0:T(8,128)S(1)}, f32[108,128]{1,0:T(8,128)S(1)}, f32[108,128]{1,0:T(8,128)S(1)}, f32[108,128]{1,0:T(8,128)S(1)}, f32[108,128]{1,0:T(...) custom-call(s32[6144]{0:T(1024)S(1)} %reshape.47.source, ...), custom_call_target="tpu_custom_call", output_to_operand_aliasing={{0}: (7, {})} | custom-call | flops 15925248 | bytes 12582912 | tf_op jit(solution)/shard_map/sweep/pallas_call | solution.py:425
  27.2 2.5 %collective-permute-start.4 = (f32[108,128]{1,0:T(8,128)S(1)}, f32[108,128]{1,0:T(8,128)S(1)}, u32[]{:S(2)}, u32[]{:S(2)}) collective-permute-start(f32[108,128]{1,0:T(8,128)S(1)} %get-tuple-element.58), channel_id=1, source_target_pairs={{0,24},{4,28},{8,0},{12,4},{16,8},{20,12},{24,16},{28,20},{1,25},{... | collective-permute-start | bytes 165896 | tf_op jit(solution)/shard_map/ppermute | solution.py:34
  30.8 1.6 %collective-permute-start.13 = (f32[216,128]{1,0:T(8,128)S(1)}, f32[216,128]{1,0:T(8,128)S(1)}, u32[]{:S(2)}, u32[]{:S(2)}) collective-permute-start(f32[216,128]{1,0:T(8,128)S(1)} %get-tuple-element.68), channel_id=1, source_target_pairs={{0,28},{4,0},{8,4},{12,8},{16,12},{20,16},{24,20},{28,24},{1,29},{... | collective-permute-start | bytes 331784 | tf_op jit(solution)/shard_map/ppermute | solution.py:34
  32.5 2.0 %collective-permute-start.15 = (f32[216,128]{1,0:T(8,128)S(1)}, f32[216,128]{1,0:T(8,128)S(1)}, u32[]{:S(2)}, u32[]{:S(2)}) collective-permute-start(f32[216,128]{1,0:T(8,128)S(1)} %get-tuple-element.70), channel_id=1, source_target_pairs={{0,8},{4,12},{8,16},{12,20},{16,24},{20,28},{24,0},{28,4},{1,9},{5... | collective-permute-start | bytes 331784 | tf_op jit(solution)/shard_map/ppermute | solution.py:34
  34.7 7.5 %collective-permute-done.7.rest_3_ = f32[108,128]{1,0:T(8,128)S(1)} collective-permute-done((f32[108,128]{1,0:T(8,128)S(1)}, f32[108,128]{1,0:T(8,128)S(1)}, u32[]{:S(2)}, u32[]{:S(2)}) %collective-permute-start.7) | collective-permute-done | bytes 55328 | tf_op jit(solution)/shard_map/ppermute | solution.py:34
  42.1 2.0 %shard_map.91 = (f32[4608,128]{1,0:T(8,128)S(1)}, f32[108,128]{1,0:T(8,128)S(1)}, f32[108,128]{1,0:T(8,128)S(1)}, f32[108,128]{1,0:T(8,128)S(1)}, f32[108,128]{1,0:T(8,128)S(1)}) custom-call(s32[512]{0:T(512)S(1)} %multiply_bitcast_fusion.source, f32[1536,128]{1,0:T(8,128)S(1)} %get-tuple-element.50.listed_weight, ...), custom_call_target="tpu_custom_call", output_to_operand_aliasing={{0}: (6, {})} | custom-call | flops 262144 | bytes 2097152 | tf_op jit(solution)/shard_map/pallas_call | solution.py:442
  47.0 2.1 %shard_map.92 = (f32[4608,128]{1,0:T(8,128)S(1)}, f32[216,128]{1,0:T(8,128)S(1)}, f32[216,128]{1,0:T(8,128)S(1)}, f32[216,128]{1,0:T(8,128)S(1)}, f32[216,128]{1,0:T(8,128)S(1)}) custom-call(s32[512]{0:T(512)S(1)} %multiply_bitcast_fusion.source, f32[1536,128]{1,0:T(8,128)S(1)} %get-tuple-element.50.listed_weight, ...), custom_call_target="tpu_custom_call", output_to_operand_aliasing={{0}: (6, {})} | custom-call | flops 524288 | bytes 4194304 | tf_op jit(solution)/shard_map/pallas_call | solution.py:442
  49.1 2.1 %collective-permute-start.16 = (f32[216,128]{1,0:T(8,128)S(1)}, f32[216,128]{1,0:T(8,128)S(1)}, u32[]{:S(2)}, u32[]{:S(2)}) collective-permute-start(f32[216,128]{1,0:T(8,128)S(1)} %get-tuple-element.72), channel_id=1, source_target_pairs={{0,8},{4,12},{8,16},{12,20},{16,24},{20,28},{24,0},{28,4},{1,9},{5... | collective-permute-start | bytes 331784 | tf_op jit(solution)/shard_map/ppermute | solution.py:34
  51.2 2.6 %collective-permute-start.18 = (f32[216,128]{1,0:T(8,128)S(1)}, f32[216,128]{1,0:T(8,128)S(1)}, u32[]{:S(2)}, u32[]{:S(2)}) collective-permute-start(f32[216,128]{1,0:T(8,128)S(1)} %get-tuple-element.74), channel_id=1, source_target_pairs={{0,28},{4,0},{8,4},{12,8},{16,12},{20,16},{24,20},{28,24},{1,29},{... | collective-permute-start | bytes 331784 | tf_op jit(solution)/shard_map/ppermute | solution.py:34
  54.1 6.4 %collective-permute-done.9.rest_1_ = f32[108,128]{1,0:T(8,128)S(1)} collective-permute-done((f32[108,128]{1,0:T(8,128)S(1)}, f32[108,128]{1,0:T(8,128)S(1)}, u32[]{:S(2)}, u32[]{:S(2)}) %collective-permute-start.9) | collective-permute-done | bytes 55328 | tf_op jit(solution)/shard_map/ppermute | solution.py:34
  60.5 9.8 %sweep.3 = (f32[4608,128]{1,0:T(8,128)S(1)}, f32[108,128]{1,0:T(8,128)S(1)}, f32[108,128]{1,0:T(8,128)S(1)}, f32[108,128]{1,0:T(8,128)S(1)}, f32[108,128]{1,0:T(...) custom-call(s32[6144]{0:T(1024)S(1)} %reshape.47.source, ...), custom_call_target="tpu_custom_call", output_to_operand_aliasing={{0}: (11, {})} | custom-call | flops 15925248 | bytes 12582912 | tf_op jit(solution)/shard_map/sweep/pallas_call | solution.py:425
  70.4 1.8 %collective-permute-start.20 = (f32[108,128]{1,0:T(8,128)S(1)}, f32[108,128]{1,0:T(8,128)S(1)}, u32[]{:S(2)}, u32[]{:S(2)}) collective-permute-start(f32[108,128]{1,0:T(8,128)S(1)} %get-tuple-element.77), channel_id=1, source_target_pairs={{0,24},{4,28},{8,0},{12,4},{16,8},{20,12},{24,16},{28,20},{1,25},{... | collective-permute-start | bytes 165896 | tf_op jit(solution)/shard_map/ppermute | solution.py:34
  74.9 2.2 %collective-permute-start.30 = (f32[216,128]{1,0:T(8,128)S(1)}, f32[216,128]{1,0:T(8,128)S(1)}, u32[]{:S(2)}, u32[]{:S(2)}) collective-permute-start(f32[216,128]{1,0:T(8,128)S(1)} %get-tuple-element.89), channel_id=1, source_target_pairs={{0,8},{4,12},{8,16},{12,20},{16,24},{20,28},{24,0},{28,4},{1,9},{5... | collective-permute-start | bytes 331784 | tf_op jit(solution)/shard_map/ppermute | solution.py:34
  77.3 7.5 %collective-permute-done.23.rest_3_ = f32[108,128]{1,0:T(8,128)S(1)} collective-permute-done((f32[108,128]{1,0:T(8,128)S(1)}, f32[108,128]{1,0:T(8,128)S(1)}, u32[]{:S(2)}, u32[]{:S(2)}) %collective-permute-start.23) | collective-permute-done | bytes 55328 | tf_op jit(solution)/shard_map/ppermute | solution.py:34
  84.7 1.6 %shard_map.93 = (f32[4608,128]{1,0:T(8,128)S(1)}, f32[216,128]{1,0:T(8,128)S(1)}, f32[216,128]{1,0:T(8,128)S(1)}, f32[216,128]{1,0:T(8,128)S(1)}, f32[216,128]{1,0:T(8,128)S(1)}) custom-call(s32[512]{0:T(512)S(1)} %multiply_bitcast_fusion.source, f32[1536,128]{1,0:T(8,128)S(1)} %get-tuple-element.50.listed_weight, ...), custom_call_target="tpu_custom_call", output_to_operand_aliasing={{0}: (6, {})} | custom-call | flops 262144 | bytes 1572864 | tf_op jit(solution)/shard_map/pallas_call | solution.py:456
  86.4 1.6 %collective-permute-start.24 = (f32[216,128]{1,0:T(8,128)S(1)}, f32[216,128]{1,0:T(8,128)S(1)}, u32[]{:S(2)}, u32[]{:S(2)}) collective-permute-start(f32[216,128]{1,0:T(8,128)S(1)} %get-tuple-element.83), channel_id=1, source_target_pairs={{0,1},{1,2},{2,3},{3,0},{4,5},{5,6},{6,7},{7,4},{8,9},{9,10},{10,1... | collective-permute-start | bytes 331784 | tf_op jit(solution)/shard_map/ppermute | solution.py:34
  88.1 1.8 %shard_map.94 = (f32[4608,128]{1,0:T(8,128)S(1)}, f32[432,128]{1,0:T(8,128)S(1)}, f32[432,128]{1,0:T(8,128)S(1)}, f32[432,128]{1,0:T(8,128)S(1)}, f32[432,128]{1,0:T(8,128)S(1)}) custom-call(s32[512]{0:T(512)S(1)} %multiply_bitcast_fusion.source, f32[1536,128]{1,0:T(8,128)S(1)} %get-tuple-element.50.listed_weight, ...), custom_call_target="tpu_custom_call", output_to_operand_aliasing={{0}: (6, {})} | custom-call | flops 524288 | bytes 3145728 | tf_op jit(solution)/shard_map/pallas_call | solution.py:456
  89.9 1.6 %collective-permute-start.31 = (f32[432,128]{1,0:T(8,128)S(1)}, f32[432,128]{1,0:T(8,128)S(1)}, u32[]{:S(2)}, u32[]{:S(2)}) collective-permute-start(f32[432,128]{1,0:T(8,128)S(1)} %get-tuple-element.92), channel_id=1, source_target_pairs={{0,1},{1,2},{2,3},{3,0},{4,5},{5,6},{6,7},{7,4},{8,9},{9,10},{10,1... | collective-permute-start | bytes 663560 | tf_op jit(solution)/shard_map/ppermute | solution.py:34
  92.7 2.7 %collective-permute-start.33 = (f32[432,128]{1,0:T(8,128)S(1)}, f32[432,128]{1,0:T(8,128)S(1)}, u32[]{:S(2)}, u32[]{:S(2)}) collective-permute-start(f32[432,128]{1,0:T(8,128)S(1)} %get-tuple-element.94), channel_id=1, source_target_pairs={{0,3},{1,0},{2,1},{3,2},{4,7},{5,4},{6,5},{7,6},{8,11},{9,8},{10,9... | collective-permute-start | bytes 663560 | tf_op jit(solution)/shard_map/ppermute | solution.py:34
  97.2 20.8 %collective-permute-done.25.rest_2_ = f32[216,128]{1,0:T(8,128)S(1)} collective-permute-done((f32[216,128]{1,0:T(8,128)S(1)}, f32[216,128]{1,0:T(8,128)S(1)}, u32[]{:S(2)}, u32[]{:S(2)}) %collective-permute-start.25) | collective-permute-done | bytes 110624 | tf_op jit(solution)/shard_map/ppermute | solution.py:34
  118.0 6.2 %interact.1 = f32[1296,256]{1,0:T(8,128)} custom-call(s32[2592]{0:T(1024)S(1)} %add_multiply_fusion.partner_source, f32[1296]{0:T(1024)S(1)} %copy-done.1, f32[216,128]{1,0:T(8,128)S(1)} %get-tuple-element.82.rest_0_, f32[216,128]{1,0:T(8,128)S(1)} %collective-permute-done.24.rest_1_, f32[216,128]{1,0:T(8,128)S(1)} %collective-permute-done.25.rest_2_, ...), custom_call_target="tpu_custom_call" | custom-call | flops 5308416 | bytes 2654208 | tf_op jit(solution)/shard_map/interact/pallas_call | solution.py:469
  (73 shorter events, 17.7 us)
Async XLA Ops:
  4.0 13.4 %collective-permute-start = (f32[324,128]{1,0:T(8,128)}, f32[324,128]{1,0:T(8,128)S(1)}, u32[]{:S(2)}, u32[]{:S(2)}) collective-permute-start(f32[324,128]{1,0:T(8,128)} %get-tuple-element.53), channel_id=1, source_target_pairs={{0,8},{4,12},{8,16},{12,20},{16,24},{20,28},{24,0},{28,4},{1,9},{5... | collective-permute-start | bytes 497672 | tf_op jit(solution)/shard_map/ppermute | solution.py:34
  5.5 11.9 %collective-permute-start.1 = (f32[324,128]{1,0:T(8,128)}, f32[324,128]{1,0:T(8,128)S(1)}, u32[]{:S(2)}, u32[]{:S(2)}) collective-permute-start(f32[324,128]{1,0:T(8,128)} %get-tuple-element.54), channel_id=1, source_target_pairs={{0,4},{4,8},{8,12},{12,16},{16,20},{20,24},{24,28},{28,0},{1,5},{5... | collective-permute-start | bytes 497672 | tf_op jit(solution)/shard_map/ppermute | solution.py:34
  5.5 11.9 %collective-permute-start.2 = (f32[324,128]{1,0:T(8,128)S(1)}, f32[324,128]{1,0:T(8,128)S(1)}, u32[]{:S(2)}, u32[]{:S(2)}) collective-permute-start(f32[324,128]{1,0:T(8,128)S(1)} %get-tuple-element.55), channel_id=1, source_target_pairs={{0,28},{4,0},{8,4},{12,8},{16,12},{20,16},{24,20},{28,24},{1,29},{... | collective-permute-start | bytes 497672 | tf_op jit(solution)/shard_map/ppermute | solution.py:34
  8.2 9.3 %collective-permute-start.3 = (f32[324,128]{1,0:T(8,128)S(1)}, f32[324,128]{1,0:T(8,128)S(1)}, u32[]{:S(2)}, u32[]{:S(2)}) collective-permute-start(f32[324,128]{1,0:T(8,128)S(1)} %get-tuple-element.56), channel_id=1, source_target_pairs={{0,24},{4,28},{8,0},{12,4},{16,8},{20,12},{24,16},{28,20},{1,25},{... | collective-permute-start | bytes 497672 | tf_op jit(solution)/shard_map/ppermute | solution.py:34
  30.2 14.7 %collective-permute-start.12 = (f32[216,128]{1,0:T(8,128)S(1)}, f32[216,128]{1,0:T(8,128)S(1)}, u32[]{:S(2)}, u32[]{:S(2)}) collective-permute-start(f32[216,128]{1,0:T(8,128)S(1)} %get-tuple-element.67), channel_id=1, source_target_pairs={{0,24},{4,28},{8,0},{12,4},{16,8},{20,12},{24,16},{28,20},{1,25},{... | collective-permute-start | bytes 331784 | tf_op jit(solution)/shard_map/ppermute | solution.py:34
  30.8 15.5 %collective-permute-start.13 = (f32[216,128]{1,0:T(8,128)S(1)}, f32[216,128]{1,0:T(8,128)S(1)}, u32[]{:S(2)}, u32[]{:S(2)}) collective-permute-start(f32[216,128]{1,0:T(8,128)S(1)} %get-tuple-element.68), channel_id=1, source_target_pairs={{0,28},{4,0},{8,4},{12,8},{16,12},{20,16},{24,20},{28,24},{1,29},{... | collective-permute-start | bytes 331784 | tf_op jit(solution)/shard_map/ppermute | solution.py:34
  32.4 14.6 %collective-permute-start.14 = (f32[216,128]{1,0:T(8,128)S(1)}, f32[216,128]{1,0:T(8,128)S(1)}, u32[]{:S(2)}, u32[]{:S(2)}) collective-permute-start(f32[216,128]{1,0:T(8,128)S(1)} %get-tuple-element.69), channel_id=1, source_target_pairs={{0,4},{4,8},{8,12},{12,16},{16,20},{20,24},{24,28},{28,0},{1,5},{5... | collective-permute-start | bytes 331784 | tf_op jit(solution)/shard_map/ppermute | solution.py:34
  32.5 14.5 %collective-permute-start.15 = (f32[216,128]{1,0:T(8,128)S(1)}, f32[216,128]{1,0:T(8,128)S(1)}, u32[]{:S(2)}, u32[]{:S(2)}) collective-permute-start(f32[216,128]{1,0:T(8,128)S(1)} %get-tuple-element.70), channel_id=1, source_target_pairs={{0,8},{4,12},{8,16},{12,20},{16,24},{20,28},{24,0},{28,4},{1,9},{5... | collective-permute-start | bytes 331784 | tf_op jit(solution)/shard_map/ppermute | solution.py:34
  45.0 8.9 %collective-permute-start.11 = (f32[108,128]{1,0:T(8,128)S(1)}, f32[108,128]{1,0:T(8,128)S(1)}, u32[]{:S(2)}, u32[]{:S(2)}) collective-permute-start(f32[108,128]{1,0:T(8,128)S(1)} %get-tuple-element.66), channel_id=1, source_target_pairs={{0,24},{4,28},{8,0},{12,4},{16,8},{20,12},{24,16},{28,20},{1,25},{... | collective-permute-start | bytes 165896 | tf_op jit(solution)/shard_map/ppermute | solution.py:34
  46.3 7.6 %collective-permute-start.8 = (f32[108,128]{1,0:T(8,128)S(1)}, f32[108,128]{1,0:T(8,128)S(1)}, u32[]{:S(2)}, u32[]{:S(2)}) collective-permute-start(f32[108,128]{1,0:T(8,128)S(1)} %get-tuple-element.63), channel_id=1, source_target_pairs={{0,8},{4,12},{8,16},{12,20},{16,24},{20,28},{24,0},{28,4},{1,9},{5... | collective-permute-start | bytes 165896 | tf_op jit(solution)/shard_map/ppermute | solution.py:34
  49.1 11.4 %collective-permute-start.16 = (f32[216,128]{1,0:T(8,128)S(1)}, f32[216,128]{1,0:T(8,128)S(1)}, u32[]{:S(2)}, u32[]{:S(2)}) collective-permute-start(f32[216,128]{1,0:T(8,128)S(1)} %get-tuple-element.72), channel_id=1, source_target_pairs={{0,8},{4,12},{8,16},{12,20},{16,24},{20,28},{24,0},{28,4},{1,9},{5... | collective-permute-start | bytes 331784 | tf_op jit(solution)/shard_map/ppermute | solution.py:34
  51.2 9.2 %collective-permute-start.17 = (f32[216,128]{1,0:T(8,128)S(1)}, f32[216,128]{1,0:T(8,128)S(1)}, u32[]{:S(2)}, u32[]{:S(2)}) collective-permute-start(f32[216,128]{1,0:T(8,128)S(1)} %get-tuple-element.73), channel_id=1, source_target_pairs={{0,4},{4,8},{8,12},{12,16},{16,20},{20,24},{24,28},{28,0},{1,5},{5... | collective-permute-start | bytes 331784 | tf_op jit(solution)/shard_map/ppermute | solution.py:34
  51.2 9.2 %collective-permute-start.18 = (f32[216,128]{1,0:T(8,128)S(1)}, f32[216,128]{1,0:T(8,128)S(1)}, u32[]{:S(2)}, u32[]{:S(2)}) collective-permute-start(f32[216,128]{1,0:T(8,128)S(1)} %get-tuple-element.74), channel_id=1, source_target_pairs={{0,28},{4,0},{8,4},{12,8},{16,12},{20,16},{24,20},{28,24},{1,29},{... | collective-permute-start | bytes 331784 | tf_op jit(solution)/shard_map/ppermute | solution.py:34
  72.6 15.4 %collective-permute-start.27 = (f32[216,128]{1,0:T(8,128)S(1)}, f32[216,128]{1,0:T(8,128)S(1)}, u32[]{:S(2)}, u32[]{:S(2)}) collective-permute-start(f32[216,128]{1,0:T(8,128)S(1)} %get-tuple-element.86), channel_id=1, source_target_pairs={{0,24},{4,28},{8,0},{12,4},{16,8},{20,12},{24,16},{28,20},{1,25},{... | collective-permute-start | bytes 331784 | tf_op jit(solution)/shard_map/ppermute | solution.py:34
  73.4 14.6 %collective-permute-start.28 = (f32[216,128]{1,0:T(8,128)S(1)}, f32[216,128]{1,0:T(8,128)S(1)}, u32[]{:S(2)}, u32[]{:S(2)}) collective-permute-start(f32[216,128]{1,0:T(8,128)S(1)} %get-tuple-element.87), channel_id=1, source_target_pairs={{0,28},{4,0},{8,4},{12,8},{16,12},{20,16},{24,20},{28,24},{1,29},{... | collective-permute-start | bytes 331784 | tf_op jit(solution)/shard_map/ppermute | solution.py:34
  74.8 13.3 %collective-permute-start.29 = (f32[216,128]{1,0:T(8,128)S(1)}, f32[216,128]{1,0:T(8,128)S(1)}, u32[]{:S(2)}, u32[]{:S(2)}) collective-permute-start(f32[216,128]{1,0:T(8,128)S(1)} %get-tuple-element.88), channel_id=1, source_target_pairs={{0,4},{4,8},{8,12},{12,16},{16,20},{20,24},{24,28},{28,0},{1,5},{5... | collective-permute-start | bytes 331784 | tf_op jit(solution)/shard_map/ppermute | solution.py:34
  74.9 13.1 %collective-permute-start.30 = (f32[216,128]{1,0:T(8,128)S(1)}, f32[216,128]{1,0:T(8,128)S(1)}, u32[]{:S(2)}, u32[]{:S(2)}) collective-permute-start(f32[216,128]{1,0:T(8,128)S(1)} %get-tuple-element.89), channel_id=1, source_target_pairs={{0,8},{4,12},{8,16},{12,20},{16,24},{20,28},{24,0},{28,4},{1,9},{5... | collective-permute-start | bytes 331784 | tf_op jit(solution)/shard_map/ppermute | solution.py:34
  77.1 7.6 %collective-permute-start.23 = (f32[108,128]{1,0:T(8,128)S(1)}, f32[108,128]{1,0:T(8,128)S(1)}, u32[]{:S(2)}, u32[]{:S(2)}) collective-permute-start(f32[108,128]{1,0:T(8,128)S(1)} %get-tuple-element.80), channel_id=1, source_target_pairs={{0,8},{4,12},{8,16},{12,20},{16,24},{20,28},{24,0},{28,4},{1,9},{5... | collective-permute-start | bytes 165896 | tf_op jit(solution)/shard_map/ppermute | solution.py:34
  86.4 9.4 %collective-permute-start.24 = (f32[216,128]{1,0:T(8,128)S(1)}, f32[216,128]{1,0:T(8,128)S(1)}, u32[]{:S(2)}, u32[]{:S(2)}) collective-permute-start(f32[216,128]{1,0:T(8,128)S(1)} %get-tuple-element.83), channel_id=1, source_target_pairs={{0,1},{1,2},{2,3},{3,0},{4,5},{5,6},{6,7},{7,4},{8,9},{9,10},{10,1... | collective-permute-start | bytes 331784 | tf_op jit(solution)/shard_map/ppermute | solution.py:34
  89.9 28.2 %collective-permute-start.31 = (f32[432,128]{1,0:T(8,128)S(1)}, f32[432,128]{1,0:T(8,128)S(1)}, u32[]{:S(2)}, u32[]{:S(2)}) collective-permute-start(f32[432,128]{1,0:T(8,128)S(1)} %get-tuple-element.92), channel_id=1, source_target_pairs={{0,1},{1,2},{2,3},{3,0},{4,5},{5,6},{6,7},{7,4},{8,9},{9,10},{10,1... | collective-permute-start | bytes 663560 | tf_op jit(solution)/shard_map/ppermute | solution.py:34
  91.5 26.5 %collective-permute-start.32 = (f32[432,128]{1,0:T(8,128)S(1)}, f32[432,128]{1,0:T(8,128)S(1)}, u32[]{:S(2)}, u32[]{:S(2)}) collective-permute-start(f32[432,128]{1,0:T(8,128)S(1)} %get-tuple-element.93), channel_id=1, source_target_pairs={{0,2},{1,3},{2,0},{3,1},{4,6},{5,7},{6,4},{7,5},{8,10},{9,11},{10,... | collective-permute-start | bytes 663560 | tf_op jit(solution)/shard_map/ppermute | solution.py:34
  92.7 25.3 %collective-permute-start.33 = (f32[432,128]{1,0:T(8,128)S(1)}, f32[432,128]{1,0:T(8,128)S(1)}, u32[]{:S(2)}, u32[]{:S(2)}) collective-permute-start(f32[432,128]{1,0:T(8,128)S(1)} %get-tuple-element.94), channel_id=1, source_target_pairs={{0,3},{1,0},{2,1},{3,2},{4,7},{5,4},{6,5},{7,6},{8,11},{9,8},{10,9... | collective-permute-start | bytes 663560 | tf_op jit(solution)/shard_map/ppermute | solution.py:34
  95.4 22.6 %collective-permute-start.25 = (f32[216,128]{1,0:T(8,128)S(1)}, f32[216,128]{1,0:T(8,128)S(1)}, u32[]{:S(2)}, u32[]{:S(2)}) collective-permute-start(f32[216,128]{1,0:T(8,128)S(1)} %get-tuple-element.84), channel_id=1, source_target_pairs={{0,2},{1,3},{2,0},{3,1},{4,6},{5,7},{6,4},{7,5},{8,10},{9,11},{10,... | collective-permute-start | bytes 331784 | tf_op jit(solution)/shard_map/ppermute | solution.py:34
  95.8 22.3 %collective-permute-start.26 = (f32[216,128]{1,0:T(8,128)S(1)}, f32[216,128]{1,0:T(8,128)S(1)}, u32[]{:S(2)}, u32[]{:S(2)}) collective-permute-start(f32[216,128]{1,0:T(8,128)S(1)} %get-tuple-element.85), channel_id=1, source_target_pairs={{0,3},{1,0},{2,1},{3,2},{4,7},{5,4},{6,5},{7,6},{8,11},{9,8},{10,9... | collective-permute-start | bytes 331784 | tf_op jit(solution)/shard_map/ppermute | solution.py:34
  (15 other events, 107.9 us)
